TPU v7x, 32 devices: a whole 2x2x4 slice. The times are simulated.
32 devices in a mesh: ctx: 16 (over z, x, core), fsdp: 2 (over y).
Axes of the slice: x: 2, y: 2, z: 4, core: 2. Of those that a mesh axis runs over, the one named last changes fastest.
Arguments:
- tokens: bfloat16 [4, 2048, 768], P('fsdp', 'ctx'), may hold values from -6 to 6
- cotangent: bfloat16 [4, 2048, 768], P('fsdp', 'ctx'), may hold values from -6 to 6
- doc_lengths: int32 [4, 4], P('fsdp'), may hold values from 1 to 1280, 2048 in all within a row
- w_qkv: bfloat16 [768, 2304], P('fsdp'), may hold values from -0.21875 to 0.21875
- w_out: bfloat16 [768, 768], P('fsdp'), may hold values from -6 to 6
- w_in: bfloat16 [768, 3072], P('fsdp'), may hold values from -0.21875 to 0.21875
- w_back: bfloat16 [3072, 768], P('fsdp'), may hold values from -0.109375 to 0.109375
- b_query: bfloat16 [768], P('fsdp'), may hold values from -4 to 4
- b_value: bfloat16 [768], P('fsdp'), may hold values from -0.3125 to 0.3125
- b_out: bfloat16 [768], P('fsdp'), may hold values from -4 to 4
- b_in: bfloat16 [3072], P('fsdp'), may hold values from -4 to 4
- b_back: bfloat16 [768], P('fsdp'), may hold values from -4 to 4
- gain_one: bfloat16 [768], P('fsdp'), may hold values from 0.5 to 1.5
- shift_one: bfloat16 [768], P('fsdp'), may hold values from -3 to 3
- gain_two: bfloat16 [768], P('fsdp'), may hold values from 0.5 to 1.5
- shift_two: bfloat16 [768], P('fsdp'), may hold values from -3 to 3
Outputs:
- output: bfloat16 [4, 2048, 768], P('fsdp', 'ctx')
- input_grad: float32 [4, 2048, 768], P('fsdp', 'ctx')
- w_qkv_grad: float32 [768, 2304], P('fsdp')
- w_out_grad: float32 [768, 768], P('fsdp')
- w_in_grad: float32 [768, 3072], P('fsdp')
- w_back_grad: float32 [3072, 768], P('fsdp')
- b_query_grad: float32 [768], P('fsdp')
- b_value_grad: float32 [768], P('fsdp')
- b_out_grad: float32 [768], P('fsdp')
- b_in_grad: float32 [3072], P('fsdp')
- b_back_grad: float32 [768], P('fsdp')
- gain_one_grad: float32 [768], P('fsdp')
- shift_one_grad: float32 [768], P('fsdp')
- gain_two_grad: float32 [768], P('fsdp')
- shift_two_grad: float32 [768], P('fsdp')
Inputs may be any that keep to these rules, and one draw needn't show every extreme that they name: `doc_lengths`: row s holds the lengths of the 4 documents of stream s in order; they sum to 2048, and in every stream the longest is 1280.
All inputs are finite; a program needn't handle non-finite values.
Results may differ from a plain program's by a relative error of at most 0.02.
Values may be sent and summed in bfloat16 or wider, within the bound.
A program may use at most 256 MiB of HBM per device.

v0:
```python
import jax
import jax.numpy as jnp
from jax import lax
from jax.sharding import PartitionSpec as P

HEADS = 12
HEAD = 64
KEYBLK = 512


EPSILON = 1e-12
NEGATIVE = -1e30


def layer_norm(values, gain_row, shift_row):
    average = jnp.mean(values, axis=-1, keepdims=True)
    centered = values - average
    variance = jnp.mean(centered * centered, axis=-1, keepdims=True)
    return centered * lax.rsqrt(variance + EPSILON) * gain_row + shift_row


def exact_gelu(values):
    return jax.nn.gelu(values, approximate=False)


def document_ids(stream_lengths, positions):
    boundary = jnp.cumsum(stream_lengths)
    return jnp.sum((positions[:, None] >= boundary[None, :]).astype(jnp.int32), axis=1)


def fetch_weights(
    w_qkv,
    w_out,
    w_in,
    w_back,
    b_query,
    b_value,
    b_out,
    b_in,
    b_back,
    gain_one,
    shift_one,
    gain_two,
    shift_two,
):
    gathered = (
        lax.all_gather(w_qkv, "fsdp", axis=0, tiled=True),
        lax.all_gather(w_out, "fsdp", axis=0, tiled=True),
        lax.all_gather(w_in, "fsdp", axis=0, tiled=True),
        lax.all_gather(w_back, "fsdp", axis=0, tiled=True),
        lax.all_gather(b_query, "fsdp", axis=0, tiled=True),
        lax.all_gather(b_value, "fsdp", axis=0, tiled=True),
        lax.all_gather(b_out, "fsdp", axis=0, tiled=True),
        lax.all_gather(b_in, "fsdp", axis=0, tiled=True),
        lax.all_gather(b_back, "fsdp", axis=0, tiled=True),
        lax.all_gather(gain_one, "fsdp", axis=0, tiled=True),
        lax.all_gather(shift_one, "fsdp", axis=0, tiled=True),
        lax.all_gather(gain_two, "fsdp", axis=0, tiled=True),
        lax.all_gather(shift_two, "fsdp", axis=0, tiled=True),
    )
    vectors = tuple((member.astype(jnp.float32) for member in gathered[4:]))
    return (gathered[0], gathered[1], gathered[2], gathered[3]) + vectors


def block_scores(queries, block_keys, query_docs, block_docs):
    scores = (
        jnp.einsum("qhd,khd->hqk", queries, block_keys, preferred_element_type=jnp.float32) * 0.125
    )
    allowed = (query_docs[:, None] == block_docs[None, :])[None]
    return (jnp.where(allowed, scores, NEGATIVE), allowed)


def attend_forward(queries, blocked_pairs, query_docs, blocked_docs):
    head_count = queries.shape[1]
    row_count = queries.shape[0]

    def total_pass(state_pair, block_item):
        running_max, running_sum = state_pair
        block_pair, block_docs = block_item
        scores, allowed = block_scores(queries, block_pair[:, 0], query_docs, block_docs)
        new_max = jnp.maximum(running_max, jnp.max(scores, axis=-1))
        shifted = jnp.where(allowed, jnp.exp(scores - new_max[:, :, None]), 0.0)
        running_sum = running_sum * jnp.exp(running_max - new_max) + jnp.sum(shifted, axis=-1)
        return ((new_max, running_sum), None)

    start_max = jnp.full((head_count, row_count), NEGATIVE, jnp.float32)
    start_sum = jnp.zeros((head_count, row_count), jnp.float32)
    (top_score, row_total), _ = lax.scan(
        total_pass, (start_max, start_sum), (blocked_pairs, blocked_docs)
    )
    log_total = top_score + jnp.log(row_total)

    def value_pass(state_pair, block_item):
        mixed_sum, leftover_sum = state_pair
        block_pair, block_docs = block_item
        scores, allowed = block_scores(queries, block_pair[:, 0], query_docs, block_docs)
        probabilities = jnp.where(allowed, jnp.exp(scores - log_total[:, :, None]), 0.0)
        rounded = probabilities.astype(jnp.bfloat16)
        leftover = (probabilities - rounded.astype(jnp.float32)).astype(jnp.bfloat16)
        mixed_sum = mixed_sum + jnp.einsum(
            "hqk,khd->qhd", rounded, block_pair[:, 1], preferred_element_type=jnp.float32
        )
        leftover_sum = leftover_sum + jnp.einsum(
            "hqk,khd->qhd", leftover, block_pair[:, 1], preferred_element_type=jnp.float32
        )
        return ((mixed_sum, leftover_sum), None)

    zero_rows = jnp.zeros(queries.shape, jnp.float32)
    (mixed_sum, leftover_sum), _ = lax.scan(
        value_pass, (zero_rows, zero_rows), (blocked_pairs, blocked_docs)
    )
    return (log_total, mixed_sum, mixed_sum + leftover_sum)


def attend_backward(queries, blocked_pairs, query_docs, blocked_docs, log_total, delta, grad_out):

    def grad_pass(grad_queries, block_item):
        block_pair, block_docs = block_item
        scores, allowed = block_scores(queries, block_pair[:, 0], query_docs, block_docs)
        probabilities = jnp.where(allowed, jnp.exp(scores - log_total[:, :, None]), 0.0)
        grad_probs = jnp.einsum(
            "qhd,khd->hqk", grad_out, block_pair[:, 1], preferred_element_type=jnp.float32
        )
        grad_scores = (probabilities * (grad_probs - delta[:, :, None])).astype(jnp.bfloat16)
        grad_queries = grad_queries + jnp.einsum(
            "hqk,khd->qhd", grad_scores, block_pair[:, 0], preferred_element_type=jnp.float32
        )
        rounded = probabilities.astype(jnp.bfloat16)
        grad_values = jnp.einsum(
            "hqk,qhd->khd", rounded, grad_out, preferred_element_type=jnp.float32
        )
        grad_keys = (
            jnp.einsum("hqk,qhd->khd", grad_scores, queries, preferred_element_type=jnp.float32)
            * 0.125
        )
        return (grad_queries, jnp.stack([grad_keys, grad_values], axis=1))

    grad_queries, block_grads = lax.scan(
        grad_pass, jnp.zeros(queries.shape, jnp.float32), (blocked_pairs, blocked_docs)
    )
    return (grad_queries * 0.125, block_grads)


def shards(
    tokens,
    cotangent,
    doc_lengths,
    w_qkv,
    w_out,
    w_in,
    w_back,
    b_query,
    b_value,
    b_out,
    b_in,
    b_back,
    gain_one,
    shift_one,
    gain_two,
    shift_two,
):
    micro_count = tokens.shape[0]
    row_count = tokens.shape[1]
    model_width = tokens.shape[2]
    length = row_count * lax.axis_size("ctx")
    block_count = length // KEYBLK
    local_positions = lax.axis_index("ctx") * row_count + jnp.arange(row_count, dtype=jnp.int32)
    all_positions = jnp.arange(length, dtype=jnp.int32)
    kept_states = []
    outputs = []
    for batch_index in range(micro_count):
        gathered = fetch_weights(
            w_qkv,
            w_out,
            w_in,
            w_back,
            b_query,
            b_value,
            b_out,
            b_in,
            b_back,
            gain_one,
            shift_one,
            gain_two,
            shift_two,
        )
        (
            full_qkv,
            full_out,
            full_in,
            full_back,
            query_bias,
            value_bias,
            out_bias,
            in_bias,
            back_bias,
            gain_first,
            shift_first,
            gain_second,
            shift_second,
        ) = gathered
        inputs = tokens[batch_index]
        joined = jnp.dot(inputs, full_qkv, preferred_element_type=jnp.float32)
        queries = (joined[:, :model_width] + query_bias).astype(jnp.bfloat16)
        pair_bias = jnp.concatenate([jnp.zeros_like(value_bias), value_bias])
        local_pair = (joined[:, model_width:] + pair_bias).astype(jnp.bfloat16)
        key_value = lax.all_gather(local_pair, "ctx", axis=0, tiled=True)
        query_docs = document_ids(doc_lengths[batch_index], local_positions)
        key_docs = document_ids(doc_lengths[batch_index], all_positions).reshape(
            block_count, KEYBLK
        )
        head_queries = queries.reshape(row_count, HEADS, HEAD)
        log_total, mixed_sum, mixed_full = attend_forward(
            head_queries,
            key_value.reshape(block_count, KEYBLK, 2, HEADS, HEAD),
            query_docs,
            key_docs,
        )
        attended = mixed_sum.reshape(row_count, model_width).astype(jnp.bfloat16)
        first_sum = inputs.astype(jnp.float32) + (
            jnp.dot(attended, full_out, preferred_element_type=jnp.float32) + out_bias
        )
        normed = layer_norm(first_sum, gain_first, shift_first)
        normed_low = normed.astype(jnp.bfloat16)
        hidden = jnp.dot(normed_low, full_in, preferred_element_type=jnp.float32) + in_bias
        activated = exact_gelu(hidden).astype(jnp.bfloat16)
        final_sum = normed + (
            jnp.dot(activated, full_back, preferred_element_type=jnp.float32) + back_bias
        )
        outputs.append(layer_norm(final_sum, gain_second, shift_second).astype(jnp.bfloat16))
        kept_states.append(
            (
                inputs,
                head_queries,
                local_pair,
                key_value,
                query_docs,
                key_docs,
                log_total,
                mixed_full,
                attended,
                first_sum,
                normed_low,
                hidden,
                activated,
                final_sum,
            )
        )
    grad_sums = None
    input_grads = []
    for batch_index in range(micro_count):
        gathered = fetch_weights(
            w_qkv,
            w_out,
            w_in,
            w_back,
            b_query,
            b_value,
            b_out,
            b_in,
            b_back,
            gain_one,
            shift_one,
            gain_two,
            shift_two,
        )
        (
            full_qkv,
            full_out,
            full_in,
            full_back,
            query_bias,
            value_bias,
            out_bias,
            in_bias,
            back_bias,
            gain_first,
            shift_first,
            gain_second,
            shift_second,
        ) = gathered
        (
            inputs,
            head_queries,
            local_pair,
            key_value,
            query_docs,
            key_docs,
            log_total,
            mixed_full,
            attended,
            first_sum,
            normed_low,
            hidden,
            activated,
            final_sum,
        ) = kept_states[batch_index]
        upstream = cotangent[batch_index].astype(jnp.float32)
        grad_final, grad_gain_two, grad_shift_two = jax.vjp(
            layer_norm, final_sum, gain_second, shift_second
        )[1](upstream)
        grad_second = grad_final.astype(jnp.bfloat16)
        grad_back_bias = jnp.sum(grad_second.astype(jnp.float32), axis=0)
        grad_back_weight = jnp.einsum(
            "rk,rm->km", activated, grad_second, preferred_element_type=jnp.float32
        )
        grad_activated = jnp.einsum(
            "rm,km->rk", grad_second, full_back, preferred_element_type=jnp.float32
        )
        grad_hidden = jax.vjp(exact_gelu, hidden)[1](grad_activated)[0].astype(jnp.bfloat16)
        grad_in_bias = jnp.sum(grad_hidden.astype(jnp.float32), axis=0)
        grad_in_weight = jnp.einsum(
            "rm,rf->mf", normed_low, grad_hidden, preferred_element_type=jnp.float32
        )
        grad_normed = grad_final + jnp.einsum(
            "rf,mf->rm", grad_hidden, full_in, preferred_element_type=jnp.float32
        )
        grad_first, grad_gain_one, grad_shift_one = jax.vjp(
            layer_norm, first_sum, gain_first, shift_first
        )[1](grad_normed)
        grad_branch = grad_first.astype(jnp.bfloat16)
        grad_out_bias = jnp.sum(grad_branch.astype(jnp.float32), axis=0)
        grad_out_weight = jnp.einsum(
            "rk,rm->km", attended, grad_branch, preferred_element_type=jnp.float32
        )
        grad_attended = jnp.einsum(
            "rm,km->rk", grad_branch, full_out, preferred_element_type=jnp.float32
        ).astype(jnp.bfloat16)
        head_grad = grad_attended.reshape(row_count, HEADS, HEAD)
        delta = jnp.einsum("qhd,qhd->hq", head_grad.astype(jnp.float32), mixed_full)
        key_value_back = lax.all_gather(local_pair, "ctx", axis=0, tiled=True)
        blocked_pairs = key_value_back.reshape(block_count, KEYBLK, 2, HEADS, HEAD)
        grad_queries, block_grads = attend_backward(
            head_queries, blocked_pairs, query_docs, key_docs, log_total, delta, head_grad
        )
        pair_grads = lax.psum_scatter(
            block_grads.reshape(length, 2 * model_width).astype(jnp.bfloat16),
            "ctx",
            scatter_dimension=0,
            tiled=True,
        )
        grad_joined = jnp.concatenate(
            [grad_queries.reshape(row_count, model_width).astype(jnp.bfloat16), pair_grads], axis=1
        )
        grad_query_bias = jnp.sum(grad_joined[:, :model_width].astype(jnp.float32), axis=0)
        grad_value_bias = jnp.sum(grad_joined[:, 2 * model_width :].astype(jnp.float32), axis=0)
        grad_qkv_weight = jnp.einsum(
            "rm,rc->mc", inputs, grad_joined, preferred_element_type=jnp.float32
        )
        input_grads.append(
            grad_first
            + jnp.einsum("rc,mc->rm", grad_joined, full_qkv, preferred_element_type=jnp.float32)
        )
        batch_terms = (
            grad_qkv_weight,
            grad_out_weight,
            grad_in_weight,
            grad_back_weight,
            grad_query_bias,
            grad_value_bias,
            grad_out_bias,
            grad_in_bias,
            grad_back_bias,
            grad_gain_one,
            grad_shift_one,
            grad_gain_two,
            grad_shift_two,
        )
        if grad_sums is None:
            grad_sums = batch_terms
        else:
            grad_sums = tuple((older + newer for older, newer in zip(grad_sums, batch_terms)))
    owned = (
        lax.psum_scatter(
            grad_sums[0].astype(jnp.bfloat16), "fsdp", scatter_dimension=0, tiled=True
        ).astype(jnp.float32),
        lax.psum_scatter(
            grad_sums[1].astype(jnp.bfloat16), "fsdp", scatter_dimension=0, tiled=True
        ).astype(jnp.float32),
        lax.psum_scatter(
            grad_sums[2].astype(jnp.bfloat16), "fsdp", scatter_dimension=0, tiled=True
        ).astype(jnp.float32),
        lax.psum_scatter(
            grad_sums[3].astype(jnp.bfloat16), "fsdp", scatter_dimension=0, tiled=True
        ).astype(jnp.float32),
        lax.psum_scatter(
            grad_sums[4].astype(jnp.bfloat16), "fsdp", scatter_dimension=0, tiled=True
        ).astype(jnp.float32),
        lax.psum_scatter(
            grad_sums[5].astype(jnp.bfloat16), "fsdp", scatter_dimension=0, tiled=True
        ).astype(jnp.float32),
        lax.psum_scatter(
            grad_sums[6].astype(jnp.bfloat16), "fsdp", scatter_dimension=0, tiled=True
        ).astype(jnp.float32),
        lax.psum_scatter(
            grad_sums[7].astype(jnp.bfloat16), "fsdp", scatter_dimension=0, tiled=True
        ).astype(jnp.float32),
        lax.psum_scatter(
            grad_sums[8].astype(jnp.bfloat16), "fsdp", scatter_dimension=0, tiled=True
        ).astype(jnp.float32),
        lax.psum_scatter(
            grad_sums[9].astype(jnp.bfloat16), "fsdp", scatter_dimension=0, tiled=True
        ).astype(jnp.float32),
        lax.psum_scatter(
            grad_sums[10].astype(jnp.bfloat16), "fsdp", scatter_dimension=0, tiled=True
        ).astype(jnp.float32),
        lax.psum_scatter(
            grad_sums[11].astype(jnp.bfloat16), "fsdp", scatter_dimension=0, tiled=True
        ).astype(jnp.float32),
        lax.psum_scatter(
            grad_sums[12].astype(jnp.bfloat16), "fsdp", scatter_dimension=0, tiled=True
        ).astype(jnp.float32),
    )
    summed = (
        lax.psum(owned[0].astype(jnp.bfloat16), "ctx").astype(jnp.float32),
        lax.psum(owned[1].astype(jnp.bfloat16), "ctx").astype(jnp.float32),
        lax.psum(owned[2].astype(jnp.bfloat16), "ctx").astype(jnp.float32),
        lax.psum(owned[3].astype(jnp.bfloat16), "ctx").astype(jnp.float32),
        lax.psum(owned[4].astype(jnp.bfloat16), "ctx").astype(jnp.float32),
        lax.psum(owned[5].astype(jnp.bfloat16), "ctx").astype(jnp.float32),
        lax.psum(owned[6].astype(jnp.bfloat16), "ctx").astype(jnp.float32),
        lax.psum(owned[7].astype(jnp.bfloat16), "ctx").astype(jnp.float32),
        lax.psum(owned[8].astype(jnp.bfloat16), "ctx").astype(jnp.float32),
        lax.psum(owned[9].astype(jnp.bfloat16), "ctx").astype(jnp.float32),
        lax.psum(owned[10].astype(jnp.bfloat16), "ctx").astype(jnp.float32),
        lax.psum(owned[11].astype(jnp.bfloat16), "ctx").astype(jnp.float32),
        lax.psum(owned[12].astype(jnp.bfloat16), "ctx").astype(jnp.float32),
    )
    return (
        jnp.stack(outputs),
        jnp.stack(input_grads),
        summed[0],
        summed[1],
        summed[2],
        summed[3],
        summed[4],
        summed[5],
        summed[6],
        summed[7],
        summed[8],
        summed[9],
        summed[10],
        summed[11],
        summed[12],
    )


def solution(mesh):
    placed = (
        P("fsdp", "ctx", None),
        P("fsdp", "ctx", None),
        P("fsdp", None),
        P("fsdp", None),
        P("fsdp", None),
        P("fsdp", None),
        P("fsdp", None),
        P("fsdp"),
        P("fsdp"),
        P("fsdp"),
        P("fsdp"),
        P("fsdp"),
        P("fsdp"),
        P("fsdp"),
        P("fsdp"),
        P("fsdp"),
    )
    return jax.shard_map(
        shards,
        mesh=mesh,
        in_specs=placed,
        out_specs=(
            P("fsdp", "ctx", None),
            P("fsdp", "ctx", None),
            P("fsdp", None),
            P("fsdp", None),
            P("fsdp", None),
            P("fsdp", None),
            P("fsdp"),
            P("fsdp"),
            P("fsdp"),
            P("fsdp"),
            P("fsdp"),
            P("fsdp"),
            P("fsdp"),
            P("fsdp"),
            P("fsdp"),
        ),
        check_vma=False,
    )
```

profile of v0, /device:TPU:9, one launch (start us, length us, event | category | flops | bytes accessed | tf_op | source)
XLA Modules:
  0.0 991.2 jit_solution(13888492631917994399)
XLA Ops:
  8.0 3.2 all-gather
  11.2 48.9 %all-gather.16.cloned.1.call-done = bf16[768,2304]{1,0:T(8,128)(2,1)} async-done(((bf16[384,2304]{1,0:T(8,128)(2,1)}), bf16[768,2304]{1,0:T(8,128)(2,1)}) %all-gather.16.cloned.1.call-update) | async-done | bytes 3538960 | tf_op jit(solution)/shard_map/all_gather | solution.py:47
  60.1 2.8 fusion.139
  76.6 3.5 all-gather.1
  82.6 3.5 all-gather.2
  88.7 3.2 all-gather.6
  94.4 3.5 all-gather.3
  100.5 3.5 all-gather.4
  106.5 3.5 all-gather.7
  112.5 3.2 all-gather.8
  118.3 3.7 all-gather.5
  128.9 8.7 copy.118
  137.5 11.2 %reshape.431 = bf16[4,512,2,12,64]{1,0,4,3,2:T(4,128)(2,1)} reshape(bf16[2048,1536]{0,1:T(8,128)(2,1)} %copy.118) | data formatting | bytes 12582912 | tf_op jit(solution)/shard_map/reshape | solution.py:215
  148.7 7.0 copy.121
  155.7 16.1 %while.78 = (s32[]{:T(128)}, f32[12,128]{1,0:T(8,128)S(1)}, f32[12,128]{1,0:T(8,128)S(1)}, s32[128]{0:T(128)S(1)}, s32[4,512]{1,0:T(4,128)}, /*index=5*/bf16[4,5...) while((s32[]{:T(128)}, f32[12,128]{1,0:T(8,128)S(1)}, ...), condition=%wide.region_6.7_spmd.clone, body=%wide.region_3.6_spmd.clone.sunk | while | flops 107027968 | bytes 10703480 | solution.py:88
  171.8 21.9 %while.79 = (s32[]{:T(128)}, f32[128,12,64]{0,2,1:T(8,128)S(1)}, f32[128,12,64]{0,2,1:T(8,128)S(1)}, bf16[4,512,2,12,64]{1,4,3,2,0:T(8,128)(2,1)}, s32[128]{0:T(...) while((s32[]{:T(128)}, f32[128,12,64]{0,2,1:T(8,128)S(1)}, ...), condition=%wide.region_8.9_spmd.clone, body=%wide.region_7.8_spmd.clone.sunk | while | flops 312672256 | bytes 16931456 | solution.py:109
  193.9 8.9 copy.122
  202.8 11.1 %reshape.436 = bf16[4,512,2,12,64]{1,0,4,3,2:T(4,128)(2,1)} reshape(bf16[2048,1536]{0,1:T(8,128)(2,1)} %copy.122) | data formatting | bytes 12582912 | tf_op jit(solution)/shard_map/reshape | solution.py:215
  213.9 7.0 copy.125
  221.0 13.6 %while.80 = (s32[]{:T(128)}, f32[12,128]{1,0:T(8,128)S(1)}, f32[12,128]{1,0:T(8,128)S(1)}, s32[128]{0:T(128)S(1)}, s32[4,512]{1,0:T(4,128)S(1)}, /*index=5*/bf16...) while((s32[]{:T(128)}, f32[12,128]{1,0:T(8,128)S(1)}, ...), condition=%wide.region_19.20_spmd.clone, body=%wide.region_16.19_spmd.clone.sunk | while | flops 107027968 | bytes 10703480 | solution.py:88
  221.1 1.7 dynamic-slice_bitcast_fusion.14
  234.6 19.5 %while.81 = (s32[]{:T(128)}, f32[128,12,64]{0,2,1:T(8,128)S(1)}, f32[128,12,64]{0,2,1:T(8,128)S(1)}, bf16[4,512,2,12,64]{1,4,3,2,0:T(8,128)(2,1)}, s32[128]{0:T(...) while((s32[]{:T(128)}, f32[128,12,64]{0,2,1:T(8,128)S(1)}, ...), condition=%wide.region_21.22_spmd.clone, body=%wide.region_20.21_spmd.clone.sunk | while | flops 312672256 | bytes 16931456 | solution.py:109
  255.0 1.8 fusion.169
  257.8 19.3 %all-gather.22.cloned.1.call-done = bf16[768,3072]{1,0:T(8,128)(2,1)} async-done(((bf16[384,3072]{1,0:T(8,128)(2,1)}), bf16[768,3072]{1,0:T(8,128)(2,1)}) %all-gather.22.cloned.1.call-update) | async-done | bytes 4718608 | tf_op jit(solution)/shard_map/all_gather | solution.py:49
  277.1 8.5 multiply_convert_fusion.1
  285.6 55.6 %all-gather.24.cloned.1.call-done = bf16[3072,768]{1,0:T(8,128)(2,1)} async-done(((bf16[1536,768]{1,0:T(8,128)(2,1)}), bf16[3072,768]{1,0:T(8,128)(2,1)}) %all-gather.24.cloned.1.call-update) | async-done | bytes 4718608 | tf_op jit(solution)/shard_map/all_gather | solution.py:50
  341.2 3.6 fusion.168
  345.1 4.2 multiply_convert_fusion
  354.1 2.5 convert_reduce_fusion
  356.6 1.7 convolution_add_fusion.5
  358.8 2.5 convert_reduce_fusion.1
  361.2 2.4 multiply_reduce_fusion.1
  367.5 3.4 broadcast.462.clone.1
  370.9 32.1 %while.82 = (s32[]{:T(128)}, f32[128,12,64]{0,2,1:T(8,128)S(1)}, bf16[4,512,2,12,64]{1,4,3,2,0:T(8,128)(2,1)}, bf16[4,512,2,12,64]{1,4,3,2,0:T(8,128)(2,1)}, s32...) while((s32[]{:T(128)}, f32[128,12,64]{0,2,1:T(8,128)S(1)}, ...), condition=%wide.region_31.32_spmd.clone, body=%wide.region_30.31_spmd.clone.sunk | while | flops 516947968 | bytes 26178196 | solution.py:138
  403.1 11.3 %copy.128 = bf16[4,512,2,12,64]{1,0,4,3,2:T(4,128)(2,1)} copy(bf16[4,512,2,12,64]{1,4,3,2,0:T(8,128)(2,1)} %get-tuple-element.291) | data formatting | bytes 12582912 | tf_op jit(solution)/shard_map/convert_element_type | solution.py:337
  414.4 8.1 copy.167
  422.4 8.6 copy.159
  433.6 3.4 broadcast.462.clone
  437.0 29.9 %while.83 = (s32[]{:T(128)}, f32[128,12,64]{0,2,1:T(8,128)S(1)}, bf16[4,512,2,12,64]{1,4,3,2,0:T(8,128)(2,1)}, bf16[4,512,2,12,64]{1,4,3,2,0:T(8,128)(2,1)}, s32...) while((s32[]{:T(128)}, f32[128,12,64]{0,2,1:T(8,128)S(1)}, ...), condition=%wide.region_38.39_spmd.clone, body=%wide.region_37.38_spmd.clone.sunk | while | flops 516947968 | bytes 26178196 | solution.py:138
  467.7 8.5 copy.131
  476.2 5.4 copy.168
  481.6 8.8 copy.161
  491.8 23.8 %reduce-scatter.19.cloned.1.call-done = bf16[128,1536]{1,0:T(8,128)(2,1)} async-done(((bf16[2048,1536]{1,0:T(8,128)(2,1)}), bf16[128,1536]{1,0:T(8,128)(2,1)}) %reduce-scatter.19.cloned.1.call-update) | async-done | bytes 393232
  516.8 4.0 fusion.133
  520.8 83.8 %reduce-scatter.21.cloned.1.call-done = bf16[128,1536]{1,0:T(8,128)(2,1)} async-done(((bf16[2048,1536]{1,0:T(8,128)(2,1)}), bf16[128,1536]{1,0:T(8,128)(2,1)}) %reduce-scatter.21.cloned.1.call-update) | async-done | bytes 393232
  605.8 6.0 fusion.96
  611.8 6.0 copy.163
  623.5 3.7 add_convert_fusion.1
  629.8 3.6 add_convert_fusion
  633.5 32.4 %reduce-scatter.23.cloned.1.call-done = bf16[384,2304]{1,0:T(8,128)(2,1)} async-done(((bf16[768,2304]{1,0:T(8,128)(2,1)}), bf16[384,2304]{1,0:T(8,128)(2,1)}) %reduce-scatter.23.cloned.1.call-update) | async-done | bytes 1769488
  665.9 3.9 copy.164
  669.8 20.7 %reduce-scatter.13.cloned.1.call-done = bf16[384,768]{1,0:T(8,128)(2,1)} async-done(((bf16[768,768]{1,0:T(8,128)(2,1)}), bf16[384,768]{1,0:T(8,128)(2,1)}) %reduce-scatter.13.cloned.1.call-update) | async-done | bytes 589840 | tf_op jit(solution)/shard_map/reduce_scatter | solution.py:377
  690.5 62.9 %reduce-scatter.15.cloned.1.call-done = bf16[384,3072]{1,0:T(8,128)(2,1)} async-done(((bf16[768,3072]{1,0:T(8,128)(2,1)}), bf16[384,3072]{1,0:T(8,128)(2,1)}) %reduce-scatter.15.cloned.1.call-update) | async-done | bytes 2359312 | tf_op jit(solution)/shard_map/reduce_scatter | solution.py:380
  753.4 62.9 %reduce-scatter.17.cloned.1.call-done = bf16[1536,768]{1,0:T(8,128)(2,1)} async-done(((bf16[3072,768]{1,0:T(8,128)(2,1)}), bf16[1536,768]{1,0:T(8,128)(2,1)}) %reduce-scatter.17.cloned.1.call-update) | async-done | bytes 2359312 | tf_op jit(solution)/shard_map/reduce_scatter | solution.py:383
  819.0 1.7 convert_reduce_fusion.2
  822.0 1.8 pad_maximum_fusion.3
  833.1 7.4 all-reduce.12
  850.6 50.2 %all-reduce.10 = (bf16[384]{0:T(512)(128)(2,1)}, bf16[384]{0:T(512)(128)(2,1)}, bf16[384]{0:T(512)(128)(2,1)}, bf16[1536]{0:T(1024)(128)(2,1)S(1)}, bf16[384]{0:...) all-reduce(bf16[384]{0:T(512)(128)(2,1)S(1)} %dynamic-slice.1, ...), channel_id=1, replica_groups=mesh['ctx'=16,'fsdp'=2] {'ctx'}, use_global_device_ids=true, to_apply=%region_51.52 | all-reduce | flops 4608 | bytes 18432 | tf_op jit(solution)/shard_map/psum | solution.py:419
  911.5 2.6 fusion.111
  916.3 56.5 %all-reduce.15.cloned.1.call-done = (bf16[384,2304]{0,1:T(8,128)(2,1)}, bf16[384,768]{1,0:T(8,128)(2,1)}, bf16[384,3072]{1,0:T(8,128)(2,1)}, bf16[1536,768]{1,0:T(8,128)(2,1)}) async-done(((bf16[384,2304]{0,1:T(8,128)(2,1)}, bf16[384,768]{1,0:T(8,128)(2,1)}, bf16[384,3072]{1,0:T(8,128)(2,1)}, bf16[1536,768]{1,0:T(8,128)(2,1)}), (bf16[384,2304]{0,1:T(8,128)(2,1)}, bf16[384,768]{1,0:T(8,128)(2,1)}, ...) | async-done | bytes 7077904 | tf_op jit(solution)/shard_map/psum | solution.py:415
  972.8 2.2 convert_element_type.386
  975.0 4.2 copy.132
  979.2 2.8 convert_element_type.388
  981.9 2.5 convert_element_type.390
  (514 shorter events, 229.7 us)
Async XLA Ops:
  7.2 53.0 %copy-start.16 = (bf16[2,128,768]{2,1,0:T(8,128)(2,1)S(1)}, bf16[2,128,768]{2,1,0:T(8,128)(2,1)}, u32[]{:S(2)}) copy-start(bf16[2,128,768]{2,1,0:T(8,128)(2,1)} %param.28) | copy-start | bytes 1179652
  7.2 52.9 %all-gather.16.cloned.1.call-start = ((), (), s32[]{:S(2)}) async-start(), calls=%async_computation.6 | async-start | bytes 5308416 | tf_op jit(solution)/shard_map/all_gather | solution.py:47
  7.9 120.9 %all-gather.18.cloned.1.call-start = ((), (), s32[]{:S(2)}) async-start(), calls=%async_computation.7 | async-start | bytes 6684672 | tf_op jit(solution)/shard_map/all_gather | solution.py:207
  60.1 3.1 copy-start
  64.9 129.0 %all-gather.26.cloned.1.call-start = ((), (), s32[]{:S(2)}) async-start(), calls=%async_computation.11 | async-start | bytes 6684672 | tf_op jit(solution)/shard_map/all_gather | solution.py:207
  65.6 189.3 %all-gather.20.cloned.1.call-start = ((), (), s32[]{:S(2)}) async-start(), calls=%async_computation.8 | async-start | bytes 1769472 | tf_op jit(solution)/shard_map/all_gather | solution.py:48
  66.2 210.9 %all-gather.22.cloned.1.call-start = ((), (), s32[]{:S(2)}) async-start(), calls=%async_computation.9 | async-start | bytes 7077888 | tf_op jit(solution)/shard_map/all_gather | solution.py:49
  66.8 274.4 %all-gather.24.cloned.1.call-start = ((), (), s32[]{:S(2)}) async-start(), calls=%async_computation.10 | async-start | bytes 7077888 | tf_op jit(solution)/shard_map/all_gather | solution.py:50
  67.3 448.2 %reduce-scatter.19.cloned.1.call-start = ((), (), s32[]{:S(2)}) async-start(), calls=%async_computation.15 | async-start | bytes 6684672
  148.7 7.0 copy-start.56
  148.7 7.0 copy-start.62
  155.7 16.1 %copy-start.53 = (f32[128,12,64]{0,2,1:T(8,128)S(1)}, f32[128,12,64]{0,2,1:T(8,128)}, u32[]{:S(2)}) copy-start(f32[128,12,64]{0,2,1:T(8,128)} %custom-call.3) | copy-start | bytes 1179652
  193.8 9.0 copy-start.54
  193.8 9.0 copy-start.63
  193.8 9.0 copy-start.74
  193.8 60.4 %copy-start.43 = (f32[128,12,64]{0,2,1:T(8,128)}, f32[128,12,64]{0,2,1:T(8,128)S(1)}, u32[]{:S(2)}) copy-start(f32[128,12,64]{0,2,1:T(8,128)S(1)} %get-tuple-element.285) | copy-start | bytes 1179652
  213.9 7.0 copy-start.55
  213.9 7.0 copy-start.58
  213.9 7.0 copy-start.59
  220.9 13.7 %copy-start.50 = (f32[128,12,64]{0,2,1:T(8,128)S(1)}, f32[128,12,64]{0,2,1:T(8,128)}, u32[]{:S(2)}) copy-start(f32[128,12,64]{0,2,1:T(8,128)} %custom-call.7) | copy-start | bytes 1179652
  234.6 20.3 %copy-start.67 = (f32[768]{0:T(1024)S(1)}, f32[768]{0:T(1024)}, u32[]{:S(2)}) copy-start(f32[768]{0:T(1024)} %reshape.462) | copy-start | bytes 9220
  254.2 2.6 copy-start.41
  254.3 3.2 copy-start.35
  256.8 106.9 %copy-start.4 = (f32[128,768]{1,0:T(8,128)}, f32[128,768]{1,0:T(8,128)S(1)}, u32[]{:S(2)}) copy-start(f32[128,768]{1,0:T(8,128)S(1)} %get-tuple-element.915) | copy-start | bytes 1179652
  256.8 20.3 %copy-start.49 = (f32[768]{0:T(1024)S(1)}, f32[768]{0:T(1024)}, u32[]{:S(2)}) copy-start(f32[768]{0:T(1024)} %reshape.463) | copy-start | bytes 9220
  256.8 20.3 %copy-start.57 = (f32[768]{0:T(1024)S(1)}, f32[768]{0:T(1024)}, u32[]{:S(2)}) copy-start(f32[768]{0:T(1024)} %reshape.464) | copy-start | bytes 9220
  256.8 20.3 %copy-start.71 = (f32[2,1,1536]{2,1,0:T(1,128)S(1)}, f32[2,1,1536]{2,1,0:T(1,128)}, u32[]{:S(2)}) copy-start(f32[2,1,1536]{2,1,0:T(1,128)} %convert_element_type.424) | copy-start | bytes 36868
  257.7 105.9 %copy-start.72 = (f32[128]{0:T(128)}, f32[128]{0:T(128)S(1)}, u32[]{:S(2)}) copy-start(f32[128]{0:T(128)S(1)} %fusion.150) | copy-start | bytes 1540
  257.8 105.9 %copy-start.69 = (f32[128]{0:T(128)}, f32[128]{0:T(128)S(1)}, u32[]{:S(2)}) copy-start(f32[128]{0:T(128)S(1)} %fusion.148) | copy-start | bytes 1540
  277.1 64.1 %copy-start.66 = (f32[768]{0:T(1024)S(1)}, f32[768]{0:T(1024)}, u32[]{:S(2)}) copy-start(f32[768]{0:T(1024)} %reshape.466) | copy-start | bytes 9220
  341.2 4.0 copy-start.2
  341.2 8.1 slice-start
  345.1 4.2 slice-start.1
  353.4 4.9 copy-start.45
  364.9 66.2 %copy-start.80 = (f32[128]{0:T(128)}, f32[128]{0:T(128)S(1)}, u32[]{:S(2)}) copy-start(f32[128]{0:T(128)S(1)} %negate_multiply_fusion.2) | copy-start | bytes 1540
  365.7 5.2 copy-start.37
  367.5 3.4 copy-start.9
  367.5 3.4 copy-start.64
  367.5 3.4 copy-start.75
  403.0 11.3 %copy-start.10 = (f32[128,12,64]{0,2,1:T(8,128)}, f32[128,12,64]{0,2,1:T(8,128)S(1)}, u32[]{:S(2)}) copy-start(f32[128,12,64]{0,2,1:T(8,128)S(1)} %get-tuple-element.290) | copy-start | bytes 1179652
  431.1 173.5 %reduce-scatter.21.cloned.1.call-start = ((), (), s32[]{:S(2)}) async-start(), calls=%async_computation.16 | async-start | bytes 6684672
  433.6 3.4 copy-start.6
  433.6 3.4 copy-start.61
  433.6 3.4 copy-start.77
  490.4 26.4 %copy-start.17 = (bf16[2,128,768]{2,1,0:T(8,128)(2,1)S(1)}, bf16[2,128,768]{2,1,0:T(8,128)(2,1)}, u32[]{:S(2)}) copy-start(bf16[2,128,768]{2,1,0:T(8,128)(2,1)} %param.28) | copy-start | bytes 1179652
  490.4 175.5 %reduce-scatter.23.cloned.1.call-start = ((), (), s32[]{:S(2)}) async-start(), calls=%async_computation.17 | async-start | bytes 5308416
  491.6 114.3 %copy-start.32 = (bf16[128,12,64]{0,2,1:T(8,128)(2,1)}, bf16[128,12,64]{0,2,1:T(8,128)(2,1)S(1)}, u32[]{:S(2)}) copy-start(bf16[128,12,64]{0,2,1:T(8,128)(2,1)S(1)} %get-tuple-element.874) | copy-start | bytes 589828
  491.8 29.0 %copy-start.30 = (bf16[128,12,64]{0,2,1:T(8,128)(2,1)}, bf16[128,12,64]{0,2,1:T(8,128)(2,1)S(1)}, u32[]{:S(2)}) copy-start(bf16[128,12,64]{0,2,1:T(8,128)(2,1)S(1)} %get-tuple-element.876) | copy-start | bytes 589828
  516.8 4.0 copy-start.12
  605.8 6.0 copy-start.14
  617.9 72.6 %reduce-scatter.13.cloned.1.call-start = ((), (), s32[]{:S(2)}) async-start(), calls=%async_computation.12 | async-start | bytes 1769472 | tf_op jit(solution)/shard_map/reduce_scatter | solution.py:377
  620.8 2.6 copy-start.5
  620.8 2.6 copy-start.23
  620.8 2.6 copy-start.73
  620.9 132.5 %reduce-scatter.15.cloned.1.call-start = ((), (), s32[]{:S(2)}) async-start(), calls=%async_computation.13 | async-start | bytes 7077888 | tf_op jit(solution)/shard_map/reduce_scatter | solution.py:380
  627.2 189.0 %reduce-scatter.17.cloned.1.call-start = ((), (), s32[]{:S(2)}) async-start(), calls=%async_computation.14 | async-start | bytes 7077888 | tf_op jit(solution)/shard_map/reduce_scatter | solution.py:383
  633.4 339.4 %all-reduce.15.cloned.1.call-start = ((), (), s32[]{:S(2)}) async-start(), calls=%async_computation.18 | async-start | bytes 14155776 | tf_op jit(solution)/shard_map/psum | solution.py:415
  816.2 95.2 %copy-start.1 = (bf16[768,2304]{1,0:T(8,128)(2,1)S(1)}, bf16[768,2304]{1,0:T(8,128)(2,1)}, u32[]{:S(2)}) copy-start(bf16[768,2304]{1,0:T(8,128)(2,1)} %all-gather.16.cloned.1.call-done) | copy-start | bytes 10616836
  911.5 2.6 copy-start.13
  911.5 2.6 copy-start.19
  911.5 2.6 copy-start.31
  911.5 2.6 copy-start.79
  975.0 4.2 copy-start.29
  979.1 2.8 copy-start.28
  (35 other events, 53.9 us)
Sparse Core Ops, SparseCore 0:
  9.6 50.5 all-gather.15
  65.0 62.2 all-gather.17
  130.1 60.4 all-gather.25
  192.0 20.9 all-gather.19
  214.4 62.6 all-gather.21
  278.5 62.6 all-gather.23
  431.2 84.3 reduce-scatter.18
  520.0 84.5 reduce-scatter.20
  618.0 47.9 reduce-scatter.22
  668.7 21.7 reduce-scatter.12
  693.3 59.9 reduce-scatter.14
  756.2 59.9 reduce-scatter.16
  820.9 151.9 all-reduce.14
where the time goes:
time: 1000 us; the launch traced here: 991 us
  waiting for transfers between devices  470 us (47%)
  local copies, waits for them, and re-layouts  215 us (22%)
  matrix products  124 us (12%)
  blocking collectives  88.2 us (9%)
  other arithmetic  75.2 us (8%)
  between operations  16.6 us (2%)
    unnamed x16, waiting for transfers between devices  143 us
    unnamed x203, local copies, waits for them, and re-layouts  85.7 us
    reduce_scatter x1, waiting for transfers between devices, shards(): lax.psum_scatter(grad_sums[2].astype(jnp.bfloat16), 'fsdp', scatter_dimen...  62.9 us
    reduce_scatter x1, waiting for transfers between devices, shards(): lax.psum_scatter(grad_sums[3].astype(jnp.bfloat16), 'fsdp', scatter_dimen...  62.9 us
    psum x1, waiting for transfers between devices, shards(): lax.psum(owned[0].astype(jnp.bfloat16), 'ctx').astype(jnp.float32)  56.5 us
    all_gather x1, waiting for transfers between devices, fetch_weights(): lax.all_gather(w_back, 'fsdp', axis=0, tiled=True)  55.6 us
    psum x1, blocking collectives, shards(): lax.psum(owned[4].astype(jnp.bfloat16), 'ctx').astype(jnp.float32)  50.2 us
    all_gather x1, waiting for transfers between devices, fetch_weights(): lax.all_gather(w_qkv, 'fsdp', axis=0, tiled=True)  48.9 us
  transfers between devices with their start and end apart: 13, of which 10 were waited for; matrix products, arithmetic and copies ran while one was open for 29% of the time, Pallas kernels for 0%

commit v1 on v0

v1 whole, which is shorter than its diff:
```python
import functools

import jax
import jax.numpy as jnp
from jax import lax
from jax.experimental import pallas as pl
from jax.experimental.pallas import tpu as pltpu
from jax.sharding import PartitionSpec as P

MESH = pl.DeviceIdType.MESH
DMA = pltpu.SemaphoreType.DMA
F32, BF16 = jnp.float32, jnp.bfloat16
EPSILON = 1e-12

def place(cols):
    index = lax.axis_index("ctx")
    return index // (2 * cols), lax.rem(index // 2, cols), lax.rem(index, 2), lax.axis_index("fsdp")

def device(a, b, c, f, cols):
    return {"ctx": (a * cols + b) * 2 + c, "fsdp": f}

def meet(peers):
    barrier = pltpu.get_barrier_semaphore()
    for peer in peers:
        pl.semaphore_signal(barrier, inc=1, device_id=peer, device_id_type=MESH)
    pl.semaphore_wait(barrier, len(peers))

def remote(source, target, send, recv, peer):
    return pltpu.make_async_remote_copy(
        src_ref=source, dst_ref=target, send_sem=send, recv_sem=recv, device_id=peer, device_id_type=MESH)

def gather_kernel(nf, cols, count, *refs):
    shards, tiny, fulls, tiny_out = refs[:count], refs[count], refs[count+1:2*count+1], refs[2*count+1]
    local_sem, s1, r1, s2, r2, s3, r3, st, rt = refs[2*count+2:]
    a, b, c, f = place(cols)
    other = 1 - c
    fpeers = [device(a, b, c, lax.rem(f + j, nf), cols) for j in range(1, nf)]
    bpeers = [device(a, lax.rem(b + k, cols), c, f, cols) for k in range(1, cols)]
    sibling = device(a, b, other, f, cols)
    meet(fpeers + bpeers + [sibling])

    def view(w, owner, bb, cc, base=0):
        rows, wide = shards[w].shape
        part, half = rows // cols, wide // 2
        return fulls[w].at[pl.ds(pl.multiple_of(owner * rows + bb * part, 8), part), pl.ds(pl.multiple_of(cc * half, 128), half)]

    waits = []
    for j in range(1, nf):
        cp = remote(tiny, tiny_out.at[f], st.at[j - 1], rt.at[j - 1], fpeers[j - 1])
        cp.start()
        waits.append(cp)
    locals_ = [pltpu.make_async_copy(tiny, tiny_out.at[f], local_sem.at[count])]
    locals_[0].start()
    first = {}
    for w in range(count):
        rows, wide = shards[w].shape
        part, half = rows // cols, wide // 2
        mine = shards[w].at[pl.ds(pl.multiple_of(b * part, 8), part), pl.ds(pl.multiple_of(c * half, 128), half)]
        for j in range(1, nf):
            cp = remote(mine, view(w, f, b, c), s1.at[w, j - 1], r1.at[w, j - 1], fpeers[j - 1])
            cp.start()
            first[w, j] = cp
    for w in range(count):
        rows = shards[w].shape[0]
        cp = pltpu.make_async_copy(shards[w], fulls[w].at[pl.ds(pl.multiple_of(f * rows, 8), rows)], local_sem.at[w])
        cp.start()
        locals_.append(cp)
    second, third = {}, []
    for w in range(count):
        for j in range(1, nf):
            owner = lax.rem(f + nf - j, nf)
            first[w, j].wait_recv()
            piece = view(w, owner, b, c)
            for k in range(1, cols):
                slot = (j - 1) * (cols - 1) + k - 1
                cp = remote(piece, piece, s2.at[w, slot], r2.at[w, slot], bpeers[k - 1])
                cp.start()
                second[w, j, k] = cp
            cp = remote(piece, piece, s3.at[w, (j - 1) * cols], r3.at[w, (j - 1) * cols], sibling)
            cp.start()
            third.append(cp)
    for w in range(count):
        for j in range(1, nf):
            owner = lax.rem(f + nf - j, nf)
            for k in range(1, cols):
                second[w, j, k].wait_recv()
                piece = view(w, owner, lax.rem(b + cols - k, cols), c)
                cp = remote(piece, piece, s3.at[w, (j - 1) * cols + k], r3.at[w, (j - 1) * cols + k], sibling)
                cp.start()
                third.append(cp)
    for cp in third:
        cp.wait_recv()
    for cp in waits:
        cp.wait()
    for cp in list(first.values()) + list(second.values()) + third:
        cp.wait_send()
    for cp in locals_:
        cp.wait()

def gather_weights(shards, tiny, nf, cols):
    count = len(shards)
    any_spec = pl.BlockSpec(memory_space=pl.ANY)
    dma = pltpu.SemaphoreType.DMA
    return pl.pallas_call(
        functools.partial(gather_kernel, nf, cols, count),
        out_shape=[jax.ShapeDtypeStruct((s.shape[0] * nf, s.shape[1]), s.dtype) for s in shards]
        + [jax.ShapeDtypeStruct((nf,) + tiny.shape, tiny.dtype)],
        in_specs=[pl.BlockSpec(memory_space=pltpu.VMEM)] * (count + 1),
        out_specs=[any_spec] * (count + 1),
        scratch_shapes=[dma((count + 1,)), dma((count, nf - 1)), dma((count, nf - 1)),
                        dma((count, (nf - 1) * (cols - 1))), dma((count, (nf - 1) * (cols - 1))),
                        dma((count, (nf - 1) * cols)), dma((count, (nf - 1) * cols)),
                        dma((nf - 1,)), dma((nf - 1,))],
        compiler_params=pltpu.CompilerParams(collective_id=1, has_side_effects=True, vmem_limit_bytes=32 << 20),
        name="gather_weights",
    )(*shards, tiny)

def octet(a, b, c, f, cols):
    me = a * 2 + c
    out = []
    for k in range(1, 8):
        other = lax.rem(me + k, 8)
        out.append((other, device(other // 2, b, lax.rem(other, 2), f, cols)))
    return me, out

def swap_kernel(cols, count, *refs):
    sources, targets = refs[:count], refs[count:2 * count]
    send, recv, here = refs[2 * count:]
    a, b, c, f = place(cols)
    me, peers = octet(a, b, c, f, cols)
    meet([p for _, p in peers])
    copies = []
    for k, (other, peer) in enumerate(peers):
        for i in range(count):
            cp = remote(sources[i].at[other], targets[i].at[me], send.at[i, k], recv.at[i, k], peer)
            cp.start()
            copies.append(cp)
    for i in range(count):
        cp = pltpu.make_async_copy(sources[i].at[me], targets[i].at[me], here.at[i])
        cp.start()
        copies.append(cp)
    for cp in copies:
        cp.wait()

def swap(arrays, cols, ident):
    count = len(arrays)
    return pl.pallas_call(
        functools.partial(swap_kernel, cols, count),
        out_shape=[jax.ShapeDtypeStruct(x.shape, x.dtype) for x in arrays],
        in_specs=[vmem()] * count, out_specs=[vmem()] * count,
        scratch_shapes=[DMA((count, 7)), DMA((count, 7)), DMA((count,))],
        compiler_params=pltpu.CompilerParams(collective_id=ident, has_side_effects=True, vmem_limit_bytes=16 << 20),
        name="swap",
    )(*arrays)

def spread_kernel(cols, q, kv, qg, full, sq, rq, sk, rk, s2, r2, here):
    a, b, c, f = place(cols)
    me, peers = octet(a, b, c, f, cols)
    bpeers = [device(a, lax.rem(b + k, cols), c, f, cols) for k in range(1, cols)]
    meet([p for _, p in peers] + bpeers)

    def slot(block, bb):
        return (block // 2 * cols + bb) * 2 + lax.rem(block, 2)

    first = []
    for k, (other, peer) in enumerate(peers):
        cp = remote(kv.at[other], full.at[slot(me, b)], sk.at[k], rk.at[k], peer)
        cp.start()
        first.append(cp)
    own = pltpu.make_async_copy(kv.at[me], full.at[slot(me, b)], here.at[0])
    own.start()
    ownq = pltpu.make_async_copy(q.at[me], qg.at[me], here.at[1])
    ownq.start()
    second = []
    for k, peer in enumerate(bpeers):
        cp = remote(kv.at[me], full.at[slot(me, b)], s2.at[7, k], r2.at[7, k], peer)
        cp.start()
        second.append(cp)
    third = []
    for k, (other, peer) in enumerate(peers):
        cp = remote(q.at[other], qg.at[me], sq.at[k], rq.at[k], peer)
        cp.start()
        third.append(cp)
    for k in range(7):
        first[k].wait_recv()
        source = lax.rem(me + 8 - (k + 1), 8)
        piece = full.at[slot(source, b)]
        for m, peer in enumerate(bpeers):
            cp = remote(piece, piece, s2.at[k, m], r2.at[k, m], peer)
            cp.start()
            second.append(cp)
    for cp in first:
        cp.wait_send()
    for cp in second + third:
        cp.wait()
    own.wait()
    ownq.wait()

def spread(q, kv, cols, ident):
    return pl.pallas_call(
        functools.partial(spread_kernel, cols),
        out_shape=[jax.ShapeDtypeStruct(q.shape, q.dtype), jax.ShapeDtypeStruct((8 * cols,) + kv.shape[1:], kv.dtype)],
        in_specs=[vmem()] * 2, out_specs=[vmem()] * 2,
        scratch_shapes=[DMA((7,))] * 4 + [DMA((8, max(cols - 1, 1)))] * 2 + [DMA((2,))],
        compiler_params=pltpu.CompilerParams(collective_id=ident, has_side_effects=True, vmem_limit_bytes=16 << 20),
        name="spread",
    )(q, kv)

def collect_kernel(cols, dq, dkv, dqo, dkvo, rbuf, total, sq, rq, sk, rk, s2, r2, here):
    a, b, c, f = place(cols)
    me, peers = octet(a, b, c, f, cols)
    bpeers = [(lax.rem(b + k, cols), device(a, lax.rem(b + k, cols), c, f, cols)) for k in range(1, cols)]
    meet([p for _, p in peers] + [p for _, p in bpeers])

    def slot(block, bb):
        return (block // 2 * cols + bb) * 2 + lax.rem(block, 2)

    order = [other for other, _ in peers] + [me]
    first = {}
    for n, block in enumerate(order):
        for k, (bb, peer) in enumerate(bpeers):
            cp = remote(dkv.at[slot(block, bb)], rbuf.at[k, n], s2.at[k, n], r2.at[k, n], peer)
            cp.start()
            first[k, n] = cp
    rest = []
    for k, (other, peer) in enumerate(peers):
        cp = remote(dq.at[other], dqo.at[me], sq.at[k], rq.at[k], peer)
        cp.start()
        rest.append(cp)
    own = pltpu.make_async_copy(dq.at[me], dqo.at[me], here.at[0])
    own.start()
    for n, block in enumerate(order):
        value = dkv[slot(block, b)].astype(F32)
        for k in range(cols - 1):
            first[k, n].wait_recv()
            value = value + rbuf[k, n].astype(F32)
        if n < 7:
            total[n] = value.astype(BF16)
            cp = remote(total.at[n], dkvo.at[me], sk.at[n], rk.at[n], peers[n][1])
            cp.start()
            rest.append(cp)
        else:
            dkvo[me] = value.astype(BF16)
    for cp in first.values():
        cp.wait_send()
    for cp in rest:
        cp.wait()
    own.wait()

def collect(dq, dkv, cols, ident):
    block = dkv.shape[1:]
    return pl.pallas_call(
        functools.partial(collect_kernel, cols),
        out_shape=[jax.ShapeDtypeStruct(dq.shape, dq.dtype), jax.ShapeDtypeStruct((8,) + block, dkv.dtype)],
        in_specs=[vmem()] * 2, out_specs=[vmem()] * 2,
        scratch_shapes=[pltpu.VMEM((max(cols - 1, 1), 8) + block, BF16), pltpu.VMEM((7,) + block, BF16)]
        + [DMA((7,))] * 4 + [DMA((max(cols - 1, 1), 8))] * 2 + [DMA((1,))],
        compiler_params=pltpu.CompilerParams(collective_id=ident, has_side_effects=True, vmem_limit_bytes=24 << 20),
        name="collect",
    )(dq, dkv)

def reduce_kernel(nf, cols, parts, grads, small, out, small_out, *refs):
    own, core_in, f_in, b_in, f_in2, b_in2, a_in, v_core, v_sum, v_f, v_b, v_a = refs[:12]
    load, sc, rc, s1, r1, s2, r2, s3, r3, s4, r4, s5, r5, s6, r6, sv, rv = refs[12:]
    a, b, c, f = place(cols)
    rows = grads.shape[5]
    fpeers = [(lax.rem(f + j, nf), device(a, b, c, lax.rem(f + j, nf), cols)) for j in range(1, nf)]
    bpeers = [(lax.rem(b + k, cols), device(a, lax.rem(b + k, cols), c, f, cols)) for k in range(1, cols)]
    apeers = [(lax.rem(a + k, 4), device(lax.rem(a + k, 4), b, c, f, cols)) for k in range(1, 4)]
    sibling = device(a, b, 1 - c, f, cols)
    meet([p for _, p in fpeers + bpeers + apeers] + [sibling])
    vector = remote(small, v_core, sv.at[0], rv.at[0], sibling)
    vector.start()
    order = [2, 1, 3, 0]
    dest = {k: lax.rem(a + k, 4) for k in range(4)}
    by_f = {k: k in (1, 2) for k in range(4)}
    loads, cores = {}, {}
    for k in order:
        for i in range(parts):
            cp = pltpu.make_async_copy(grads.at[c, dest[k], i], own.at[k, i], load.at[k, i])
            cp.start()
            loads[k, i] = cp
            cp = remote(grads.at[1 - c, dest[k], i], core_in.at[k, i], sc.at[k, i], rc.at[k, i], sibling)
            cp.start()
            cores[k, i] = cp
    one, two, three = {}, {}, {}
    vec = {}
    vector.wait_recv()
    v_sum[...] = small[...] + v_core[...]
    for j, (ff, peer) in enumerate(fpeers):
        vec[0, j] = remote(v_sum.at[ff], v_f.at[j], sv.at[1 + j], rv.at[1 + j], peer)
        vec[0, j].start()
    for k in order:
        for i in range(parts):
            loads[k, i].wait()
            cores[k, i].wait_recv()

            @pl.loop(0, nf * cols)
            def _(n):
                ff, bb = n // cols, lax.rem(n, cols)
                own[k, i, ff, bb] = (own[k, i, ff, bb].astype(F32) + core_in[k, i, ff, bb].astype(F32)).astype(BF16)

            if by_f[k]:
                for j, (ff, peer) in enumerate(fpeers):
                    cp = remote(own.at[k, i, ff], f_in.at[k, i, j], s1.at[k, i, j], r1.at[k, i, j], peer)
                    cp.start()
                    one[k, i, j] = cp
            else:
                for m, (bb, peer) in enumerate(bpeers):
                    for ff in range(nf):
                        cp = remote(own.at[k, i, ff, bb], b_in.at[k, i, m, ff], s1.at[k, i, m * nf + ff], r1.at[k, i, m * nf + ff], peer)
                        cp.start()
                        one[k, i, m * nf + ff] = cp
    value = v_sum[f]
    for j in range(nf - 1):
        vec[0, j].wait_recv()
        value = value + v_f[j]
    v_b[b] = value
    for m, (bb, peer) in enumerate(bpeers):
        vec[1, m] = remote(v_b.at[b], v_b.at[b], sv.at[nf + m], rv.at[nf + m], peer)
        vec[1, m].start()
    for k in order:
        for i in range(parts):
            if by_f[k]:
                for j in range(nf - 1):
                    one[k, i, j].wait_recv()

                @pl.loop(0, cols)
                def _(bb):
                    value = own[k, i, f, bb].astype(F32)
                    for j in range(nf - 1):
                        value = value + f_in[k, i, j, bb].astype(F32)
                    own[k, i, f, bb] = value.astype(BF16)

                for m, (bb, peer) in enumerate(bpeers):
                    cp = remote(own.at[k, i, f, bb], b_in2.at[k, i, m], s2.at[k, i, m], r2.at[k, i, m], peer)
                    cp.start()
                    two[k, i, m] = cp
            else:
                for m in range(cols - 1):
                    for ff in range(nf):
                        one[k, i, m * nf + ff].wait_recv()

                @pl.loop(0, nf)
                def _(ff):
                    value = own[k, i, ff, b].astype(F32)
                    for m in range(cols - 1):
                        value = value + b_in[k, i, m, ff].astype(F32)
                    own[k, i, ff, b] = value.astype(BF16)

                for j, (ff, peer) in enumerate(fpeers):
                    cp = remote(own.at[k, i, ff, b], f_in2.at[k, i, j], s2.at[k, i, j], r2.at[k, i, j], peer)
                    cp.start()
                    two[k, i, j] = cp
    for m in range(cols - 1):
        vec[1, m].wait_recv()
    value = v_b[0]
    for m in range(1, cols):
        value = value + v_b[m]
    v_a[a] = value
    for k in range(1, 4):
        vec[2, k] = remote(v_a.at[a], v_a.at[a], sv.at[nf + cols + k - 2], rv.at[nf + cols + k - 2], apeers[k - 1][1])
        vec[2, k].start()
    for k in order:
        for i in range(parts):
            value = own[k, i, f, b].astype(F32)
            if by_f[k]:
                for m in range(cols - 1):
                    two[k, i, m].wait_recv()
                    value = value + b_in2[k, i, m].astype(F32)
            else:
                for j in range(nf - 1):
                    two[k, i, j].wait_recv()
                    value = value + f_in2[k, i, j].astype(F32)
            if k != 0:
                own[k, i, f, b] = value.astype(BF16)
                cp = remote(own.at[k, i, f, b], a_in.at[k - 1, i], s3.at[k - 1, i], r3.at[k - 1, i], apeers[k - 1][1])
                cp.start()
                three[k, i] = cp
            else:
                own[k, i, f, b] = value.astype(BF16)
    for k in range(1, 4):
        vec[2, k].wait_recv()
    small_out[...] = v_a[0] + v_a[1] + v_a[2] + v_a[3]
    four, five, six = {}, {}, {}

    def piece(aa, bb, cc, i):
        return out.at[cc, aa, bb, i]

    pending = []
    for i in range(parts):
        value = own[0, i, f, b].astype(F32)
        for k in range(1, 4):
            three[k, i].wait_recv()
            value = value + a_in[k - 1, i].astype(F32)
        out[c, a, b, i] = value.astype(BF16)
        mine = piece(a, b, c, i)
        for k in (2, 1, 3):
            cp = remote(mine, mine, s4.at[k - 1, i], r4.at[k - 1, i], apeers[k - 1][1])
            cp.start()
            four[k, i] = cp
        for m, (bb, peer) in enumerate(bpeers):
            cp = remote(mine, mine, s5.at[0, i, m], r5.at[0, i, m], peer)
            cp.start()
            five[0, i, m] = cp
        cp = remote(mine, mine, s6.at[0, i, 0], r6.at[0, i, 0], sibling)
        cp.start()
        six[0, i, 0] = cp
    for i in range(parts):
        for k in (1, 3, 2):
            four[k, i].wait_recv()
            got = piece(lax.rem(a + 4 - k, 4), b, c, i)
            for m, (bb, peer) in enumerate(bpeers):
                cp = remote(got, got, s5.at[k, i, m], r5.at[k, i, m], peer)
                cp.start()
                five[k, i, m] = cp
            cp = remote(got, got, s6.at[k, i, 0], r6.at[k, i, 0], sibling)
            cp.start()
            six[k, i, 0] = cp
    for i in range(parts):
        for k in (0, 1, 3, 2):
            for m in range(cols - 1):
                five[k, i, m].wait_recv()
                got = piece(lax.rem(a + 4 - k, 4), lax.rem(b + cols - (m + 1), cols), c, i)
                cp = remote(got, got, s6.at[k, i, m + 1], r6.at[k, i, m + 1], sibling)
                cp.start()
                six[k, i, m + 1] = cp
    for cp in six.values():
        cp.wait_recv()
    vector.wait_send()
    for group in (cores, one, two, three, four, five, six, vec):
        for cp in group.values():
            cp.wait_send()

def reduce_grads(grads, small, nf, cols, ident):
    _, _, parts, _, _, rows, width = grads.shape
    block = (rows, width)
    m = max(cols - 1, 1)
    n = max((cols - 1) * nf, nf - 1)
    return pl.pallas_call(
        functools.partial(reduce_kernel, nf, cols, parts),
        out_shape=[jax.ShapeDtypeStruct((2, 4, cols, parts) + block, BF16), jax.ShapeDtypeStruct(small.shape[1:], F32)],
        in_specs=[pl.BlockSpec(memory_space=pl.ANY), vmem()], out_specs=[vmem()] * 2,
        scratch_shapes=[pltpu.VMEM((4, parts, nf, cols) + block, BF16), pltpu.VMEM((4, parts, nf, cols) + block, BF16),
                        pltpu.VMEM((4, parts, nf - 1, cols) + block, BF16), pltpu.VMEM((4, parts, m, nf) + block, BF16),
                        pltpu.VMEM((4, parts, nf - 1) + block, BF16), pltpu.VMEM((4, parts, m) + block, BF16),
                        pltpu.VMEM((3, parts) + block, BF16),
                        pltpu.VMEM(small.shape, F32), pltpu.VMEM(small.shape, F32), pltpu.VMEM((nf - 1,) + small.shape[1:], F32),
                        pltpu.VMEM((cols,) + small.shape[1:], F32), pltpu.VMEM((4,) + small.shape[1:], F32),
                        DMA((4, parts)), DMA((4, parts)), DMA((4, parts)), DMA((4, parts, n)), DMA((4, parts, n)),
                        DMA((4, parts, max(m, nf - 1))), DMA((4, parts, max(m, nf - 1))),
                        DMA((3, parts)), DMA((3, parts)), DMA((3, parts)), DMA((3, parts)),
                        DMA((4, parts, m)), DMA((4, parts, m)), DMA((4, parts, cols)), DMA((4, parts, cols)),
                        DMA((nf + cols + 2,)), DMA((nf + cols + 2,))],
        compiler_params=pltpu.CompilerParams(collective_id=ident, has_side_effects=True, vmem_limit_bytes=56 << 20),
        name="reduce_grads",
    )(grads, small)
KB = 256
SPAN = 256
MASKED = -1e30

def dot(x, y, dims):
    return lax.dot_general(x, y, (dims, ((), ())), preferred_element_type=F32)

NT = ((1,), (1,))
NN = ((1,), (0,))
TN = ((0,), (0,))

def bounds(lens, stream):
    ends, total = [], 0
    for j in range(4):
        total = total + lens[stream, j]
        ends.append(total)
    return ends

def doc_range(pos, ends):
    start = jnp.where(pos >= ends[0], ends[0], 0)
    stop = jnp.where(pos < ends[0], ends[0], ends[3])
    for j in (1, 2):
        start = jnp.where(pos >= ends[j], ends[j], start)
    for j in (2, 1, 0):
        stop = jnp.where(pos < ends[j], ends[j], stop)
    return start, stop

def block_range(base, ends):
    low, _ = doc_range(base, ends)
    _, high = doc_range(base + (SPAN - 1), ends)
    return low // KB, (high + (KB - 1)) // KB

def lane_head(shape, shift):
    lane = lax.broadcasted_iota(jnp.int32, shape, 1)
    return (lane - shift) // 64

def forward_kernel(cols, lens, q_ref, kv_ref, o_ref, ot_ref, lse_ref, qm, vt, acc):
    index = lax.axis_index("ctx")
    b, c = lax.rem(index // 2, cols), lax.rem(index, 2)
    ends = bounds(lens, c)
    total = kv_ref.shape[0]

    @pl.loop(0, total // KB)
    def _(n):
        rows = pl.ds(pl.multiple_of(n * KB, KB), KB)
        vt[:, rows] = kv_ref[rows, 128:384].astype(F32).T.astype(BF16)

    @pl.loop(0, 4)
    def _(stripe):
        base = SPAN * (stripe * cols + b)
        rows = pl.ds(pl.multiple_of(stripe * SPAN, SPAN), SPAN)
        head = lane_head((SPAN, 256), 0)
        q = q_ref[rows].astype(F32) * 0.125
        for h in range(3):
            qm[h] = jnp.where(head == h, q, 0.0).astype(BF16)
        qpos = base + lax.broadcasted_iota(jnp.int32, (1, SPAN), 1)
        start, stop = doc_range(qpos, ends)
        low, high = block_range(base, ends)
        acc[...] = jnp.zeros_like(acc)

        def step(n, state):
            krows = pl.ds(pl.multiple_of(n * KB, KB), KB)
            keys = kv_ref[krows, 0:256]
            kpos = n * KB + lax.broadcasted_iota(jnp.int32, (KB, 1), 0)
            allowed = (kpos >= start) & (kpos < stop)
            out = []
            for h in range(3):
                top, tot = state[h]
                s = jnp.where(allowed, dot(keys, qm[h], NT), MASKED)
                new = jnp.maximum(top, jnp.max(s, axis=0, keepdims=True))
                p = jnp.exp(s - new)
                scale = jnp.exp(top - new)
                hrows = pl.ds(64 * (h + 1), 64)
                acc[hrows] = acc[hrows] * scale + dot(vt[hrows, krows], p.astype(BF16), NN)
                out.append((new, tot * scale + jnp.sum(p, axis=0, keepdims=True)))
            return tuple(out)

        first = tuple((jnp.full((1, SPAN), MASKED, F32), jnp.zeros((1, SPAN), F32)) for _ in range(3))
        final = lax.fori_loop(low, high, step, first)
        for h in range(3):
            top, tot = final[h]
            hrows = pl.ds(64 * (h + 1), 64)
            acc[hrows] = acc[hrows] * (1.0 / tot)
            lse_ref[stripe, pl.ds(h, 1)] = top + jnp.log(tot)
        ot_ref[stripe] = acc[...]
        o_ref[rows] = acc[...].T.astype(BF16)

def vmem():
    return pl.BlockSpec(memory_space=pltpu.VMEM)

def attend_forward(lens, q, kv, cols):
    total = kv.shape[0]
    return pl.pallas_call(
        functools.partial(forward_kernel, cols),
        out_shape=[jax.ShapeDtypeStruct(q.shape, BF16), jax.ShapeDtypeStruct((4, 256, SPAN), F32),
                   jax.ShapeDtypeStruct((4, 8, SPAN), F32)],
        in_specs=[pl.BlockSpec(memory_space=pltpu.SMEM), vmem(), vmem()],
        out_specs=[vmem()] * 3,
        scratch_shapes=[pltpu.VMEM((3, SPAN, 256), BF16), pltpu.VMEM((256, total), BF16), pltpu.VMEM((256, SPAN), F32)],
        compiler_params=pltpu.CompilerParams(vmem_limit_bytes=32 << 20),
        name="attend_forward",
    )(lens, q, kv)

def backward_kernel(cols, lens, q_ref, kv_ref, do_ref, ot_ref, lse_ref, dq_ref, dkv_ref, qm, dm, kt, dk, dv, acc):
    index = lax.axis_index("ctx")
    b, c = lax.rem(index // 2, cols), lax.rem(index, 2)
    ends = bounds(lens, c)
    total = kv_ref.shape[0]

    @pl.loop(0, total // KB)
    def _(n):
        rows = pl.ds(pl.multiple_of(n * KB, KB), KB)
        kt[:, rows] = kv_ref[rows, 0:256].astype(F32).T.astype(BF16)
        dk[rows] = jnp.zeros((KB, 256), F32)
        dv[rows] = jnp.zeros((KB, 256), F32)

    @pl.loop(0, 4)
    def _(stripe):
        base = SPAN * (stripe * cols + b)
        rows = pl.ds(pl.multiple_of(stripe * SPAN, SPAN), SPAN)
        head = lane_head((SPAN, 256), 0)
        headv = lane_head((SPAN, 256), 64)
        q = q_ref[rows].astype(F32) * 0.125
        grad = do_ref[rows].astype(F32)
        for h in range(3):
            qm[h] = jnp.where(head == h, q, 0.0).astype(BF16)
            dm[h] = jnp.where(headv == h, grad, 0.0).astype(BF16)
        prod = grad.T * ot_ref[stripe]
        deltas = [jnp.sum(prod[64 * (h + 1):64 * (h + 2)], axis=0, keepdims=True) for h in range(3)]
        lses = [lse_ref[stripe, pl.ds(h, 1)] for h in range(3)]
        qpos = base + lax.broadcasted_iota(jnp.int32, (1, SPAN), 1)
        start, stop = doc_range(qpos, ends)
        low, high = block_range(base, ends)
        acc[...] = jnp.zeros_like(acc)

        @pl.loop(low, high)
        def _(n):
            krows = pl.ds(pl.multiple_of(n * KB, KB), KB)
            keys = kv_ref[krows, 0:256]
            vals = kv_ref[krows, 128:384]
            kpos = n * KB + lax.broadcasted_iota(jnp.int32, (KB, 1), 0)
            allowed = (kpos >= start) & (kpos < stop)
            newk, newv = dk[krows], dv[krows]
            for h in range(3):
                s = jnp.where(allowed, dot(keys, qm[h], NT), MASKED)
                p = jnp.exp(s - lses[h])
                gp = dot(vals, dm[h], NT)
                ds = (p * (gp - deltas[h])).astype(BF16)
                newv = newv + dot(p.astype(BF16), dm[h], NN)
                newk = newk + dot(ds, qm[h], NN)
                hrows = pl.ds(64 * h, 64)
                acc[hrows] = acc[hrows] + dot(kt[hrows, krows], ds, NN)
            dk[krows] = newk
            dv[krows] = newv

        dq_ref[rows] = (acc[...] * 0.125).T.astype(BF16)

    @pl.loop(0, total // KB)
    def _(n):
        rows = pl.ds(pl.multiple_of(n * KB, KB), KB)
        dkv_ref[rows, 0:128] = dk[rows, 0:128].astype(BF16)
        dkv_ref[rows, 128:256] = (dk[rows, 128:256] + dv[rows, 0:128]).astype(BF16)
        dkv_ref[rows, 256:384] = dv[rows, 128:256].astype(BF16)

def attend_backward(lens, q, kv, do, ot, lse, cols):
    total = kv.shape[0]
    return pl.pallas_call(
        functools.partial(backward_kernel, cols),
        out_shape=[jax.ShapeDtypeStruct(q.shape, BF16), jax.ShapeDtypeStruct(kv.shape, BF16)],
        in_specs=[pl.BlockSpec(memory_space=pltpu.SMEM)] + [vmem()] * 5,
        out_specs=[vmem()] * 2,
        scratch_shapes=[pltpu.VMEM((3, SPAN, 256), BF16), pltpu.VMEM((3, SPAN, 256), BF16), pltpu.VMEM((256, total), BF16),
                        pltpu.VMEM((total, 256), F32), pltpu.VMEM((total, 256), F32), pltpu.VMEM((256, SPAN), F32)],
        compiler_params=pltpu.CompilerParams(vmem_limit_bytes=40 << 20),
        name="attend_backward",
    )(lens, q, kv, do, ot, lse)


def layer_norm(values, gain_row, shift_row):
    average = jnp.mean(values, axis=-1, keepdims=True)
    centered = values - average
    variance = jnp.mean(centered * centered, axis=-1, keepdims=True)
    return centered * lax.rsqrt(variance + EPSILON) * gain_row + shift_row


def exact_gelu(values):
    return jax.nn.gelu(values, approximate=False)


def by_group(rows, micro, front, back):
    parts = rows.reshape(micro, -1, 4, 192).transpose(2, 0, 1, 3)
    parts = jnp.pad(parts, ((0, 0), (0, 0), (0, 0), (front, back)))
    return parts.reshape((-1,) + parts.shape[2:])


def from_group(blocks, micro, front):
    rows = blocks.shape[1]
    parts = blocks.reshape(4, micro, rows, -1)[..., front:front + 192]
    return parts.transpose(1, 2, 0, 3).reshape(micro * rows, 768)


def shards(tokens, cotangent, doc_lengths, w_qkv, w_out, w_in, w_back, *vectors):
    micro, per, width = tokens.shape
    nf, cols = lax.axis_size("fsdp"), lax.axis_size("ctx") // 8
    share = width // nf
    tiny = jnp.concatenate(vectors).reshape(8, -1)
    full_qkv, full_out, full_in, full_back, tinies = gather_weights((w_qkv, w_out, w_in, w_back), tiny, nf, cols)
    tinies = tinies.reshape(nf, -1).astype(F32)
    named, at = [], 0
    for vector in vectors:
        size = vector.shape[0]
        named.append(tinies[:, at:at + size].reshape(-1))
        at += size
    b_query, b_value, b_out, b_in, b_back, gain_one, shift_one, gain_two, shift_two = named
    inputs = tokens.reshape(micro * per, width)
    joined = jnp.dot(inputs, full_qkv, preferred_element_type=F32)
    bias = jnp.concatenate([b_query, jnp.zeros_like(b_query), b_value])
    joined = (joined + bias).astype(BF16)
    q_sent = by_group(joined[:, :width], micro, 0, 64)
    kv_sent = jnp.concatenate([by_group(joined[:, width:2 * width], micro, 0, 0), by_group(joined[:, 2 * width:], micro, 0, 0)], axis=2)
    q_held, kv_held = spread(q_sent, kv_sent, cols, 2)
    q_held = q_held.reshape(8 * per, 256)
    kv_held = kv_held.reshape(-1, 384)
    mixed, mixed_t, log_total = attend_forward(doc_lengths, q_held, kv_held, cols)
    (back,) = swap([mixed.reshape(8, per, 256)], cols, 3)
    attended = from_group(back, micro, 64)
    first_sum = inputs.astype(F32) + (jnp.dot(attended, full_out, preferred_element_type=F32) + b_out)
    normed = layer_norm(first_sum, gain_one, shift_one)
    normed_low = normed.astype(BF16)
    hidden = jnp.dot(normed_low, full_in, preferred_element_type=F32) + b_in
    activated = exact_gelu(hidden).astype(BF16)
    final_sum = normed + (jnp.dot(activated, full_back, preferred_element_type=F32) + b_back)
    output = layer_norm(final_sum, gain_two, shift_two).astype(BF16)

    upstream = cotangent.reshape(micro * per, width).astype(F32)
    grad_final, g_gain_two, g_shift_two = jax.vjp(layer_norm, final_sum, gain_two, shift_two)[1](upstream)
    grad_second = grad_final.astype(BF16)
    g_back_bias = jnp.sum(grad_second.astype(F32), axis=0)
    grad_activated = jnp.einsum("rm,km->rk", grad_second, full_back, preferred_element_type=F32)
    grad_hidden = jax.vjp(exact_gelu, hidden)[1](grad_activated)[0].astype(BF16)
    g_in_bias = jnp.sum(grad_hidden.astype(F32), axis=0)
    grad_normed = grad_final + jnp.einsum("rf,mf->rm", grad_hidden, full_in, preferred_element_type=F32)
    grad_first, g_gain_one, g_shift_one = jax.vjp(layer_norm, first_sum, gain_one, shift_one)[1](grad_normed)
    grad_branch = grad_first.astype(BF16)
    g_out_bias = jnp.sum(grad_branch.astype(F32), axis=0)
    grad_attended = jnp.einsum("rm,km->rk", grad_branch, full_out, preferred_element_type=F32).astype(BF16)
    (do_held,) = swap([by_group(grad_attended, micro, 64, 0)], cols, 4)
    dq, dkv = attend_backward(doc_lengths, q_held, kv_held, do_held.reshape(8 * per, 256), mixed_t, log_total, cols)
    dq_own, dkv_own = collect(dq.reshape(8, per, 256), dkv.reshape(8 * cols, per, 384), cols, 5)
    grad_joined = jnp.concatenate(
        [from_group(dq_own, micro, 0), from_group(dkv_own, micro, 0), from_group(dkv_own, micro, 192)], axis=1)
    g_query_bias = jnp.sum(grad_joined[:, :width].astype(F32), axis=0)
    g_value_bias = jnp.sum(grad_joined[:, 2 * width:].astype(F32), axis=0)
    input_grad = grad_first + jnp.einsum("rc,mc->rm", grad_joined, full_qkv, preferred_element_type=F32)

    def halves(left, right):
        blocks = right.shape[1] // 384
        return jnp.einsum("rm,rhc->hmc", left, right.reshape(-1, blocks, 384), preferred_element_type=F32).astype(BF16)

    back_grads = jnp.einsum("rk,rm->km", activated, grad_second, preferred_element_type=F32).astype(BF16)
    back_grads = back_grads.reshape(nf, 4, share, 2, 384).transpose(1, 3, 0, 2, 4).reshape(8, width, 384)
    grads = jnp.concatenate(
        [halves(inputs, grad_joined), halves(attended, grad_branch), halves(normed_low, grad_hidden), back_grads])
    grads = grads.reshape(2, 4, 3, nf, cols, share // cols, 384)
    small = (g_query_bias, g_value_bias, g_out_bias, g_in_bias, g_back_bias, g_gain_one, g_shift_one, g_gain_two, g_shift_two)
    small = jnp.concatenate([x.reshape(nf, -1) for x in small], axis=1).reshape(nf, 8, -1)
    owned, small_owned = reduce_grads(grads, small, nf, cols, 6)
    owned = owned.transpose(0, 1, 3, 2, 4, 5).reshape(24, share, 384)

    def columns(first, last):
        return owned[first:last].transpose(1, 0, 2).reshape(share, -1).astype(F32)

    g_back = owned[16:].reshape(4, 2, share, 384).transpose(0, 2, 1, 3).reshape(4 * share, width).astype(F32)
    small_owned = small_owned.reshape(-1)
    small_grads, at = [], 0
    for vector in vectors:
        small_grads.append(small_owned[at:at + vector.shape[0]])
        at += vector.shape[0]
    return (output.reshape(tokens.shape), input_grad.reshape(tokens.shape), columns(0, 6), columns(6, 8), columns(8, 16), g_back) + tuple(small_grads)


def solution(mesh):
    rows, flat = P("fsdp", "ctx", None), P("fsdp", None)
    return jax.shard_map(
        shards,
        mesh=mesh,
        in_specs=(rows, rows, flat) + (flat,) * 4 + (P("fsdp"),) * 9,
        out_specs=(rows, rows) + (flat,) * 4 + (P("fsdp"),) * 9,
        check_vma=False,
    )
```

time: 1000 us -> 579 us (0.58)
  waiting for transfers between devices: 470 us -> 0 us
  Pallas kernels: 0 us -> 339 us
  blocking collectives: 88.2 us -> 0 us
  matrix products: 124 us -> 47.6 us
  local copies, waits for them, and re-layouts: 215 us -> 146 us
  other arithmetic: 75.2 us -> 34.2 us
  between operations: 16.6 us -> 1.78 us
    pallas_call x0 -> x8, Pallas kernels: none -> 339 us  [the longest x1 153 us: reduce_grads(): pl.pallas_call(functools.partial(reduce_kernel, nf, cols, parts), out_sha...]
    reduce_scatter x3 -> x0, waiting for transfers between devices: 146 us -> none  [the longest x1 62.9 us: shards(): lax.psum_scatter(grad_sums[2].astype(jnp.bfloat16), 'fsdp', scatter_dimen...]
    unnamed x16 -> x0, waiting for transfers between devices: 143 us -> none
    all_gather x6 -> x0, waiting for transfers between devices: 124 us -> none  [the longest x1 55.6 us: fetch_weights(): lax.all_gather(w_back, 'fsdp', axis=0, tiled=True)]
    dot_general x96 -> x12, matrix products: 124 us -> 47.6 us  [the longest x1 11.6 us: shards(): hidden = jnp.dot(normed_low, full_in, preferred_element_type=F32) + b_in]
    psum x1 -> x0, waiting for transfers between devices: 56.5 us -> none  [shards(): lax.psum(owned[0].astype(jnp.bfloat16), 'ctx').astype(jnp.float32)]
    psum x1 -> x0, blocking collectives: 50.2 us -> none  [shards(): lax.psum(owned[4].astype(jnp.bfloat16), 'ctx').astype(jnp.float32)]
    unnamed x203 -> x104, local copies, waits for them, and re-layouts: 85.7 us -> 42.7 us
  transfers between devices with their start and end apart: 13 -> 0, of which waited for: 10 -> 0; matrix products, arithmetic and copies ran while one was open for 29% -> 0% of each run, Pallas kernels for 0% -> 0%
where the time goes in v1:
time: 579 us; the launch traced here: 568 us
  Pallas kernels  339 us (59%)
  local copies, waits for them, and re-layouts  146 us (25%)
  matrix products  47.6 us (8%)
  other arithmetic  34.2 us (6%)
    pallas_call x1, Pallas kernels, reduce_grads(): pl.pallas_call(functools.partial(reduce_kernel, nf, cols, parts), out_sha...  153 us
    pallas_call x1, Pallas kernels, gather_weights(): pl.pallas_call(functools.partial(gather_kernel, nf, cols, count), out_sha...  58 us
    reshape x3, local copies, waits for them, and re-layouts, shards(): back_grads.reshape(nf, 4, share, 2, 384).transpose(1, 3, 0, 2, 4)  43.7 us
    unnamed x104, local copies, waits for them, and re-layouts  42.7 us
    pallas_call x1, Pallas kernels, spread(): pl.pallas_call(functools.partial(spread_kernel, cols), out_shape=[jax.Sha...  32.3 us
    pallas_call x1, Pallas kernels, collect(): pl.pallas_call(functools.partial(collect_kernel, cols), out_shape=[jax.Sh...  32 us
    pallas_call x2, Pallas kernels, swap(): pl.pallas_call(functools.partial(swap_kernel, cols, count), out_shape=[ja...  29.5 us
    pallas_call x1, Pallas kernels, attend_backward(): pl.pallas_call(functools.partial(backward_kernel, cols), out_shape=[jax.S...  20.6 us

profile of v1, /device:TPU:9, one launch (start us, length us, event | category | flops | bytes accessed | tf_op | source)
XLA Modules:
  0.0 568.4 jit_solution(13635960091762256669)
XLA Ops:
  0.6 1.1 convert_reduce_fusion.1
  9.6 1.7 copy-done
  11.2 1.7 copy-done.1
  12.9 1.5 copy-done.2
  14.4 1.1 copy-done.7
  15.4 58.0 %gather_weights.1 = (bf16[768,2304]{1,0:T(8,128)(2,1)S(1)}, bf16[768,768]{1,0:T(8,128)(2,1)S(1)}, bf16[768,3072]{1,0:T(8,128)(2,1)S(1)}, bf16[3072,768]{1,0:T(8,128)(2,1)S(1)}, bf16[2,8,576]{2,1,0:T(8,128)(2,1)S(1)}) custom-call(bf16[384,2304]{1,0:T(8,128)(2,1)S(1)} %copy-done.2, bf16[384,768]{1,0:T(8,128)(2,1)S(1)} %copy-done.7, ...), custom_call_target="tpu_custom_call" | custom-call | tf_op jit(solution)/shard_map/gather_weights/pallas_call | solution.py:104
  73.5 1.0 copy-done.3
  74.5 2.2 copy-done.9
  76.6 2.2 copy-done.10
  78.8 1.8 copy-done.11
  80.9 3.3 fusion.1
  86.2 32.3 %spread.1 = (bf16[8,128,256]{2,1,0:T(8,128)(2,1)S(1)}, bf16[16,128,384]{2,1,0:T(8,128)(2,1)S(1)}) custom-call(bf16[8,128,256]{2,1,0:T(8,128)(2,1)S(1)} %bitcast.147, bf16[8,128,384]{2,1,0:T(8,128)(2,1)S(1)} %pad_maximum_fusion.1.kv), custom_call_target="tpu_custom_call" | custom-call | tf_op jit(solution)/shard_map/spread/pallas_call | solution.py:200
  118.5 13.0 %attend_forward.1 = (bf16[1024,256]{1,0:T(8,128)(2,1)S(1)}, f32[4,256,256]{2,1,0:T(8,128)S(1)}, f32[4,8,256]{2,1,0:T(8,128)S(1)}) custom-call(s32[2,4]{1,0:T(2,128)S(1)} %copy-done.8, bf16[1024,256]{1,0:T(8,128)(2,1)S(1)} %bitcast.151, bf16[2048,384]{1,0:T(8,128)(2,1)S(1)} %bitcast.145), custom_call_target="tpu_custom_call" | custom-call | tf_op jit(solution)/shard_map/attend_forward/pallas_call | solution.py:550
  131.5 1.0 copy-done.5
  132.6 14.7 %swap.2 = bf16[8,128,256]{2,1,0:T(8,128)(2,1)S(1)} custom-call(bf16[8,128,256]{2,1,0:T(8,128)(2,1)S(1)} %bitcast.156), custom_call_target="tpu_custom_call" | custom-call | tf_op jit(solution)/shard_map/swap/pallas_call | solution.py:147
  147.2 1.0 slice.121
  148.3 2.0 copy.86
  150.3 1.9 fusion.44
  152.4 11.6 %multiply_convert_fusion = (bf16[256,3072]{1,0:T(8,128)(2,1)S(1)}, f32[256,3072]{1,0:T(8,128)}, f32[256,3072]{1,0:T(8,128)}) fusion(f32[3072]{0:T(1024)S(1)} %add.107, bf16[768,3072]{1,0:T(8,128)(2,1)} %copy-done.9, f32[256,768]{1,0:T(8,128)S(1)} %get-tuple-element.119, f32[768]{0:T(1024)S(1)} %add.104, f32[768]{0:T(1024)S(1)} %mul.155, ...), kind=kOutput, calls=%fused_computation.15 | convolution fusion | flops 1260847104 | bytes 13389824 | tf_op jit(solution)/shard_map/dot_general | solution.py:687
  164.1 1.5 fusion.45
  166.9 2.5 fusion.37
  170.5 6.7 %convert_reduce_fusion = (f32[3072]{0:T(1024)S(1)}, bf16[256,3072]{1,0:T(8,128)(2,1)}) fusion(f32[256,3072]{1,0:T(8,128)S(1)} %copy-done.36, f32[256,3072]{1,0:T(8,128)} %get-tuple-element.120, bf16[256,768]{1,0:T(8,128)(2,1)S(1)} %get-tuple-element.83, bf16[3072,768]{1,0:T(8,128)(2,1)} %copy-done.10), kind=kOutput, calls=%fused_computation.13 | convolution fusion | flops 1220539392 | bytes 12988416 | tf_op jit(solution)/shard_map/rm,km->rk/dot_general | solution.py:696
  177.2 5.7 %multiply_reduce_fusion = (f32[768]{0:T(1024)S(1)}, f32[256]{0:T(256)S(1)}, f32[768]{0:T(1024)S(1)}, f32[256,768]{1,0:T(8,128)}) fusion(f32[256,768]{1,0:T(8,128)} %copy-done.13, f32[256]{0:T(256)S(1)} %fusion.30, f32[256]{0:T(256)S(1)} %broadcast_multiply_fusion.1, f32[768]{0:T(1024)S(1)} %mul.155, bf16[256,3072]{1,0:T(8,128)(2,1)} %get-tuple-element.85, ...), kind=kOutput, calls=%fused_computation.59 | convolution fusion | flops 1209923840 | bytes 8664064 | tf_op jit(solution)/shard_map/rf,mf->rm/dot_general | solution.py:699
  182.9 2.5 fusion.36
  185.5 1.3 convert_reduce_fusion.3
  186.7 1.3 convolution_convert_fusion.2
  188.0 2.0 copy.64
  190.0 1.8 reshape.283
  191.9 1.9 copy.90
  193.8 1.3 pad.9.clone
  195.1 14.8 %swap.3 = bf16[8,128,256]{2,1,0:T(8,128)(2,1)S(1)} custom-call(bf16[8,128,256]{2,1,0:T(8,128)(2,1)S(1)} %bitcast.148), custom_call_target="tpu_custom_call" | custom-call | tf_op jit(solution)/shard_map/swap/pallas_call | solution.py:147
  209.9 20.6 %attend_backward.1 = (bf16[1024,256]{1,0:T(8,128)(2,1)S(1)}, bf16[2048,384]{1,0:T(8,128)(2,1)S(1)}) custom-call(s32[2,4]{1,0:T(2,128)S(1)} %copy-done.8, bf16[1024,256]{1,0:T(8,128)(2,1)S(1)} %bitcast.152, bf16[2048,384]{1,0:T(8,128)(2,1)S(1)} %bitcast.146, bf16[1024,256]{1,0:T(8,128)(2,1)S(1)} %bitcast.150, f32[4,256,256]{2,1,0:T(8,128)S(1)} %copy-done.6, ...), custom_call_target="tpu_custom_call" | custom-call | tf_op jit(solution)/shard_map/attend_backward/pallas_call | solution.py:624
  230.5 32.0 %collect.1 = (bf16[8,128,256]{2,1,0:T(8,128)(2,1)S(1)}, bf16[8,128,384]{2,1,0:T(8,128)(2,1)S(1)}) custom-call(bf16[8,128,256]{2,1,0:T(8,128)(2,1)S(1)} %bitcast.157, bf16[16,128,384]{2,1,0:T(8,128)(2,1)S(1)} %bitcast.153), custom_call_target="tpu_custom_call" | custom-call | tf_op jit(solution)/shard_map/collect/pallas_call | solution.py:252
  262.9 1.5 convert_reduce_fusion.5
  265.9 1.5 convert_reduce_fusion.4
  268.2 1.0 concatenate.33
  269.2 1.1 concatenate.32
  270.3 2.2 concatenate.31
  272.5 1.8 copy.109
  274.3 1.9 copy.83
  276.2 2.7 fusion.8
  278.9 1.2 copy_bitcast_fusion
  280.2 2.7 convolution_add_fusion.3
  282.9 1.8 copy.85
  284.7 3.7 convert_bitcast_fusion.2
  288.4 2.9 convert_bitcast_fusion.4
  291.3 3.6 convolution_convert_fusion
  295.0 10.1 %reshape.296 = bf16[2,4,384,2,384]{4,3,2,1,0:T(2,128)(2,1)} reshape(bf16[3072,768]{1,0:T(8,128)(2,1)} %convolution_convert_fusion) | data formatting | bytes 9437184 | tf_op jit(solution)/shard_map/reshape | solution.py:718
  305.0 22.1 %copy.72 = bf16[2,4,384,2,384]{2,0,4,3,1:T(2,128)(2,1)} copy(bf16[2,4,384,2,384]{4,3,2,1,0:T(2,128)(2,1)} %reshape.296) | data formatting | bytes 9437184 | tf_op jit(solution)/shard_map/reshape | solution.py:718
  327.2 11.5 %reshape.297 = bf16[8,768,384]{1,2,0:T(8,128)(2,1)} reshape(bf16[4,2,2,384,384]{3,2,4,1,0:T(2,128)(2,1)} %bitcast.164) | data formatting | bytes 9437184 | tf_op jit(solution)/shard_map/reshape | solution.py:718
  338.6 12.4 %pad_maximum_fusion = bf16[24,768,384]{1,2,0:T(8,128)(2,1)} fusion(bf16[8,768,384]{1,2,0:T(8,128)(2,1)} %reshape.297, bf16[8,768,384]{1,2,0:T(8,128)(2,1)} %convert_bitcast_fusion.2, bf16[2,768,384]{1,2,0:T(8,128)(2,1)S(1)} %copy-done.18, bf16[6,768,384]{1,2,0:T(8,128)(2,1)} %convert_bitcast_fusion.4), kind=kLoop, calls=%fused_computation | loop fusion | flops 21233664 | bytes 28311552 | tf_op jit(solution)/shard_map/concatenate | solution.py:719
  351.1 18.9 %copy.73 = bf16[24,768,384]{2,1,0:T(8,128)(2,1)} copy(bf16[24,768,384]{1,2,0:T(8,128)(2,1)} %pad_maximum_fusion) | data formatting | bytes 28311552 | tf_op jit(solution)/shard_map/concatenate | solution.py:719
  370.0 153.4 %reduce_grads.1 = (bf16[2,4,2,3,192,384]{5,4,3,2,1,0:T(8,128)(2,1)}, f32[8,576]{1,0:T(8,128)}) custom-call(bf16[2,4,3,2,2,192,384]{6,5,4,3,2,1,0:T(8,128)(2,1)} %bitcast.160, f32[2,8,576]{2,1,0:T(8,128)} %reshape.308.small), custom_call_target="tpu_custom_call" | custom-call | tf_op jit(solution)/shard_map/reduce_grads/pallas_call | solution.py:440
  523.4 6.9 %copy.74 = bf16[2,4,3,2,192,384]{5,4,3,2,1,0:T(8,128)(2,1)} copy(bf16[2,4,3,2,192,384]{5,4,2,3,1,0:T(8,128)(2,1)} %bitcast.169) | data formatting | bytes 14155776 | tf_op jit(solution)/shard_map/transpose | solution.py:725
  531.6 1.1 convert_bitcast_fusion.5
  533.1 1.4 copy.80
  534.5 3.5 convert_bitcast_fusion.3
  538.0 3.3 copy.75
  541.3 2.9 copy.79
  544.3 5.2 fusion.39
  549.7 3.6 copy.78
  553.4 2.5 copy.95
  555.9 6.0 %copy.77 = f32[384,8,384]{0,2,1:T(8,128)} copy(f32[384,8,384]{2,0,1:T(8,128)} %get-tuple-element.95) | data formatting | bytes 9437184 | tf_op jit(solution)/shard_map/convert_element_type | solution.py:728
  561.9 6.0 %copy.81 = f32[384,3072]{1,0:T(8,128)} copy(f32[384,3072]{0,1:T(8,128)} %bitcast.166) | data formatting | bytes 9437184
  (144 shorter events, 17.3 us)
Async XLA Ops:
  9.6 1.7 copy-start
  11.2 1.7 copy-start.1
  12.9 1.5 copy-start.2
  14.4 1.1 copy-start.7
  15.4 65.5 %copy-start.34 = (bf16[2,128,768]{2,1,0:T(8,128)(2,1)S(1)}, bf16[2,128,768]{2,1,0:T(8,128)(2,1)}, u32[]{:S(2)}) copy-start(bf16[2,128,768]{2,1,0:T(8,128)(2,1)} %param.16) | copy-start | bytes 1179652
  73.4 1.0 copy-start.3
  74.5 2.2 copy-start.9
  76.6 2.2 copy-start.10
  78.8 1.8 copy-start.11
  85.3 33.3 %copy-start.8 = (s32[2,4]{1,0:T(2,128)S(1)}, s32[2,4]{1,0:T(2,128)}, u32[]{:S(2)}) copy-start(s32[2,4]{1,0:T(2,128)} %lens.3) | copy-start | bytes 100
  118.5 31.8 %copy-start.4 = (bf16[768,768]{1,0:T(8,128)(2,1)S(1)}, bf16[768,768]{1,0:T(8,128)(2,1)}, u32[]{:S(2)}) copy-start(bf16[768,768]{1,0:T(8,128)(2,1)} %copy-done.3) | copy-start | bytes 3538948
  131.5 1.1 copy-start.5
  150.3 13.8 %slice-start = ((s8[4718592]{0:T(1024)(128)(4,1)}), s8[4194304]{0:T(1024)(128)(4,1)S(1)}, s32[]{:S(2)}) async-start(s8[4718592]{0:T(1024)(128)(4,1)} %bitcast.158), calls=%async_computation | async-start | bytes 8388608
  152.1 11.9 %copy-start.13 = (f32[256,768]{1,0:T(8,128)}, f32[256,768]{1,0:T(8,128)S(1)}, u32[]{:S(2)}) copy-start(f32[256,768]{1,0:T(8,128)S(1)} %get-tuple-element.119) | copy-start | bytes 2359300
  152.4 11.7 %slice-start.1 = ((s8[4718592]{0:T(1024)(128)(4,1)}), s8[524288]{0:T(1024)(128)(4,1)S(1)}, s32[]{:S(2)}) async-start(s8[4718592]{0:T(1024)(128)(4,1)} %bitcast.158), calls=%async_computation.1 | async-start | bytes 1048576
  164.0 1.6 copy-start.22
  164.1 2.4 copy-start.19
  165.6 0.9 copy-start.15
  166.9 3.6 copy-start.36
  169.4 0.9 copy-start.25
  170.4 6.8 %copy-start.26 = (bf16[256,768]{1,0:T(8,128)(2,1)}, bf16[256,768]{1,0:T(8,128)(2,1)S(1)}, u32[]{:S(2)}) copy-start(bf16[256,768]{1,0:T(8,128)(2,1)S(1)} %get-tuple-element.83) | copy-start | bytes 1179652
  185.5 9.6 %copy-start.33 = (f32[256]{0:T(256)}, f32[256]{0:T(256)S(1)}, u32[]{:S(2)}) copy-start(f32[256]{0:T(256)S(1)} %negate_multiply_fusion.1) | copy-start | bytes 3076
  186.7 1.3 copy-start.21
  188.0 21.9 %copy-start.6 = (f32[4,256,256]{2,1,0:T(8,128)S(1)}, f32[4,256,256]{2,1,0:T(8,128)}, u32[]{:S(2)}) copy-start(f32[4,256,256]{2,1,0:T(8,128)} %copy-done.5) | copy-start | bytes 3145732
  262.9 6.3 %copy-start.16 = (bf16[4,2,128,192]{2,1,3,0:T(2,128)(2,1)}, bf16[4,2,128,192]{2,1,3,0:T(2,128)(2,1)S(1)}, u32[]{:S(2)}) copy-start(bf16[4,2,128,192]{2,1,3,0:T(2,128)(2,1)S(1)} %copy.87) | copy-start | bytes 1179652
  265.2 4.1 copy-start.20
  265.8 3.4 copy-start.17
  270.3 9.9 %copy-start.12 = (bf16[768,2304]{1,0:T(8,128)(2,1)S(1)}, bf16[768,2304]{1,0:T(8,128)(2,1)}, u32[]{:S(2)}) copy-start(bf16[768,2304]{1,0:T(8,128)(2,1)} %copy-done.11) | copy-start | bytes 10616836
  276.2 4.0 copy-start.24
  276.2 4.0 copy-start.31
  282.9 1.8 copy-start.14
  284.7 3.7 copy-start.28
  284.7 3.7 copy-start.29
  284.7 3.7 copy-start.30
  284.7 3.7 copy-start.35
  288.4 2.9 copy-start.23
  288.4 2.9 copy-start.27
  327.2 11.5 %copy-start.18 = (bf16[2,768,384]{1,2,0:T(8,128)(2,1)S(1)}, bf16[2,768,384]{1,2,0:T(8,128)(2,1)}, u32[]{:S(2)}) copy-start(bf16[2,768,384]{1,2,0:T(8,128)(2,1)} %fusion.8) | copy-start | bytes 3538948
  523.4 6.9 %copy-start.32 = (f32[8,576]{1,0:T(8,128)S(1)}, f32[8,576]{1,0:T(8,128)}, u32[]{:S(2)}) copy-start(f32[8,576]{1,0:T(8,128)} %get-tuple-element.46) | copy-start | bytes 55300

commit v2 on v1

--- a/solution.py
+++ b/solution.py
@@ -633,6 +633,460 @@
     )(lens, q, kv, do, ot, lse)
 
 
+class Wires:
+    def __init__(self, send, recv):
+        self.send, self.recv, self.made = send, recv, []
+
+    def go(self, source, target, peer):
+        n = len(self.made)
+        cp = remote(source, target, self.send.at[n], self.recv.at[n], peer)
+        cp.start()
+        self.made.append(cp)
+        return cp
+
+
+def transpose_into(target, source, base):
+    width = source.shape[1]
+
+    @pl.loop(0, width // 128)
+    def _(n):
+        at = pl.multiple_of(n * 128, 128)
+        target[pl.ds(base + at, 128)] = source[:, pl.ds(at, 128)].astype(F32).T.astype(BF16)
+
+
+def pair_columns(even, odd, lane, second):
+    if second:
+        return jnp.where(lane < 192, pltpu.roll(even, 192, 1), odd)
+    return jnp.where(lane < 192, even, pltpu.roll(odd, 192, 1))
+
+
+BLK = 48
+Z1, X1, Y1, Z2, Y2, X2 = (0, 1152), (1152, 1920), (1920, 3456), (3456, 3840), (3840, 4224), (4224, 4608)
+
+
+def gradient_kernel(tok, att, low, act, gbr, ghid, gsec, gfirst, wqkv, small, dq, dkv,
+                    out, igrad, small_out,
+                    xt, joined, mine, sib, cin, dqo, dkvo, rbuf, total,
+                    y8, y4, x8, x4, z4, z1r, zyb, zxb, v_own, v_core, v_f, v_b, v_a, send, recv, here):
+    a, b, c, f = place(2)
+    me, peers = octet(a, b, c, f, 2)
+    xp, yp, sp = device(a, 1 - b, c, f, 2), device(a, b, c, 1 - f, 2), device(a, b, 1 - c, f, 2)
+    up, down = lax.rem(a + 1, 4), lax.rem(a + 3, 4)
+    upp, downp = device(up, b, c, f, 2), device(down, b, c, f, 2)
+    meet([p for _, p in peers] + [xp, yp])
+    wires = Wires(send, recv)
+    go = wires.go
+
+    order = [other for other, _ in peers] + [me]
+
+    def slot(block, bb):
+        return (block // 2 * 2 + bb) * 2 + lax.rem(block, 2)
+
+    crossed = [go(dkv.at[slot(block, 1 - b)], rbuf.at[n], xp) for n, block in enumerate(order)]
+    swapped = [go(dq.at[other], dqo.at[me], peer) for other, peer in peers]
+    own_q = pltpu.make_async_copy(dq.at[me], dqo.at[me], here.at[0])
+    own_q.start()
+
+    transpose_into(xt, att, 0)
+    transpose_into(xt, low, 768)
+    transpose_into(xt, act, 1536)
+    transpose_into(xt, tok, 4608)
+
+    def produce(kind, first, count, part, finish):
+        @pl.loop(0, 2 * count)
+        def _(n):
+            ff, j = lax.rem(n, 2), first + n // 2
+            if kind == "out":
+                left, right = xt[pl.ds(pl.multiple_of(ff * 384, 128), 384)], gbr[:, pl.ds(pl.multiple_of(part * 384, 128), 384)]
+                col = 0
+            elif kind == "in":
+                left = xt[pl.ds(pl.multiple_of(768 + ff * 384, 128), 384)]
+                right = ghid[:, pl.ds(pl.multiple_of(part * 1536 + j * 384, 128), 384)]
+                col = pl.multiple_of(384 + j * 384, 128)
+            elif kind == "back":
+                left = xt[pl.ds(pl.multiple_of(1536 + ff * 1536 + j * 384, 128), 384)]
+                right = gsec[:, pl.ds(pl.multiple_of(part * 384, 128), 384)]
+                col = pl.multiple_of(1920 + j * 384, 128)
+            else:
+                left = xt[pl.ds(pl.multiple_of(4608 + ff * 384, 128), 384)]
+                right = joined[:, pl.ds(pl.multiple_of(part * 1152 + j * 384, 128), 384)]
+                col = pl.multiple_of(3456 + j * 384, 128)
+            finish(pl.ds(ff * 2, 2), pl.ds(col, 384), dot(left, right, NN).reshape(2, 4, BLK, 384))
+
+    def keep(rows, cols, value):
+        sib[rows, :, :, cols] = value.astype(BF16)
+
+    def join(rows, cols, value):
+        mine[rows, :, :, cols] = (value + cin[rows, :, :, cols].astype(F32)).astype(BF16)
+
+    core = {}
+
+    def share(span):
+        cols = slice(span[0], span[1])
+        core[span] = go(sib.at[:, :, :, cols], cin.at[:, :, :, cols], sp)
+
+    def inside(span, group):
+        base = 0
+        for member in group:
+            if member == span:
+                return slice(base, base + span[1] - span[0])
+            base += member[1] - member[0]
+
+    YS, XS, ZS, RS = (Y1, Y2), (X1, X2), (Z1, Z2), (Y1, X1, Y2, X2)
+
+    def add(target, source):
+        def step(n):
+            t, s = target(n), source(n)
+            t[...] = (t[...].astype(F32) + s[...].astype(F32)).astype(BF16)
+        return step
+
+    def accumulate(target, source, count):
+        pl.loop(0, count)(add(target, source))
+
+    def start_y(span):
+        cols, own = slice(span[0], span[1]), inside(span, YS)
+        return go(mine.at[pl.ds((1 - f) * 2, 2), :, :, cols], y8.at[:, :, :, own], yp)
+
+    def start_x(span):
+        cols, own = slice(span[0], span[1]), inside(span, XS)
+        return [go(mine.at[ff * 2 + 1 - b, :, :, cols], x8.at[ff, :, :, own], xp) for ff in range(2)]
+
+    def next_y(span, cp):
+        cols, own = slice(span[0], span[1]), inside(span, YS)
+        cp.wait_recv()
+        accumulate(lambda n: mine.at[f * 2 + n // 4, lax.rem(n, 4), :, cols], lambda n: y8.at[n // 4, lax.rem(n, 4), :, own], 8)
+        return go(mine.at[f * 2 + 1 - b, :, :, cols], x4.at[:, :, own], xp)
+
+    def next_x(span, cps):
+        cols, own = slice(span[0], span[1]), inside(span, XS)
+        for cp in cps:
+            cp.wait_recv()
+        accumulate(lambda n: mine.at[n // 4 * 2 + b, lax.rem(n, 4), :, cols], lambda n: x8.at[n // 4, lax.rem(n, 4), :, own], 8)
+        return go(mine.at[(1 - f) * 2 + b, :, :, cols], y4.at[:, :, own], yp)
+
+    def last_y(span, cp):
+        cols, own = slice(span[0], span[1]), inside(span, YS)
+        cp.wait_recv()
+        accumulate(lambda n: mine.at[f * 2 + b, n, :, cols], lambda n: x4.at[n, :, own], 4)
+
+    def last_x(span, cp):
+        cols, own = slice(span[0], span[1]), inside(span, XS)
+        cp.wait_recv()
+        accumulate(lambda n: mine.at[f * 2 + b, n, :, cols], lambda n: y4.at[n, :, own], 4)
+
+    def halves(span):
+        tiles = (span[1] - span[0]) // 128
+        mid = span[0] + tiles // 2 * 128
+        return (span[0], mid), (mid, span[1])
+
+    def landing(span, step, part, small_ring):
+        base = inside(span, RS if small_ring else ZS).start - span[0]
+        cols = slice(base + part[0], base + part[1])
+        return z1r.at[step, :, cols] if small_ring else z4.at[step, :, :, cols]
+
+    def ring_source(aa, part, small_ring):
+        cols = slice(part[0], part[1])
+        return mine.at[f * 2 + b, aa, :, cols] if small_ring else mine.at[:, aa, :, cols]
+
+    def ring_send(span, step, small_ring):
+        lo, hi = halves(span)
+        ud, dd = lax.rem(a + 3 - step, 4), lax.rem(a + 1 + step, 4)
+        return (go(ring_source(ud, lo, small_ring), landing(span, step, lo, small_ring), upp),
+                go(ring_source(dd, hi, small_ring), landing(span, step, hi, small_ring), downp))
+
+    def ring_add(span, step, small_ring, cps):
+        lo, hi = halves(span)
+        ud, dd = lax.rem(a + 6 - step, 4), lax.rem(a + 2 + step, 4)
+        for cp, part, aa in zip(cps, (lo, hi), (ud, dd)):
+            cp.wait_recv()
+            got = landing(span, step, part, small_ring)
+            if small_ring:
+                add(lambda n: ring_source(aa, part, True), lambda n: got)(0)
+            else:
+                cols = slice(part[0], part[1])
+                accumulate(lambda n: mine.at[n, aa, :, cols], lambda n: got.at[n], 4)
+
+    def tail_z_y(span):
+        cols, own = slice(span[0], span[1]), inside(span, ZS)
+        return go(mine.at[pl.ds((1 - f) * 2, 2), a, :, cols], zyb.at[:, :, own], yp)
+
+    def tail_z_x(span, cp):
+        cols, own = slice(span[0], span[1]), inside(span, ZS)
+        cp.wait_recv()
+        accumulate(lambda n: mine.at[f * 2 + n, a, :, cols], lambda n: zyb.at[n, :, own], 2)
+        return go(mine.at[f * 2 + 1 - b, a, :, cols], zxb.at[:, own], xp)
+
+    def tail_z_end(span, cp):
+        cols, own = slice(span[0], span[1]), inside(span, ZS)
+        cp.wait_recv()
+        add(lambda n: mine.at[f * 2 + b, a, :, cols], lambda n: zxb.at[:, own])(0)
+
+    produce("out", 0, 1, 1 - c, keep)
+    produce("in", 0, 2, 1 - c, keep)
+    share(Z1)
+    produce("back", 0, 4, 1 - c, keep)
+    share(Y1)
+    produce("in", 2, 2, 1 - c, keep)
+    share(X1)
+    core[Z1].wait_recv()
+    produce("out", 0, 1, c, join)
+    produce("in", 0, 2, c, join)
+    z1 = ring_send(Z1, 0, False)
+    core[Y1].wait_recv()
+    produce("back", 0, 4, c, join)
+    y1 = start_y(Y1)
+    core[X1].wait_recv()
+    produce("in", 2, 2, c, join)
+
+    for n, block in enumerate(order):
+        crossed[n].wait_recv()
+        value = (dkv[slot(block, b)].astype(F32) + rbuf[n].astype(F32)).astype(BF16)
+        if n < 7:
+            total[n] = value
+            swapped.append(go(total.at[n], dkvo.at[me], peers[n][1]))
+        else:
+            dkvo[me] = value
+    x1 = start_x(X1)
+
+    ring_add(Z1, 0, False, z1)
+    z1 = ring_send(Z1, 1, False)
+    y1 = next_y(Y1, y1)
+    ring_add(Z1, 1, False, z1)
+    z1 = ring_send(Z1, 2, False)
+    x1 = next_x(X1, x1)
+
+    own_q.wait()
+    for cp in swapped:
+        cp.wait_recv()
+    lane = lax.broadcasted_iota(jnp.int32, (128, 384), 1)
+    for s in range(2):
+        rows = slice(s * 128, s * 128 + 128)
+        for p in range(2):
+            even, odd = 4 * p + s, 4 * p + 2 + s
+            blank = jnp.zeros((128, 128), F32)
+            qe = jnp.concatenate([dqo[even].astype(F32), blank], axis=1)
+            qo = jnp.concatenate([dqo[odd].astype(F32), blank], axis=1)
+            joined[rows, 384 * p:384 * p + 384] = pair_columns(qe, qo, lane, False).astype(BF16)
+            ke, ko = dkvo[even].astype(F32), dkvo[odd].astype(F32)
+            joined[rows, 768 + 384 * p:1152 + 384 * p] = pair_columns(ke, ko, lane, False).astype(BF16)
+            joined[rows, 1536 + 384 * p:1920 + 384 * p] = pair_columns(ke, ko, lane, True).astype(BF16)
+    produce("qkv", 0, 3, 1 - c, keep)
+    for span in (Z2, Y2, X2):
+        share(span)
+    v_own[...] = small[...]
+    v_own[0:1] = jnp.sum(joined[:, 0:768].astype(F32), axis=0, keepdims=True)
+    v_own[1:2] = jnp.sum(joined[:, 1536:2304].astype(F32), axis=0, keepdims=True)
+    vec = go(v_own, v_core, sp)
+    for span in (Z2, Y2, X2):
+        core[span].wait_recv()
+    produce("qkv", 0, 3, c, join)
+    z2 = ring_send(Z2, 0, False)
+    y2 = start_y(Y2)
+    x2 = start_x(X2)
+
+    ring_add(Z1, 2, False, z1)
+    z1 = tail_z_y(Z1)
+    last_y(Y1, y1)
+    y1 = ring_send(Y1, 0, True)
+    last_x(X1, x1)
+    x1 = ring_send(X1, 0, True)
+
+    @pl.loop(0, 3)
+    def _(n):
+        rows = pl.ds(pl.multiple_of(n * 256, 256), 256)
+        igrad[:, rows] = gfirst[:, rows] + dot(joined[...], wqkv[rows], NT)
+
+    vec.wait_recv()
+    v_own2 = v_own[...] + v_core[...]
+    v_core[...] = v_own2
+    vec = go(v_core.at[:, pl.ds(pl.multiple_of((1 - f) * 384, 128), 384)], v_f, yp)
+
+    z1 = tail_z_x(Z1, z1)
+    ring_add(Y1, 0, True, y1)
+    y1 = ring_send(Y1, 1, True)
+    ring_add(X1, 0, True, x1)
+    x1 = ring_send(X1, 1, True)
+    ring_add(Z2, 0, False, z2)
+    z2 = ring_send(Z2, 1, False)
+    y2 = next_y(Y2, y2)
+    x2 = next_x(X2, x2)
+    vec.wait_recv()
+    v_b[b] = v_core[:, pl.ds(pl.multiple_of(f * 384, 128), 384)] + v_f[...]
+    vec = go(v_b.at[b], v_b.at[b], xp)
+    ring_add(Y1, 1, True, y1)
+    y1 = ring_send(Y1, 2, True)
+    ring_add(X1, 1, True, x1)
+    x1 = ring_send(X1, 2, True)
+    ring_add(Z2, 1, False, z2)
+    z2 = ring_send(Z2, 2, False)
+    tail_z_end(Z1, z1)
+    vec.wait_recv()
+    v_a[a] = v_b[0] + v_b[1]
+    vec = [go(v_a.at[a], v_a.at[a], device(lax.rem(a + k, 4), b, c, f, 2)) for k in range(1, 4)]
+
+    pending = []
+
+    def piece(cc, bb, aa, span):
+        return out.at[cc, bb * 4 + aa, :, span[0]:span[1]]
+
+    class Gather:
+        def __init__(self, span, first):
+            self.span, self.first = span, first
+            out[c, b * 4 + a, :, span[0]:span[1]] = mine[f * 2 + b, a, :, span[0]:span[1]]
+            self.spread(b, a, span)
+            self.ring = self.around(b)
+            self.cross = go(piece(c, b, a, span), piece(c, b, a, span), xp)
+
+        def spread(self, bb, aa, span):
+            pending.append(go(piece(c, bb, aa, span), piece(c, bb, aa, span), sp))
+
+        def around(self, bb):
+            p = piece(c, bb, a, self.span)
+            return go(p, p, upp), go(p, p, downp)
+
+        def passed(self, bb, ring):
+            lo, hi = halves(self.span)
+            ring[0].wait_recv()
+            p = piece(c, bb, down, lo)
+            first = go(p, p, upp)
+            ring[1].wait_recv()
+            p = piece(c, bb, up, hi)
+            second = go(p, p, downp)
+            for aa in (down, up):
+                self.spread(bb, aa, self.span)
+            return first, second
+
+        def arrived(self, bb, ring):
+            for cp in ring:
+                cp.wait_recv()
+            self.spread(bb, lax.rem(a + 2, 4), self.span)
+
+        def second(self):
+            self.ring2 = self.passed(b, self.ring)
+            if self.first == "b":
+                self.cross.wait_recv()
+                self.spread(1 - b, a, self.span)
+                self.other = self.around(1 - b)
+            else:
+                self.more = [go(piece(c, b, aa, self.span), piece(c, b, aa, self.span), xp) for aa in (down, up)]
+
+        def third(self):
+            self.arrived(b, self.ring2)
+            if self.first == "b":
+                self.other2 = self.passed(1 - b, self.other)
+            else:
+                p = piece(c, b, lax.rem(a + 2, 4), self.span)
+                self.more.append(go(p, p, xp))
+                self.cross.wait_recv()
+                self.spread(1 - b, a, self.span)
+
+        def fourth(self):
+            if self.first == "b":
+                self.arrived(1 - b, self.other2)
+            else:
+                for cp, aa in zip(self.more, (down, up, lax.rem(a + 2, 4))):
+                    cp.wait_recv()
+                    self.spread(1 - b, aa, self.span)
+
+    g_z1 = Gather(Z1, "a")
+    ring_add(Y1, 2, True, y1)
+    g_y1 = Gather(Y1, "b")
+    ring_add(X1, 2, True, x1)
+    g_x1 = Gather(X1, "b")
+    ring_add(Z2, 2, False, z2)
+    z2 = tail_z_y(Z2)
+    last_y(Y2, y2)
+    y2 = ring_send(Y2, 0, True)
+    last_x(X2, x2)
+    x2 = ring_send(X2, 0, True)
+    g_z1.second()
+    z2 = tail_z_x(Z2, z2)
+    ring_add(Y2, 0, True, y2)
+    y2 = ring_send(Y2, 1, True)
+    ring_add(X2, 0, True, x2)
+    x2 = ring_send(X2, 1, True)
+    g_y1.second()
+    g_x1.second()
+    tail_z_end(Z2, z2)
+    g_z2 = Gather(Z2, "a")
+    ring_add(Y2, 1, True, y2)
+    y2 = ring_send(Y2, 2, True)
+    ring_add(X2, 1, True, x2)
+    x2 = ring_send(X2, 2, True)
+    g_z1.third()
+    ring_add(Y2, 2, True, y2)
+    g_y2 = Gather(Y2, "b")
+    ring_add(X2, 2, True, x2)
+    g_x2 = Gather(X2, "b")
+    g_y1.third()
+    g_x1.third()
+    g_z1.fourth()
+    g_z2.second()
+    g_y2.second()
+    g_x2.second()
+    g_y1.fourth()
+    g_x1.fourth()
+    g_z2.third()
+    g_y2.third()
+    g_x2.third()
+    g_z2.fourth()
+    g_y2.fourth()
+    g_x2.fourth()
+    for cp in vec + pending:
+        cp.wait_recv()
+    small_out[...] = v_a[0] + v_a[1] + v_a[2] + v_a[3]
+    for cp in wires.made:
+        cp.wait_send()
+
+
+def reduce_all(tok, att, low, act, gbr, ghid, gsec, gfirst, wqkv, small, dq, dkv, ident):
+    block = (BLK,)
+    wires = 192
+    return pl.pallas_call(
+        gradient_kernel,
+        out_shape=[jax.ShapeDtypeStruct((2, 8, BLK, 4608), BF16), jax.ShapeDtypeStruct(gfirst.shape, F32), jax.ShapeDtypeStruct((16, 384), F32)],
+        in_specs=[vmem()] * 12, out_specs=[vmem()] * 3,
+        scratch_shapes=[
+            pltpu.VMEM((5376, 256), BF16), pltpu.VMEM((256, 2304), BF16),
+            pltpu.VMEM((4, 4, BLK, 4608), BF16), pltpu.VMEM((4, 4, BLK, 4608), BF16), pltpu.VMEM((4, 4, BLK, 4608), BF16),
+            pltpu.VMEM(dq.shape, BF16), pltpu.VMEM((8,) + dkv.shape[1:], BF16),
+            pltpu.VMEM((8,) + dkv.shape[1:], BF16), pltpu.VMEM((7,) + dkv.shape[1:], BF16),
+            pltpu.VMEM((2, 4, BLK, 1920), BF16), pltpu.VMEM((4, BLK, 1152), BF16),
+            pltpu.VMEM((2, 4, BLK, 1152), BF16), pltpu.VMEM((4, BLK, 1920), BF16),
+            pltpu.VMEM((3, 4, BLK, 1536), BF16), pltpu.VMEM((3, BLK, 3072), BF16),
+            pltpu.VMEM((2, BLK, 1536), BF16), pltpu.VMEM((BLK, 1536), BF16),
+            pltpu.VMEM((16, 768), F32), pltpu.VMEM((16, 768), F32), pltpu.VMEM((16, 384), F32),
+            pltpu.VMEM((2, 16, 384), F32), pltpu.VMEM((4, 16, 384), F32),
+            DMA((wires,)), DMA((wires,)), DMA((1,))],
+        compiler_params=pltpu.CompilerParams(collective_id=ident, has_side_effects=True, vmem_limit_bytes=62 << 20),
+        name="reduce_all",
+    )(tok, att, low, act, gbr, ghid, gsec, gfirst, wqkv, small, dq, dkv)
+
+
+def widen_kernel(grads, g_qkv, g_out, g_in, g_back):
+    for core in range(2):
+        part = grads.at[core]
+        g_out[:, core * 384:core * 384 + 384] = part[:, 0:384].astype(F32)
+        g_in[:, core * 1536:core * 1536 + 1536] = part[:, 384:1920].astype(F32)
+        for j in range(4):
+            g_back[j, :, core * 384:core * 384 + 384] = part[:, 1920 + 384 * j:2304 + 384 * j].astype(F32)
+        g_qkv[:, core * 1152:core * 1152 + 1152] = part[:, 3456:4608].astype(F32)
+
+
+def widen(grads):
+    rows, step = 384, 48
+    spec = lambda wide: pl.BlockSpec((step, wide), lambda n: (n, 0))
+    return pl.pallas_call(
+        widen_kernel,
+        grid=(rows // step,),
+        out_shape=[jax.ShapeDtypeStruct((rows, 2304), F32), jax.ShapeDtypeStruct((rows, 768), F32),
+                   jax.ShapeDtypeStruct((rows, 3072), F32), jax.ShapeDtypeStruct((4, rows, 768), F32)],
+        in_specs=[pl.BlockSpec((2, step, 4608), lambda n: (0, n, 0))],
+        out_specs=[spec(2304), spec(768), spec(3072), pl.BlockSpec((4, step, 768), lambda n: (0, n, 0))],
+        name="widen",
+    )(grads)
+
+
 def layer_norm(values, gain_row, shift_row):
     average = jnp.mean(values, axis=-1, keepdims=True)
     centered = values - average
@@ -702,7 +1156,17 @@
     g_out_bias = jnp.sum(grad_branch.astype(F32), axis=0)
     grad_attended = jnp.einsum("rm,km->rk", grad_branch, full_out, preferred_element_type=F32).astype(BF16)
     (do_held,) = swap([by_group(grad_attended, micro, 64, 0)], cols, 4)
+    if nf == 2 and cols == 2:
+        small = [jnp.zeros((2, width), F32)] + [x[None] for x in (g_out_bias, g_back_bias, g_gain_one, g_shift_one, g_gain_two, g_shift_two)]
+        small += [g_in_bias.reshape(2, 4, share).transpose(1, 0, 2).reshape(4, width), jnp.zeros((4, width), F32)]
     dq, dkv = attend_backward(doc_lengths, q_held, kv_held, do_held.reshape(8 * per, 256), mixed_t, log_total, cols)
+    if nf == 2 and cols == 2:
+        grads, input_grad, sums = reduce_all(
+            inputs, attended, normed_low, activated, grad_branch, grad_hidden, grad_second, grad_first, full_qkv,
+            jnp.concatenate(small), dq.reshape(8, per, 256), dkv.reshape(8 * cols, per, 384), 5)
+        g_qkv, g_out, g_in, g_back = widen(grads.reshape(2, share, 4608))
+        rows = [sums[0], sums[1], sums[2], sums[8:12].reshape(-1), sums[3], sums[4], sums[5], sums[6], sums[7]]
+        return (output.reshape(tokens.shape), input_grad.reshape(tokens.shape), g_qkv, g_out, g_in, g_back.reshape(4 * share, width)) + tuple(rows)
     dq_own, dkv_own = collect(dq.reshape(8, per, 256), dkv.reshape(8 * cols, per, 384), cols, 5)
     grad_joined = jnp.concatenate(
         [from_group(dq_own, micro, 0), from_group(dkv_own, micro, 0), from_group(dkv_own, micro, 192)], axis=1)

time: 579 us -> 413 us (0.71)
  local copies, waits for them, and re-layouts: 146 us -> 43.5 us
  other arithmetic: 34.2 us -> 7.75 us
  matrix products: 47.6 us -> 30.1 us
  Pallas kernels: 339 us -> 325 us
    reshape x16 -> x6, local copies, waits for them, and re-layouts: 48.4 us -> 0.64 us  [the longest x1 0.61 us: shards(): sums[8:12].reshape(-1)]
    concatenate x5 -> x1, local copies, waits for them, and re-layouts: 23.2 us -> 1.25 us  [shards(): jnp.concatenate(small)]
    pallas_call x2, Pallas kernels: 185 us -> 167 us  [the longest x1 158 us: reduce_all(): pl.pallas_call(gradient_kernel, out_shape=[jax.ShapeDtypeStruct((2, 8, BL...]
    unnamed x104 -> x80, local copies, waits for them, and re-layouts: 42.7 us -> 26.6 us
    dot_general x5 -> x0, matrix products: 15.6 us -> none  [the longest x3 9.27 us: halves(): jnp.einsum('rm,rhc->hmc', left, right.reshape(-1, blocks, 384), preferred...]
    convert_element_type x4 -> x0, local copies, waits for them, and re-layouts: 13.3 us -> none  [the longest x3 9.7 us: columns(): return owned[first:last].transpose(1, 0, 2).reshape(share, -1).astype(F32)]
    concatenate x1 -> x0, other arithmetic: 12.4 us -> none  [shards(): jnp.concatenate([halves(inputs, grad_joined), halves(attended, grad_branc...]
    transpose x1 -> x0, local copies, waits for them, and re-layouts: 6.91 us -> none  [shards(): owned = owned.transpose(0, 1, 3, 2, 4, 5).reshape(24, share, 384)]
where the time goes in v2:
time: 413 us; the launch traced here: 408 us
  Pallas kernels  325 us (79%)
  local copies, waits for them, and re-layouts  43.5 us (11%)
  matrix products  30.1 us (7%)
  other arithmetic  7.75 us (2%)
    pallas_call x1, Pallas kernels, reduce_all(): pl.pallas_call(gradient_kernel, out_shape=[jax.ShapeDtypeStruct((2, 8, BL...  158 us
    pallas_call x1, Pallas kernels, gather_weights(): pl.pallas_call(functools.partial(gather_kernel, nf, cols, count), out_sha...  58 us
    pallas_call x1, Pallas kernels, spread(): pl.pallas_call(functools.partial(spread_kernel, cols), out_shape=[jax.Sha...  32.3 us
    pallas_call x2, Pallas kernels, swap(): pl.pallas_call(functools.partial(swap_kernel, cols, count), out_shape=[ja...  29.5 us
    unnamed x80, local copies, waits for them, and re-layouts  26.6 us
    pallas_call x1, Pallas kernels, attend_backward(): pl.pallas_call(functools.partial(backward_kernel, cols), out_shape=[jax.S...  23.4 us
    pallas_call x1, Pallas kernels, attend_forward(): pl.pallas_call(functools.partial(forward_kernel, cols), out_shape=[jax.Sh...  14.8 us
    dot_general x1, matrix products, shards(): hidden = jnp.dot(normed_low, full_in, preferred_element_type=F32) + b_in  11.4 us

profile of v2, /device:TPU:9, one launch (start us, length us, event | category | flops | bytes accessed | tf_op | source)
XLA Modules:
  0.0 408.0 jit_solution(11808244041319106)
XLA Ops:
  0.7 0.9 dynamic-update-slice
  1.5 0.9 dynamic-update-slice.1
  2.4 0.9 dynamic-update-slice.2
  3.2 0.9 dynamic-update-slice.3
  4.1 0.9 dynamic-update-slice.4
  5.0 0.9 dynamic-update-slice.5
  5.8 0.9 dynamic-update-slice.6
  6.7 0.9 dynamic-update-slice.7
  7.5 0.9 dynamic-update-slice.8
  8.5 1.7 copy-done.1
  10.2 1.7 copy-done.2
  11.8 1.5 copy-done.3
  13.3 1.1 copy-done.8
  14.4 58.0 %gather_weights.1 = (bf16[768,2304]{1,0:T(8,128)(2,1)S(1)}, bf16[768,768]{1,0:T(8,128)(2,1)S(1)}, bf16[768,3072]{1,0:T(8,128)(2,1)S(1)}, bf16[3072,768]{1,0:T(8,128)(2,1)S(1)}, bf16[2,8,576]{2,1,0:T(8,128)(2,1)S(1)}) custom-call(bf16[384,2304]{1,0:T(8,128)(2,1)S(1)} %copy-done.3, bf16[384,768]{1,0:T(8,128)(2,1)S(1)} %copy-done.8, ...), custom_call_target="tpu_custom_call" | custom-call | tf_op jit(solution)/shard_map/gather_weights/pallas_call | solution.py:104
  72.4 1.0 copy-done.5
  73.4 0.6 copy-done.10
  74.0 2.2 copy-done.12
  76.2 2.2 copy-done.13
  78.4 1.8 reshape.224
  80.1 1.4 fusion.21
  81.5 0.6 add.107
  82.1 0.7 slice.97
  82.9 0.6 add.104
  83.5 0.7 add.96
  84.2 0.7 reshape.196
  84.8 0.7 reshape.195
  85.5 2.3 fusion.1
  87.9 1.0 fusion.20
  88.9 1.1 reshape.197
  90.0 0.4 copy.36
  90.5 1.1 reshape.201
  91.6 0.4 copy.38
  92.1 0.4 copy.37
  92.8 32.3 %spread.1 = (bf16[8,128,256]{2,1,0:T(8,128)(2,1)S(1)}, bf16[16,128,384]{2,1,0:T(8,128)(2,1)S(1)}) custom-call(bf16[8,128,256]{2,1,0:T(8,128)(2,1)S(1)} %bitcast.75, bf16[8,128,384]{2,1,0:T(8,128)(2,1)S(1)} %pad_maximum_fusion.kv), custom_call_target="tpu_custom_call" | custom-call | tf_op jit(solution)/shard_map/spread/pallas_call | solution.py:200
  125.1 14.8 %attend_forward.1 = (bf16[1024,256]{1,0:T(8,128)(2,1)S(1)}, f32[4,256,256]{2,1,0:T(8,128)S(1)}, f32[4,8,256]{2,1,0:T(8,128)S(1)}) custom-call(s32[2,4]{1,0:T(2,128)S(1)} %copy-done.11, bf16[1024,256]{1,0:T(8,128)(2,1)S(1)} %bitcast.79, bf16[2048,384]{1,0:T(8,128)(2,1)S(1)} %bitcast.73), custom_call_target="tpu_custom_call" | custom-call | tf_op jit(solution)/shard_map/attend_forward/pallas_call | solution.py:550
  139.9 1.1 copy-done.6
  141.0 14.7 %swap.2 = bf16[8,128,256]{2,1,0:T(8,128)(2,1)S(1)} custom-call(bf16[8,128,256]{2,1,0:T(8,128)(2,1)S(1)} %bitcast.83), custom_call_target="tpu_custom_call" | custom-call | tf_op jit(solution)/shard_map/swap/pallas_call | solution.py:147
  155.9 0.4 copy.43
  156.3 2.1 fusion.22
  159.0 11.4 %multiply_convert_fusion = (bf16[256,3072]{1,0:T(8,128)(2,1)S(1)}, f32[256,3072]{1,0:T(8,128)}, f32[256,3072]{1,0:T(8,128)}) fusion(f32[3072]{0:T(1024)S(1)} %copy-done.30, bf16[256,768]{1,0:T(8,128)(2,1)S(1)} %fusion.14.low, bf16[768,3072]{1,0:T(8,128)(2,1)} %copy-done.12), kind=kOutput, calls=%fused_computation.8 | convolution fusion | flops 1259864064 | bytes 12988416 | tf_op jit(solution)/shard_map/dot_general | solution.py:1141
  170.4 1.5 fusion.23
  172.0 0.9 copy-done.14
  173.1 1.5 fusion.13
  174.6 2.5 fusion.18
  177.1 1.1 copy.50
  178.2 0.9 copy.42.att
  179.1 1.3 convert_reduce_fusion.2
  180.4 6.4 %convert_reduce_fusion = (f32[3072]{0:T(1024)S(1)}, bf16[256,3072]{1,0:T(8,128)(2,1)S(1)}) fusion(f32[256,3072]{1,0:T(8,128)} %get-tuple-element.78, f32[256,3072]{1,0:T(8,128)} %get-tuple-element.93, bf16[256,768]{1,0:T(8,128)(2,1)S(1)} %get-tuple-element.69.gsec, bf16[3072,768]{1,0:T(8,128)(2,1)} %copy-done.13), kind=kOutput, calls=%fused_computation.6 | convolution fusion | flops 1220539392 | bytes 12988416 | tf_op jit(solution)/shard_map/rm,km->rk/dot_general | solution.py:1150
  186.9 4.6 %multiply_reduce_fusion = (f32[768]{0:T(1024)S(1)}, f32[256]{0:T(256)S(1)}, f32[768]{0:T(1024)S(1)}, f32[256,768]{1,0:T(8,128)S(1)}) fusion(f32[256,768]{1,0:T(8,128)S(1)} %get-tuple-element.92, f32[256]{0:T(256)S(1)} %fusion.15, f32[256]{0:T(256)S(1)} %broadcast_multiply_fusion.1, f32[768]{0:T(1024)S(1)} %mul.155, ...), kind=kOutput, calls=%fused_computation.38 | convolution fusion | flops 1209923840 | bytes 8664064 | tf_op jit(solution)/shard_map/rf,mf->rm/dot_general | solution.py:1153
  191.5 0.3 fusion.17
  191.9 1.0 convert_reduce_fusion.3
  193.1 1.3 concatenate.15.small
  194.3 1.8 convolution_convert_fusion
  196.4 0.4 copy.44
  197.0 14.8 %swap.3 = bf16[8,128,256]{2,1,0:T(8,128)(2,1)S(1)} custom-call(bf16[8,128,256]{2,1,0:T(8,128)(2,1)S(1)} %bitcast.76), custom_call_target="tpu_custom_call" | custom-call | tf_op jit(solution)/shard_map/swap/pallas_call | solution.py:147
  211.9 1.2 copy-done.7
  213.1 23.4 %attend_backward.1 = (bf16[1024,256]{1,0:T(8,128)(2,1)S(1)}, bf16[2048,384]{1,0:T(8,128)(2,1)S(1)}) custom-call(s32[2,4]{1,0:T(2,128)S(1)} %copy-done.11, bf16[1024,256]{1,0:T(8,128)(2,1)S(1)} %bitcast.80, bf16[2048,384]{1,0:T(8,128)(2,1)S(1)} %bitcast.74, bf16[1024,256]{1,0:T(8,128)(2,1)S(1)} %bitcast.78, f32[4,256,256]{2,1,0:T(8,128)S(1)} %copy-done.7, ...), custom_call_target="tpu_custom_call" | custom-call | tf_op jit(solution)/shard_map/attend_backward/pallas_call | solution.py:624
  236.5 1.1 copy-done.4
  237.6 0.8 copy-done.9
  238.4 158.0 %reduce_all.1 = (bf16[2,8,48,4608]{3,2,1,0:T(8,128)(2,1)}, f32[256,768]{1,0:T(8,128)}, f32[16,384]{1,0:T(8,128)}) custom-call(bf16[256,768]{1,0:T(8,128)(2,1)} %bitcast.97, bf16[256,768]{1,0:T(8,128)(2,1)} %copy.42.att, bf16[256,768]{1,0:T(8,128)(2,1)} %copy-done.19, bf16[256,3072]{1,0:T(8,128)(2,1)} %copy-done.23, bf16[256,768]{1,0:T(8,128)(2,1)} %copy-done.15, ...), custom_call_target="tpu_custom_call" | custom-call | tf_op jit(solution)/shard_map/reduce_all/pallas_call | solution.py:1045
  396.5 9.4 %widen.1 = (f32[384,2304]{1,0:T(8,128)}, f32[384,768]{1,0:T(8,128)}, f32[384,3072]{1,0:T(8,128)}, f32[4,384,768]{2,1,0:T(8,128)}) custom-call(bf16[2,384,4608]{2,1,0:T(8,128)(2,1)} %bitcast.86), custom_call_target="tpu_custom_call" | custom-call | tf_op jit(solution)/shard_map/widen/pallas_call | solution.py:1079
  405.9 0.6 slice_reduce_fusion
  406.5 0.6 reshape.223
  407.1 0.9 copy.61
  (93 shorter events, 2.3 us)
Async XLA Ops:
  8.5 1.7 copy-start.1
  10.2 1.7 copy-start.2
  11.8 1.5 copy-start.3
  13.3 1.1 copy-start.8
  72.4 1.0 copy-start.5
  73.4 0.6 copy-start.10
  74.0 2.2 copy-start.12
  76.2 2.2 copy-start.13
  78.4 9.5 %copy-start = (bf16[768,2304]{1,0:T(8,128)(2,1)}, bf16[768,2304]{1,0:T(8,128)(2,1)S(1)}, u32[]{:S(2)}) copy-start(bf16[768,2304]{1,0:T(8,128)(2,1)S(1)} %get-tuple-element.34.wqkv) | copy-start | bytes 10616836
  88.9 3.1 copy-start.22
  90.5 34.6 %copy-start.11 = (s32[2,4]{1,0:T(2,128)S(1)}, s32[2,4]{1,0:T(2,128)}, u32[]{:S(2)}) copy-start(s32[2,4]{1,0:T(2,128)} %lens.3) | copy-start | bytes 100
  139.9 1.1 copy-start.6
  141.0 17.5 %copy-start.29 = (f32[2,384]{1,0:T(2,128)S(1)}, f32[2,384]{1,0:T(2,128)}, u32[]{:S(2)}) copy-start(f32[2,384]{1,0:T(2,128)} %get-tuple-element.86) | copy-start | bytes 9220
  141.0 17.5 %copy-start.28 = (f32[2,384]{1,0:T(2,128)S(1)}, f32[2,384]{1,0:T(2,128)}, u32[]{:S(2)}) copy-start(f32[2,384]{1,0:T(2,128)} %get-tuple-element.87) | copy-start | bytes 9220
  155.9 3.1 copy-start.30
  156.3 2.4 copy-start.21
  158.7 11.6 %slice-start = ((s8[4718592]{0:T(1024)(128)(4,1)}), s8[4194304]{0:T(1024)(128)(4,1)S(1)}, s32[]{:S(2)}) async-start(s8[4718592]{0:T(1024)(128)(4,1)} %bitcast.84), calls=%async_computation | async-start | bytes 8388608
  159.0 11.4 %copy-start.19 = (bf16[256,768]{1,0:T(8,128)(2,1)}, bf16[256,768]{1,0:T(8,128)(2,1)S(1)}, u32[]{:S(2)}) copy-start(bf16[256,768]{1,0:T(8,128)(2,1)S(1)} %fusion.14.low) | copy-start | bytes 1179652
  159.0 11.4 %slice-start.1 = ((s8[4718592]{0:T(1024)(128)(4,1)}), s8[524288]{0:T(1024)(128)(4,1)S(1)}, s32[]{:S(2)}) async-start(s8[4718592]{0:T(1024)(128)(4,1)} %bitcast.84), calls=%async_computation.1 | async-start | bytes 1048576
  159.0 11.4 %copy-start.31 = (f32[768]{0:T(1024)S(1)}, f32[768]{0:T(1024)}, u32[]{:S(2)}) copy-start(f32[768]{0:T(1024)} %add.107) | copy-start | bytes 9220
  170.4 1.6 copy-start.23
  170.4 2.7 copy-start.27
  170.4 2.7 copy-start.16
  171.9 0.9 copy-start.14
  180.4 6.4 %copy-start.20 = (bf16[256,768]{1,0:T(8,128)(2,1)}, bf16[256,768]{1,0:T(8,128)(2,1)S(1)}, u32[]{:S(2)}) copy-start(bf16[256,768]{1,0:T(8,128)(2,1)S(1)} %get-tuple-element.69.gsec) | copy-start | bytes 1179652
  180.4 6.4 %copy-start.18 = (f32[256,768]{1,0:T(8,128)S(1)}, f32[256,768]{1,0:T(8,128)}, u32[]{:S(2)}) copy-start(f32[256,768]{1,0:T(8,128)} %get-tuple-element.76) | copy-start | bytes 2359300
  186.8 4.6 %copy-start.24 = (bf16[256,3072]{1,0:T(8,128)(2,1)}, bf16[256,3072]{1,0:T(8,128)(2,1)S(1)}, u32[]{:S(2)}) copy-start(bf16[256,3072]{1,0:T(8,128)(2,1)S(1)} %get-tuple-element.67.ghid) | copy-start | bytes 4718596
  191.5 1.5 copy-start.17
  192.9 19.0 %copy-start.15 = (bf16[256,768]{1,0:T(8,128)(2,1)}, bf16[256,768]{1,0:T(8,128)(2,1)S(1)}, u32[]{:S(2)}) copy-start(bf16[256,768]{1,0:T(8,128)(2,1)S(1)} %get-tuple-element.71.gbr) | copy-start | bytes 1179652
  211.9 1.2 copy-start.7
  236.5 1.1 copy-start.4
  237.6 0.8 copy-start.9
  396.4 9.4 %copy-start.26 = (f32[16,384]{1,0:T(8,128)S(1)}, f32[16,384]{1,0:T(8,128)}, u32[]{:S(2)}) copy-start(f32[16,384]{1,0:T(8,128)} %get-tuple-element.52) | copy-start | bytes 73732
  396.4 10.7 %copy-start.25 = (f32[256,768]{1,0:T(8,128)S(1)}, f32[256,768]{1,0:T(8,128)}, u32[]{:S(2)}) copy-start(f32[256,768]{1,0:T(8,128)} %get-tuple-element.46) | copy-start | bytes 2359300

commit v3 on v2

--- a/solution.py
+++ b/solution.py
@@ -1086,6 +1086,247 @@
         name="widen",
     )(grads)
 
+STEPS = ((1, 0), (3, 0), (1, 1), (3, 1), (2, 0), (0, 1), (2, 1))
+
+
+class Octet:
+    def __init__(self, go):
+        self.go = go
+        self.a, self.b, self.c, self.f = a, b, c, f = place(2)
+        self.me = a * 2 + c
+        self.others = [lax.rem(a + da, 4) * 2 + lax.rem(c + dc, 2) for da, dc in STEPS]
+        self.sources = [lax.rem(a + 4 - da, 4) * 2 + lax.rem(c + dc, 2) for da, dc in STEPS]
+        self.devices = [device(lax.rem(a + da, 4), b, lax.rem(c + dc, 2), f, 2) for da, dc in STEPS]
+        self.relay, self.beyond = self.devices[3], self.devices[1]
+        self.origin = lax.rem(a + 1, 4) * 2 + 1 - c
+
+    def send(self, n, source, target, spare):
+        if n < 6:
+            return self.go(source, target(self.me), self.devices[n])
+        return self.go(source, spare, self.relay)
+
+    def forward(self, copy, target, spare):
+        copy.wait_recv()
+        return self.go(spare, target(self.origin), self.beyond)
+
+
+def project_kernel(tokens, *refs):
+    shards, vectors = refs[:4], refs[4:13]
+    q_held, kv_held, f_qkv, f_out, f_in, f_back, vec = refs[13:20]
+    own = refs[20:24]
+    whole, acc, q_sent, kv_sent, v_own, token, q_spare, kv_spare = refs[24:32]
+    flat, (send, recv, here) = refs[32:41], refs[41:]
+    fulls = (f_qkv, f_out, f_in, f_back)
+    a, b, c, f = place(2)
+    group = Octet(None)
+    me = group.me
+    odd_a = lax.rem(a, 2)
+    xp, yp, sp = device(a, 1 - b, c, f, 2), device(a, b, c, 1 - f, 2), device(a, b, 1 - c, f, 2)
+    pairs = [device(lax.rem(a + 5 - 2 * odd_a, 4), b, c, f, 2), device(lax.rem(a + 3 + 2 * odd_a, 4), b, c, f, 2)]
+    loads = [pltpu.make_async_copy(shards[w], own[w], here.at[w]) for w in range(4)]
+    flats = [pltpu.make_async_copy(ref, flat[n], here.at[12 + n]) for n, ref in enumerate(vectors)]
+    flats.append(pltpu.make_async_copy(tokens, token, here.at[11]))
+    for cp in flats + loads:
+        cp.start()
+    meet(group.devices + [xp, yp])
+    wires = Wires(send, recv)
+    go = group.go = wires.go
+
+    def rows_of(w, which, chunk):
+        size = shards[w].shape[0] // 4
+        return pl.multiple_of(which * 2 * size + chunk * size, 16), size
+
+    def cols_of(w, cc):
+        half = shards[w].shape[1] // 2
+        return pl.ds(pl.multiple_of(cc * half, 128), half)
+
+    def region(target, w, owner, which, cc, chunk):
+        start, size = rows_of(w, which, chunk)
+        return target.at[pl.ds(owner * shards[w].shape[0] + start, size), cols_of(w, cc)]
+
+    def source(w, which, chunk):
+        start, size = rows_of(w, which, chunk)
+        return shards[w].at[pl.ds(start, size), cols_of(w, c)]
+
+    other_f = 1 - f
+
+    class Fetch:
+        def __init__(self, target, w, chunk, pair=None):
+            self.target, self.w, self.chunk = target, w, chunk
+            self.which = b if pair is None else odd_a
+            self.peer = xp if pair is None else pairs[pair]
+            self.first = go(source(w, self.which, chunk), region(target, w, f, self.which, c, chunk), yp)
+
+        def second(self):
+            self.first.wait_recv()
+            got = region(self.target, self.w, other_f, self.which, c, self.chunk)
+            self.cross = go(got, got, self.peer)
+            self.side = go(got, got, sp)
+
+        def third(self):
+            self.cross.wait_recv()
+            got = region(self.target, self.w, other_f, 1 - self.which, c, self.chunk)
+            self.side2 = go(got, got, sp)
+
+        def end(self):
+            self.side.wait_recv()
+            self.side2.wait_recv()
+
+    class Straight:
+        def __init__(self, target, w, chunk, which):
+            self.place = (target, w, other_f, which, c, chunk)
+            self.first = go(source(w, which, chunk), region(target, w, f, which, c, chunk), yp)
+
+        def second(self):
+            self.first.wait_recv()
+            got = region(*self.place)
+            self.side = go(got, got, sp)
+
+        def third(self):
+            pass
+
+        def end(self):
+            self.side.wait_recv()
+
+    qkv = [Fetch(whole, 0, 0)]
+    for cp in flats:
+        cp.wait()
+    for n in range(9):
+        value = flat[n][...].astype(F32)
+        if n == 3:
+            for j in range(4):
+                v_own[8 + j:9 + j] = value[384 * j:384 * j + 384].reshape(1, 384)
+        else:
+            row = n if n < 3 else n - 1
+            v_own[row:row + 1] = value.reshape(1, 384)
+    v_own[12:16] = jnp.zeros((4, 384), F32)
+    vec[f] = v_own[...]
+    small = go(v_own, vec.at[f], yp)
+    loads[0].wait()
+    mine = pl.ds(pl.multiple_of(f * 384, 128), 384)
+    theirs = pl.ds(pl.multiple_of(other_f * 384, 128), 384)
+
+    @pl.loop(0, 6)
+    def _(n):
+        cols = pl.ds(pl.multiple_of(n * 384, 128), 384)
+        acc[:, cols] = dot(token[:, mine], own[0][:, cols], NN)
+
+    qkv[0].second()
+    qkv.append(Fetch(whole, 0, 1))
+    qkv[1].second()
+    outer = [Fetch(f_back, 3, chunk, chunk) for chunk in range(2)]
+    rest = [Fetch(f_out, 1, chunk) for chunk in range(2)]
+    inner = [Straight(f_in, 2, chunk, which) for chunk in range(2) for which in range(2)]
+    qkv[0].third()
+    qkv[1].third()
+    stores = []
+    for w in range(4):
+        if w > 0:
+            loads[w].wait()
+        rows = shards[w].shape[0]
+        cp = pltpu.make_async_copy(own[w], fulls[w].at[pl.ds(pl.multiple_of(f * rows, 16), rows)], here.at[4 + w])
+        cp.start()
+        stores.append(cp)
+    small.wait_recv()
+    qkv[0].end()
+    qkv[1].end()
+    cp = pltpu.make_async_copy(whole.at[pl.ds(pl.multiple_of(other_f * 384, 16), 384)],
+                               f_qkv.at[pl.ds(pl.multiple_of(other_f * 384, 16), 384)], here.at[8])
+    cp.start()
+    stores.append(cp)
+
+    def column(n):
+        cols = slice(384 * n, 384 * n + 384)
+        value = acc[:, cols] + dot(token[:, theirs], whole[pl.ds(pl.multiple_of(other_f * 384, 16), 384), cols], NN)
+        if n < 2:
+            value = value + vec[n, 0:1]
+        if n >= 4:
+            value = value + vec[n - 4, 1:2]
+        return value
+
+    lane = lax.broadcasted_iota(jnp.int32, (256, 384), 1)
+    for p in range(2):
+        k, v = column(2 + p), column(4 + p)
+        turned_k, turned_v = pltpu.roll(k, 192, 1), pltpu.roll(v, 192, 1)
+        even = jnp.where(lane < 192, k, turned_v).astype(BF16)
+        odd = jnp.where(lane < 192, turned_k, v).astype(BF16)
+        q = column(p)
+        q_even = jnp.where(lane < 192, q, 0.0)[:, :256].astype(BF16)
+        q_odd = jnp.where(lane < 192, pltpu.roll(q, 192, 1), 0.0)[:, :256].astype(BF16)
+        for s in range(2):
+            rows = slice(128 * s, 128 * s + 128)
+            kv_sent[4 * p + s], kv_sent[4 * p + 2 + s] = even[rows], odd[rows]
+            q_sent[4 * p + s], q_sent[4 * p + 2 + s] = q_even[rows], q_odd[rows]
+
+    def slot(block, bb):
+        return (block // 2 * 2 + bb) * 2 + lax.rem(block, 2)
+
+    kv_slot = lambda block: kv_held.at[slot(block, b)]
+    q_slot = lambda block: q_held.at[block]
+    first = [group.send(n, kv_sent.at[group.others[n]], kv_slot, kv_spare) for n in (6, 0, 1, 2, 3, 4, 5)]
+    first = first[1:] + first[:1]
+    own_kv = pltpu.make_async_copy(kv_sent.at[me], kv_held.at[slot(me, b)], here.at[9])
+    own_kv.start()
+    own_q = pltpu.make_async_copy(q_sent.at[me], q_held.at[me], here.at[10])
+    own_q.start()
+    crossed = [go(kv_sent.at[me], kv_held.at[slot(me, b)], xp)]
+    third = [group.send(n, q_sent.at[group.others[n]], q_slot, q_spare) for n in (6, 0, 1, 2, 3, 4, 5)]
+    third = third[1:] + third[:1]
+
+    def onward(n):
+        first[n].wait_recv()
+        piece = kv_slot(group.sources[n])
+        crossed.append(go(piece, piece, xp))
+
+    onward(5)
+    onward(0)
+    onward(1)
+    first[6] = group.forward(first[6], kv_slot, kv_spare)
+    for cp in outer:
+        cp.second()
+    for cp in rest:
+        cp.second()
+    onward(2)
+    onward(3)
+    third[6] = group.forward(third[6], q_slot, q_spare)
+    onward(4)
+    onward(6)
+    for cp in inner:
+        cp.second()
+    for cp in outer:
+        cp.third()
+    for cp in rest:
+        cp.third()
+    for cp in crossed + third:
+        cp.wait_recv()
+    for cp in rest + inner + outer:
+        cp.end()
+    for cp in wires.made:
+        cp.wait_send()
+    for cp in stores + [own_kv, own_q]:
+        cp.wait()
+
+
+def project(tokens, shards, vectors, ident):
+    rows, width = tokens.shape
+    anywhere = pl.BlockSpec(memory_space=pl.ANY)
+    wires = 64
+    return pl.pallas_call(
+        project_kernel,
+        out_shape=[jax.ShapeDtypeStruct((8, 128, 256), BF16), jax.ShapeDtypeStruct((16, 128, 384), BF16)]
+        + [jax.ShapeDtypeStruct((2 * s.shape[0], s.shape[1]), BF16) for s in shards]
+        + [jax.ShapeDtypeStruct((2, 16, 384), F32)],
+        in_specs=[pl.BlockSpec(memory_space=pltpu.HBM)] * 14,
+        out_specs=[vmem()] * 2 + [anywhere] * 4 + [vmem()],
+        scratch_shapes=[pltpu.VMEM(s.shape, BF16) for s in shards]
+        + [pltpu.VMEM((768, 2304), BF16), pltpu.VMEM((256, 2304), F32), pltpu.VMEM((8, 128, 256), BF16),
+           pltpu.VMEM((8, 128, 384), BF16), pltpu.VMEM((16, 384), F32), pltpu.VMEM(tokens.shape, BF16),
+           pltpu.VMEM((128, 256), BF16), pltpu.VMEM((128, 384), BF16),
+           *[pltpu.VMEM(v.shape, BF16) for v in vectors], DMA((wires,)), DMA((wires,)), DMA((21,))],
+        compiler_params=pltpu.CompilerParams(collective_id=ident, has_side_effects=True, vmem_limit_bytes=62 << 20),
+        name="project",
+    )(tokens, *shards, *vectors)
+
 
 def layer_norm(values, gain_row, shift_row):
     average = jnp.mean(values, axis=-1, keepdims=True)
@@ -1114,24 +1355,32 @@
     micro, per, width = tokens.shape
     nf, cols = lax.axis_size("fsdp"), lax.axis_size("ctx") // 8
     share = width // nf
-    tiny = jnp.concatenate(vectors).reshape(8, -1)
-    full_qkv, full_out, full_in, full_back, tinies = gather_weights((w_qkv, w_out, w_in, w_back), tiny, nf, cols)
-    tinies = tinies.reshape(nf, -1).astype(F32)
-    named, at = [], 0
-    for vector in vectors:
-        size = vector.shape[0]
-        named.append(tinies[:, at:at + size].reshape(-1))
-        at += size
-    b_query, b_value, b_out, b_in, b_back, gain_one, shift_one, gain_two, shift_two = named
     inputs = tokens.reshape(micro * per, width)
-    joined = jnp.dot(inputs, full_qkv, preferred_element_type=F32)
-    bias = jnp.concatenate([b_query, jnp.zeros_like(b_query), b_value])
-    joined = (joined + bias).astype(BF16)
-    q_sent = by_group(joined[:, :width], micro, 0, 64)
-    kv_sent = jnp.concatenate([by_group(joined[:, width:2 * width], micro, 0, 0), by_group(joined[:, 2 * width:], micro, 0, 0)], axis=2)
-    q_held, kv_held = spread(q_sent, kv_sent, cols, 2)
-    q_held = q_held.reshape(8 * per, 256)
-    kv_held = kv_held.reshape(-1, 384)
+    cube = nf == 2 and cols == 2
+    if cube:
+        q_held, kv_held, full_qkv, full_out, full_in, full_back, sides = project(inputs, (w_qkv, w_out, w_in, w_back), vectors, 1)
+        q_held = q_held.reshape(8 * per, 256)
+        kv_held = kv_held.reshape(-1, 384)
+        b_out, b_back, gain_one, shift_one, gain_two, shift_two = [sides[:, n].reshape(-1) for n in range(2, 8)]
+        b_in = sides[:, 8:12].reshape(-1)
+    else:
+        tiny = jnp.concatenate(vectors).reshape(8, -1)
+        full_qkv, full_out, full_in, full_back, tinies = gather_weights((w_qkv, w_out, w_in, w_back), tiny, nf, cols)
+        tinies = tinies.reshape(nf, -1).astype(F32)
+        named, at = [], 0
+        for vector in vectors:
+            size = vector.shape[0]
+            named.append(tinies[:, at:at + size].reshape(-1))
+            at += size
+        b_query, b_value, b_out, b_in, b_back, gain_one, shift_one, gain_two, shift_two = named
+        joined = jnp.dot(inputs, full_qkv, preferred_element_type=F32)
+        bias = jnp.concatenate([b_query, jnp.zeros_like(b_query), b_value])
+        joined = (joined + bias).astype(BF16)
+        q_sent = by_group(joined[:, :width], micro, 0, 64)
+        kv_sent = jnp.concatenate([by_group(joined[:, width:2 * width], micro, 0, 0), by_group(joined[:, 2 * width:], micro, 0, 0)], axis=2)
+        q_held, kv_held = spread(q_sent, kv_sent, cols, 2)
+        q_held = q_held.reshape(8 * per, 256)
+        kv_held = kv_held.reshape(-1, 384)
     mixed, mixed_t, log_total = attend_forward(doc_lengths, q_held, kv_held, cols)
     (back,) = swap([mixed.reshape(8, per, 256)], cols, 3)
     attended = from_group(back, micro, 64)
@@ -1156,11 +1405,11 @@
     g_out_bias = jnp.sum(grad_branch.astype(F32), axis=0)
     grad_attended = jnp.einsum("rm,km->rk", grad_branch, full_out, preferred_element_type=F32).astype(BF16)
     (do_held,) = swap([by_group(grad_attended, micro, 64, 0)], cols, 4)
-    if nf == 2 and cols == 2:
+    if cube:
         small = [jnp.zeros((2, width), F32)] + [x[None] for x in (g_out_bias, g_back_bias, g_gain_one, g_shift_one, g_gain_two, g_shift_two)]
         small += [g_in_bias.reshape(2, 4, share).transpose(1, 0, 2).reshape(4, width), jnp.zeros((4, width), F32)]
     dq, dkv = attend_backward(doc_lengths, q_held, kv_held, do_held.reshape(8 * per, 256), mixed_t, log_total, cols)
-    if nf == 2 and cols == 2:
+    if cube:
         grads, input_grad, sums = reduce_all(
             inputs, attended, normed_low, activated, grad_branch, grad_hidden, grad_second, grad_first, full_qkv,
             jnp.concatenate(small), dq.reshape(8, per, 256), dkv.reshape(8 * cols, per, 384), 5)

time: 413 us -> 363 us (0.88)
  local copies, waits for them, and re-layouts: 43.5 us -> 19.3 us
  Pallas kernels: 325 us -> 307 us
    pallas_call x2 -> x1, Pallas kernels: 90.3 us -> 69.7 us  [project(): pl.pallas_call(project_kernel, out_shape=[jax.ShapeDtypeStruct((8, 128, 2...]
    unnamed x80 -> x42, local copies, waits for them, and re-layouts: 26.6 us -> 8.72 us
    pallas_call x1, Pallas kernels: 158 us -> 165 us  [reduce_all(): pl.pallas_call(gradient_kernel, out_shape=[jax.ShapeDtypeStruct((2, 8, BL...]
    pallas_call x1, Pallas kernels: 23.4 us -> 18.6 us  [attend_backward(): pl.pallas_call(functools.partial(backward_kernel, cols), out_shape=[jax.S...]
where the time goes in v3:
time: 363 us; the launch traced here: 361 us
  Pallas kernels  307 us (85%)
  matrix products  28.6 us (8%)
  local copies, waits for them, and re-layouts  19.3 us (5%)
  other arithmetic  5.27 us (1%)
    pallas_call x1, Pallas kernels, reduce_all(): pl.pallas_call(gradient_kernel, out_shape=[jax.ShapeDtypeStruct((2, 8, BL...  165 us
    pallas_call x1, Pallas kernels, project(): pl.pallas_call(project_kernel, out_shape=[jax.ShapeDtypeStruct((8, 128, 2...  69.7 us
    pallas_call x2, Pallas kernels, swap(): pl.pallas_call(functools.partial(swap_kernel, cols, count), out_shape=[ja...  32.6 us
    pallas_call x1, Pallas kernels, attend_backward(): pl.pallas_call(functools.partial(backward_kernel, cols), out_shape=[jax.S...  18.6 us
    pallas_call x1, Pallas kernels, attend_forward(): pl.pallas_call(functools.partial(forward_kernel, cols), out_shape=[jax.Sh...  11.8 us
    dot_general x1, matrix products, shards(): hidden = jnp.dot(normed_low, full_in, preferred_element_type=F32) + b_in  11.4 us
    pallas_call x1, Pallas kernels, widen(): pl.pallas_call(widen_kernel, grid=(rows // step,), out_shape=[jax.ShapeDt...  9.41 us
    unnamed x42, local copies, waits for them, and re-layouts  8.72 us

profile of v3, /device:TPU:9, one launch (start us, length us, event | category | flops | bytes accessed | tf_op | source)
XLA Modules:
  0.0 361.2 jit_solution(4626430956448066252)
XLA Ops:
  0.7 0.0 copy-start.6
  0.7 0.0 copy-start.9
  0.7 69.7 %project.1 = (bf16[8,128,256]{2,1,0:T(8,128)(2,1)}, bf16[16,128,384]{2,1,0:T(8,128)(2,1)}, bf16[768,2304]{1,0:T(8,128)(2,1)}, bf16[768,768]{1,0:T(8,128)(2,1)}, ...) custom-call(bf16[256,768]{1,0:T(8,128)(2,1)} %bitcast.66, bf16[384,2304]{1,0:T(8,128)(2,1)} %refs_0_.1, ...), custom_call_target="tpu_custom_call" | custom-call | tf_op jit(solution)/shard_map/project/pallas_call | solution.py:1314
  70.4 1.0 slice_reduce_fusion.1
  71.5 0.7 slice.55
  72.2 0.0 copy-done.6
  72.2 0.0 copy-start
  72.2 1.4 copy-done
  73.6 1.0 copy-done.2
  74.7 11.8 %attend_forward.1 = (bf16[1024,256]{1,0:T(8,128)(2,1)S(1)}, f32[4,256,256]{2,1,0:T(8,128)S(1)}, f32[4,8,256]{2,1,0:T(8,128)S(1)}) custom-call(s32[2,4]{1,0:T(2,128)S(1)} %copy-done.6, bf16[1024,256]{1,0:T(8,128)(2,1)S(1)} %bitcast.60, bf16[2048,384]{1,0:T(8,128)(2,1)S(1)} %bitcast.55), custom_call_target="tpu_custom_call" | custom-call | tf_op jit(solution)/shard_map/attend_forward/pallas_call | solution.py:550
  86.5 17.7 %swap.2 = bf16[8,128,256]{2,1,0:T(8,128)(2,1)S(1)} custom-call(bf16[8,128,256]{2,1,0:T(8,128)(2,1)S(1)} %bitcast.64), custom_call_target="tpu_custom_call" | custom-call | tf_op jit(solution)/shard_map/swap/pallas_call | solution.py:147
  104.2 0.2 slice.68
  104.4 0.4 copy.37
  104.9 0.0 copy-start.12
  104.9 0.0 copy-done.9
  104.9 2.0 fusion.18
  106.9 0.2 multiply_reduce_fusion.3
  107.1 0.0 copy-done.12
  107.2 0.0 slice-start
  107.2 0.2 fusion.12.low
  107.4 0.0 copy-start.10
  107.4 0.0 slice-start.1
  107.4 11.4 %multiply_convert_fusion = (bf16[256,3072]{1,0:T(8,128)(2,1)S(1)}, f32[256,3072]{1,0:T(8,128)}, f32[256,3072]{1,0:T(8,128)}) fusion(f32[3072]{0:T(1024)S(1)} %add.91, bf16[256,768]{1,0:T(8,128)(2,1)S(1)} %fusion.12.low, bf16[768,3072]{1,0:T(8,128)(2,1)} %get-tuple-element.39), kind=kOutput, calls=%fused_computation.5 | convolution fusion | flops 1259864064 | bytes 12988416 | tf_op jit(solution)/shard_map/dot_general | solution.py:1390
  118.8 0.0 copy-done.10
  118.8 0.0 slice-done
  118.8 0.0 slice-done.1
  118.8 0.0 copy-start.7
  118.8 1.5 fusion.19
  120.3 0.0 copy-done.13
  120.3 0.2 multiply_reduce_fusion.2
  120.6 0.0 copy-done.7
  120.6 0.4 fusion.11
  121.0 1.4 fusion.16
  122.3 1.1 copy.44
  123.4 0.9 copy.36.att
  124.3 1.3 convert_reduce_fusion.2
  125.6 0.0 copy-start.11
  125.6 0.0 copy-start.8
  125.6 6.4 %convert_reduce_fusion = (f32[3072]{0:T(1024)S(1)}, bf16[256,3072]{1,0:T(8,128)(2,1)S(1)}) fusion(f32[256,3072]{1,0:T(8,128)} %get-tuple-element.84, f32[256,3072]{1,0:T(8,128)} %get-tuple-element.88, bf16[256,768]{1,0:T(8,128)(2,1)S(1)} %get-tuple-element.75.gsec, bf16[3072,768]{1,0:T(8,128)(2,1)} %get-tuple-element.40), kind=kOutput, calls=%fused_computation.3 | convolution fusion | flops 1220539392 | bytes 12988416 | tf_op jit(solution)/shard_map/rm,km->rk/dot_general | solution.py:1399
  132.0 0.0 copy-done.11
  132.1 0.0 copy-start.14
  132.1 4.6 %multiply_reduce_fusion = (f32[768]{0:T(1024)S(1)}, f32[256]{0:T(256)S(1)}, f32[768]{0:T(1024)S(1)}, f32[256,768]{1,0:T(8,128)S(1)}) fusion(f32[256,768]{1,0:T(8,128)S(1)} %get-tuple-element.87, f32[256]{0:T(256)S(1)} %fusion.13, f32[256]{0:T(256)S(1)} %broadcast_multiply_fusion.1, f32[768]{0:T(1024)S(1)} %mul.155, ...), kind=kOutput, calls=%fused_computation.34 | convolution fusion | flops 1209923840 | bytes 8664064 | tf_op jit(solution)/shard_map/rf,mf->rm/dot_general | solution.py:1402
  136.7 0.0 copy-done.14
  136.7 0.3 fusion.15
  137.0 1.2 convert_reduce_fusion.3
  138.2 0.1 convert_reduce_fusion.1
  138.4 1.3 concatenate.3.small
  139.6 2.8 convolution_convert_fusion
  142.4 1.9 copy.34
  144.3 1.9 reshape.175
  146.2 1.9 copy.38
  148.1 1.3 pad.4.clone
  149.4 14.9 %swap.3 = bf16[8,128,256]{2,1,0:T(8,128)(2,1)S(1)} custom-call(bf16[8,128,256]{2,1,0:T(8,128)(2,1)S(1)} %bitcast.57), custom_call_target="tpu_custom_call" | custom-call | tf_op jit(solution)/shard_map/swap/pallas_call | solution.py:147
  164.3 18.6 %attend_backward.1 = (bf16[1024,256]{1,0:T(8,128)(2,1)S(1)}, bf16[2048,384]{1,0:T(8,128)(2,1)S(1)}) custom-call(s32[2,4]{1,0:T(2,128)S(1)} %copy-done.6, bf16[1024,256]{1,0:T(8,128)(2,1)S(1)} %bitcast.61, bf16[2048,384]{1,0:T(8,128)(2,1)S(1)} %bitcast.56, bf16[1024,256]{1,0:T(8,128)(2,1)S(1)} %bitcast.59, f32[4,256,256]{2,1,0:T(8,128)S(1)} %get-tuple-element.42.ot_ref, ...), custom_call_target="tpu_custom_call" | custom-call | tf_op jit(solution)/shard_map/attend_backward/pallas_call | solution.py:624
  182.9 0.0 copy-start.4
  182.9 1.1 copy-done.4
  184.0 0.8 copy-done.5
  184.8 164.8 %reduce_all.1 = (bf16[2,8,48,4608]{3,2,1,0:T(8,128)(2,1)}, f32[256,768]{1,0:T(8,128)}, f32[16,384]{1,0:T(8,128)}) custom-call(bf16[256,768]{1,0:T(8,128)(2,1)} %bitcast.67, bf16[256,768]{1,0:T(8,128)(2,1)} %copy.36.att, bf16[256,768]{1,0:T(8,128)(2,1)} %copy-done.10, bf16[256,3072]{1,0:T(8,128)(2,1)} %copy-done.13, bf16[256,768]{1,0:T(8,128)(2,1)} %get-tuple-element.77.gbr, ...), custom_call_target="tpu_custom_call" | custom-call | tf_op jit(solution)/shard_map/reduce_all/pallas_call | solution.py:1045
  349.6 0.0 copy-start.16
  349.6 0.0 copy-start.15
  349.6 9.4 %widen.1 = (f32[384,2304]{1,0:T(8,128)}, f32[384,768]{1,0:T(8,128)}, f32[384,3072]{1,0:T(8,128)}, f32[4,384,768]{2,1,0:T(8,128)}) custom-call(bf16[2,384,4608]{2,1,0:T(8,128)(2,1)} %bitcast.65), custom_call_target="tpu_custom_call" | custom-call | tf_op jit(solution)/shard_map/widen/pallas_call | solution.py:1079
  359.1 0.6 slice_reduce_fusion.6
  359.7 0.6 reshape.183
  360.3 0.9 copy.46
  (36 shorter events, 0.2 us)
Async XLA Ops:
  0.7 71.6 %copy-start.6 = (s32[2,4]{1,0:T(2,128)S(1)}, s32[2,4]{1,0:T(2,128)}, u32[]{:S(2)}) copy-start(s32[2,4]{1,0:T(2,128)} %lens.3) | copy-start | bytes 100
  0.7 104.2 %copy-start.9 = (bf16[2,128,768]{2,1,0:T(8,128)(2,1)S(1)}, bf16[2,128,768]{2,1,0:T(8,128)(2,1)}, u32[]{:S(2)}) copy-start(bf16[2,128,768]{2,1,0:T(8,128)(2,1)} %param.16) | copy-start | bytes 1179652
  72.2 1.4 copy-start
  73.6 1.0 copy-start.2
  104.9 2.3 copy-start.12
  107.2 11.6 %slice-start = ((s8[4718592]{0:T(1024)(128)(4,1)}), s8[4194304]{0:T(1024)(128)(4,1)S(1)}, s32[]{:S(2)}) async-start(s8[4718592]{0:T(1024)(128)(4,1)} %bitcast.76), calls=%async_computation | async-start | bytes 8388608
  107.4 11.4 %copy-start.10 = (bf16[256,768]{1,0:T(8,128)(2,1)}, bf16[256,768]{1,0:T(8,128)(2,1)S(1)}, u32[]{:S(2)}) copy-start(bf16[256,768]{1,0:T(8,128)(2,1)S(1)} %fusion.12.low) | copy-start | bytes 1179652
  107.4 11.4 %slice-start.1 = ((s8[4718592]{0:T(1024)(128)(4,1)}), s8[524288]{0:T(1024)(128)(4,1)S(1)}, s32[]{:S(2)}) async-start(s8[4718592]{0:T(1024)(128)(4,1)} %bitcast.76), calls=%async_computation.1 | async-start | bytes 1048576
  118.8 1.5 copy-start.13
  118.8 1.8 copy-start.7
  125.6 6.4 %copy-start.11 = (bf16[256,768]{1,0:T(8,128)(2,1)}, bf16[256,768]{1,0:T(8,128)(2,1)S(1)}, u32[]{:S(2)}) copy-start(bf16[256,768]{1,0:T(8,128)(2,1)S(1)} %get-tuple-element.75.gsec) | copy-start | bytes 1179652
  125.6 6.5 %copy-start.8 = (f32[256,768]{1,0:T(8,128)S(1)}, f32[256,768]{1,0:T(8,128)}, u32[]{:S(2)}) copy-start(f32[256,768]{1,0:T(8,128)} %get-tuple-element.82) | copy-start | bytes 2359300
  132.1 4.6 %copy-start.14 = (bf16[256,3072]{1,0:T(8,128)(2,1)}, bf16[256,3072]{1,0:T(8,128)(2,1)S(1)}, u32[]{:S(2)}) copy-start(bf16[256,3072]{1,0:T(8,128)(2,1)S(1)} %get-tuple-element.73.ghid) | copy-start | bytes 4718596
  139.6 24.7 %copy-start.1 = (bf16[16,128,384]{2,1,0:T(8,128)(2,1)S(1)}, bf16[16,128,384]{2,1,0:T(8,128)(2,1)}, u32[]{:S(2)}) copy-start(bf16[16,128,384]{2,1,0:T(8,128)(2,1)} %get-tuple-element.35) | copy-start | bytes 4718596
  139.6 24.7 %copy-start.3 = (bf16[8,128,256]{2,1,0:T(8,128)(2,1)S(1)}, bf16[8,128,256]{2,1,0:T(8,128)(2,1)}, u32[]{:S(2)}) copy-start(bf16[8,128,256]{2,1,0:T(8,128)(2,1)} %get-tuple-element.34) | copy-start | bytes 1572868
  182.9 1.1 copy-start.4
  184.0 0.8 copy-start.5
  349.6 9.4 %copy-start.16 = (f32[16,384]{1,0:T(8,128)S(1)}, f32[16,384]{1,0:T(8,128)}, u32[]{:S(2)}) copy-start(f32[16,384]{1,0:T(8,128)} %get-tuple-element.52) | copy-start | bytes 73732
  349.6 10.7 %copy-start.15 = (f32[256,768]{1,0:T(8,128)S(1)}, f32[256,768]{1,0:T(8,128)}, u32[]{:S(2)}) copy-start(f32[256,768]{1,0:T(8,128)} %get-tuple-element.46) | copy-start | bytes 2359300

commit v4 on v1

--- a/solution.py
+++ b/solution.py
@@ -633,6 +633,822 @@
     )(lens, q, kv, do, ot, lse)
 
 
+STEPS = ((1, 0), (3, 0), (1, 1), (3, 1), (2, 0), (0, 1), (2, 1))
+
+
+class Octet:
+    def __init__(self, go):
+        self.go = go
+        self.a, self.b, self.c, self.f = a, b, c, f = place(2)
+        self.me = a * 2 + c
+        self.others = [lax.rem(a + da, 4) * 2 + lax.rem(c + dc, 2) for da, dc in STEPS]
+        self.sources = [lax.rem(a + 4 - da, 4) * 2 + lax.rem(c + dc, 2) for da, dc in STEPS]
+        self.devices = [device(lax.rem(a + da, 4), b, lax.rem(c + dc, 2), f, 2) for da, dc in STEPS]
+        self.relay, self.beyond = self.devices[3], self.devices[1]
+        self.origin = lax.rem(a + 1, 4) * 2 + 1 - c
+
+    def send(self, n, source, target, spare):
+        if n < 6:
+            return self.go(source, target(self.me), self.devices[n])
+        return self.go(source, spare, self.relay)
+
+    def forward(self, copy, target, spare):
+        copy.wait_recv()
+        return self.go(spare, target(self.origin), self.beyond)
+
+
+def project_kernel(tokens, *refs):
+    shards, vectors = refs[:4], refs[4:13]
+    q_held, kv_held, f_qkv, f_out, f_in, f_back, vec, turned = refs[13:21]
+    own = refs[21:25]
+    whole, acc, q_sent, kv_sent, v_own, token, q_spare, kv_spare, held, held_spare = refs[25:35]
+    flat, (send, recv, here) = refs[35:44], refs[44:]
+    fulls = (f_qkv, f_out, f_in, f_back)
+    a, b, c, f = place(2)
+    group = Octet(None)
+    me = group.me
+    odd_a = lax.rem(a, 2)
+    xp, yp, sp = device(a, 1 - b, c, f, 2), device(a, b, c, 1 - f, 2), device(a, b, 1 - c, f, 2)
+    pairs = [device(lax.rem(a + 5 - 2 * odd_a, 4), b, c, f, 2), device(lax.rem(a + 3 + 2 * odd_a, 4), b, c, f, 2)]
+    loads = [pltpu.make_async_copy(shards[w], own[w], here.at[w]) for w in range(4)]
+    flats = [pltpu.make_async_copy(ref, flat[n], here.at[12 + n]) for n, ref in enumerate(vectors)]
+    flats.append(pltpu.make_async_copy(tokens, token, here.at[11]))
+    for cp in flats + loads:
+        cp.start()
+    meet(group.devices + [xp, yp])
+    wires = Wires(send, recv)
+    go = group.go = wires.go
+
+    def rows_of(w, which, chunk):
+        size = shards[w].shape[0] // 4
+        return pl.multiple_of(which * 2 * size + chunk * size, 16), size
+
+    def cols_of(w, cc):
+        half = shards[w].shape[1] // 2
+        return pl.ds(pl.multiple_of(cc * half, 128), half)
+
+    def region(target, w, owner, which, cc, chunk):
+        start, size = rows_of(w, which, chunk)
+        return target.at[pl.ds(owner * shards[w].shape[0] + start, size), cols_of(w, cc)]
+
+    def source(w, which, chunk):
+        start, size = rows_of(w, which, chunk)
+        return shards[w].at[pl.ds(start, size), cols_of(w, c)]
+
+    other_f = 1 - f
+
+    class Fetch:
+        def __init__(self, target, w, chunk, pair=None):
+            self.target, self.w, self.chunk = target, w, chunk
+            self.which = b if pair is None else odd_a
+            self.peer = xp if pair is None else pairs[pair]
+            self.first = go(source(w, self.which, chunk), region(target, w, f, self.which, c, chunk), yp)
+
+        def second(self):
+            self.first.wait_recv()
+            got = region(self.target, self.w, other_f, self.which, c, self.chunk)
+            self.cross = go(got, got, self.peer)
+            self.side = go(got, got, sp)
+
+        def third(self):
+            self.cross.wait_recv()
+            got = region(self.target, self.w, other_f, 1 - self.which, c, self.chunk)
+            self.side2 = go(got, got, sp)
+
+        def end(self):
+            self.side.wait_recv()
+            self.side2.wait_recv()
+
+    class Straight:
+        def __init__(self, target, w, chunk, which):
+            self.place = (target, w, other_f, which, c, chunk)
+            self.first = go(source(w, which, chunk), region(target, w, f, which, c, chunk), yp)
+
+        def second(self):
+            self.first.wait_recv()
+            got = region(*self.place)
+            self.side = go(got, got, sp)
+
+        def third(self):
+            pass
+
+        def end(self):
+            self.side.wait_recv()
+
+    qkv = [Fetch(whole, 0, 0)]
+    for cp in flats:
+        cp.wait()
+    held_slot = lambda block: held.at[block]
+
+    def token_block(dc):
+        return token.at[pl.ds(pl.multiple_of(lax.rem(c + dc, 2) * 128, 128), 128)]
+
+    toks = {n: group.send(n, token_block(STEPS[n][1]), held_slot, held_spare) for n in (6, 0, 1, 2, 3, 4, 5)}
+    held[me] = token[pl.ds(pl.multiple_of(c * 128, 128), 128)]
+    for n in range(9):
+        value = flat[n][...].astype(F32)
+        if n == 3:
+            for j in range(4):
+                v_own[8 + j:9 + j] = value[384 * j:384 * j + 384].reshape(1, 384)
+        else:
+            row = n if n < 3 else n - 1
+            v_own[row:row + 1] = value.reshape(1, 384)
+    v_own[12:16] = jnp.zeros((4, 384), F32)
+    vec[f] = v_own[...]
+    small = go(v_own, vec.at[f], yp)
+    loads[0].wait()
+    mine = pl.ds(pl.multiple_of(f * 384, 128), 384)
+    theirs = pl.ds(pl.multiple_of(other_f * 384, 128), 384)
+
+    @pl.loop(0, 6)
+    def _(n):
+        cols = pl.ds(pl.multiple_of(n * 384, 128), 384)
+        acc[:, cols] = dot(token[:, mine], own[0][:, cols], NN)
+
+    qkv[0].second()
+    qkv.append(Fetch(whole, 0, 1))
+    qkv[1].second()
+    outer = [Fetch(f_back, 3, chunk, chunk) for chunk in range(2)]
+    rest = [Fetch(f_out, 1, chunk) for chunk in range(2)]
+    inner = [Straight(f_in, 2, chunk, which) for chunk in range(2) for which in range(2)]
+    toks[6] = group.forward(toks[6], held_slot, held_spare)
+    qkv[0].third()
+    qkv[1].third()
+    stores = []
+    for w in range(4):
+        if w > 0:
+            loads[w].wait()
+        rows = shards[w].shape[0]
+        cp = pltpu.make_async_copy(own[w], fulls[w].at[pl.ds(pl.multiple_of(f * rows, 16), rows)], here.at[4 + w])
+        cp.start()
+        stores.append(cp)
+    small.wait_recv()
+    qkv[0].end()
+    qkv[1].end()
+    cp = pltpu.make_async_copy(whole.at[pl.ds(pl.multiple_of(other_f * 384, 16), 384)],
+                               f_qkv.at[pl.ds(pl.multiple_of(other_f * 384, 16), 384)], here.at[8])
+    cp.start()
+    stores.append(cp)
+
+    def column(n):
+        cols = slice(384 * n, 384 * n + 384)
+        value = acc[:, cols] + dot(token[:, theirs], whole[pl.ds(pl.multiple_of(other_f * 384, 16), 384), cols], NN)
+        if n < 2:
+            value = value + vec[n, 0:1]
+        if n >= 4:
+            value = value + vec[n - 4, 1:2]
+        return value
+
+    lane = lax.broadcasted_iota(jnp.int32, (256, 384), 1)
+    for p in range(2):
+        k, v = column(2 + p), column(4 + p)
+        turned_k, turned_v = pltpu.roll(k, 192, 1), pltpu.roll(v, 192, 1)
+        even = jnp.where(lane < 192, k, turned_v).astype(BF16)
+        odd = jnp.where(lane < 192, turned_k, v).astype(BF16)
+        q = column(p)
+        q_even = jnp.where(lane < 192, q, 0.0)[:, :256].astype(BF16)
+        q_odd = jnp.where(lane < 192, pltpu.roll(q, 192, 1), 0.0)[:, :256].astype(BF16)
+        for s in range(2):
+            rows = slice(128 * s, 128 * s + 128)
+            kv_sent[4 * p + s], kv_sent[4 * p + 2 + s] = even[rows], odd[rows]
+            q_sent[4 * p + s], q_sent[4 * p + 2 + s] = q_even[rows], q_odd[rows]
+
+    def slot(block, bb):
+        return (block // 2 * 2 + bb) * 2 + lax.rem(block, 2)
+
+    kv_slot = lambda block: kv_held.at[slot(block, b)]
+    q_slot = lambda block: q_held.at[block]
+    first = [group.send(n, kv_sent.at[group.others[n]], kv_slot, kv_spare) for n in (6, 0, 1, 2, 3, 4, 5)]
+    first = first[1:] + first[:1]
+    own_kv = pltpu.make_async_copy(kv_sent.at[me], kv_held.at[slot(me, b)], here.at[9])
+    own_kv.start()
+    own_q = pltpu.make_async_copy(q_sent.at[me], q_held.at[me], here.at[10])
+    own_q.start()
+    crossed = [go(kv_sent.at[me], kv_held.at[slot(me, b)], xp)]
+    third = [group.send(n, q_sent.at[group.others[n]], q_slot, q_spare) for n in (6, 0, 1, 2, 3, 4, 5)]
+    third = third[1:] + third[:1]
+
+    def onward(n):
+        first[n].wait_recv()
+        piece = kv_slot(group.sources[n])
+        crossed.append(go(piece, piece, xp))
+
+    onward(5)
+    onward(0)
+    onward(1)
+    first[6] = group.forward(first[6], kv_slot, kv_spare)
+    for cp in outer:
+        cp.second()
+    for cp in rest:
+        cp.second()
+    onward(2)
+    onward(3)
+    third[6] = group.forward(third[6], q_slot, q_spare)
+    onward(4)
+    onward(6)
+    for cp in toks.values():
+        cp.wait_recv()
+
+    @pl.loop(0, 8)
+    def _(n):
+        @pl.loop(0, 6)
+        def _(m):
+            lanes = pl.ds(pl.multiple_of(m * 128, 128), 128)
+            turned[n, lanes] = held[n, :, lanes].astype(F32).T.astype(BF16)
+
+    for cp in inner:
+        cp.second()
+    for cp in outer:
+        cp.third()
+    for cp in rest:
+        cp.third()
+    for cp in crossed + third:
+        cp.wait_recv()
+    for cp in rest + inner + outer:
+        cp.end()
+    for cp in wires.made:
+        cp.wait_send()
+    for cp in stores + [own_kv, own_q]:
+        cp.wait()
+
+
+def project(tokens, shards, vectors, ident):
+    rows, width = tokens.shape
+    anywhere = pl.BlockSpec(memory_space=pl.ANY)
+    wires = 80
+    return pl.pallas_call(
+        project_kernel,
+        out_shape=[jax.ShapeDtypeStruct((8, 128, 256), BF16), jax.ShapeDtypeStruct((16, 128, 384), BF16)]
+        + [jax.ShapeDtypeStruct((2 * s.shape[0], s.shape[1]), BF16) for s in shards]
+        + [jax.ShapeDtypeStruct((2, 16, 384), F32), jax.ShapeDtypeStruct((8, 768, 128), BF16)],
+        in_specs=[pl.BlockSpec(memory_space=pltpu.HBM)] * 14,
+        out_specs=[vmem()] * 2 + [anywhere] * 4 + [vmem()] * 2,
+        scratch_shapes=[pltpu.VMEM(s.shape, BF16) for s in shards]
+        + [pltpu.VMEM((768, 2304), BF16), pltpu.VMEM((256, 2304), F32), pltpu.VMEM((8, 128, 256), BF16),
+           pltpu.VMEM((8, 128, 384), BF16), pltpu.VMEM((16, 384), F32), pltpu.VMEM(tokens.shape, BF16),
+           pltpu.VMEM((128, 256), BF16), pltpu.VMEM((128, 384), BF16),
+           pltpu.VMEM((8, 128, 768), BF16), pltpu.VMEM((128, 768), BF16),
+           *[pltpu.VMEM(v.shape, BF16) for v in vectors], DMA((wires,)), DMA((wires,)), DMA((21,))],
+        compiler_params=pltpu.CompilerParams(collective_id=ident, has_side_effects=True, vmem_limit_bytes=62 << 20),
+        name="project",
+    )(tokens, *shards, *vectors)
+
+
+BLK = 48
+Z1, X1, Y1 = (0, 1152), (1152, 1920), (1920, 3456)
+L0, L1 = (0, 256), (256, 640)
+
+
+class Wires:
+    def __init__(self, send, recv):
+        self.send, self.recv, self.made = send, recv, []
+
+    def go(self, source, target, peer):
+        n = len(self.made)
+        cp = remote(source, target, self.send.at[n], self.recv.at[n], peer)
+        cp.start()
+        self.made.append(cp)
+        return cp
+
+
+def transpose_into(target, source, base):
+    width = source.shape[1]
+
+    @pl.loop(0, width // 128)
+    def _(n):
+        at = pl.multiple_of(n * 128, 128)
+        target[pl.ds(base + at, 128)] = source[:, pl.ds(at, 128)].astype(F32).T.astype(BF16)
+
+
+def pair_columns(even, odd, lane, second):
+    if second:
+        return jnp.where(lane < 192, pltpu.roll(even, 192, 1), odd)
+    return jnp.where(lane < 192, even, pltpu.roll(odd, 192, 1))
+
+
+def halves(span):
+    tiles = (span[1] - span[0]) // 128
+    mid = span[0] + tiles // 2 * 128
+    return (span[0], mid), (mid, span[1])
+
+
+def within(span, group):
+    base = 0
+    for member in group:
+        if member == span:
+            return slice(base, base + span[1] - span[0])
+        base += member[1] - member[0]
+
+
+def gradient_kernel(lens, tt, att, low, act, gbr, ghid, gsec, small, do_sent, q_ref, kv_ref, ot_ref, lse_ref,
+                    out, late_out, joined, small_out,
+                    xt, mine, sib, cin, y8, y4, x8, x4, z4, z1r, zyb, zxb,
+                    do_held, qm, dm, kt, dk, dv, acc, rowsc, delta, dq_all, dkv_all, dqo, dkvo, xsend, rbuf,
+                    l_sib, l_in, l_acc, l_mine, ly, lx,
+                    do_spare, dq_spare, dkv_spare, v_own, v_core, v_f, v_b, v_a, send, recv, here):
+    group = Octet(None)
+    a, b, c, f, me = group.a, group.b, group.c, group.f, group.me
+    xp, yp, sp = device(a, 1 - b, c, f, 2), device(a, b, c, 1 - f, 2), device(a, b, 1 - c, f, 2)
+    up, down = lax.rem(a + 1, 4), lax.rem(a + 3, 4)
+    upp, downp = device(up, b, c, f, 2), device(down, b, c, f, 2)
+    ends = bounds(lens, c)
+    total = kv_ref.shape[0]
+    meet(group.devices + [xp, yp])
+    wires = Wires(send, recv)
+    go = group.go = wires.go
+    pending = []
+
+    do_slot = lambda block: do_held.at[block]
+    swaps = {n: group.send(n, do_sent.at[group.others[n]], do_slot, do_spare) for n in (6, 0, 1, 2, 3, 4, 5)}
+    do_held[me] = do_sent[me]
+
+    transpose_into(xt, act, 1536)
+
+    def produce(kind, first, count, part, finish):
+        @pl.loop(0, 2 * count)
+        def _(n):
+            ff, j = lax.rem(n, 2), first + n // 2
+            if kind == "out":
+                left, right = xt[pl.ds(pl.multiple_of(ff * 384, 128), 384)], gbr[:, pl.ds(pl.multiple_of(part * 384, 128), 384)]
+                col = 0
+            elif kind == "in":
+                left = xt[pl.ds(pl.multiple_of(768 + ff * 384, 128), 384)]
+                right = ghid[:, pl.ds(pl.multiple_of(part * 1536 + j * 384, 128), 384)]
+                col = pl.multiple_of(384 + j * 384, 128)
+            else:
+                left = xt[pl.ds(pl.multiple_of(1536 + ff * 1536 + j * 384, 128), 384)]
+                right = gsec[:, pl.ds(pl.multiple_of(part * 384, 128), 384)]
+                col = pl.multiple_of(1920 + j * 384, 128)
+            finish(pl.ds(ff * 2, 2), pl.ds(col, 384), dot(left, right, NN).reshape(2, 4, BLK, 384))
+
+    def keep(rows, cols, value):
+        sib[rows, :, :, cols] = value.astype(BF16)
+
+    def join(rows, cols, value):
+        mine[rows, :, :, cols] = (value + cin[rows, :, :, cols].astype(F32)).astype(BF16)
+
+    core = {}
+
+    def share(span):
+        cols = slice(span[0], span[1])
+        core[span] = go(sib.at[:, :, :, cols], cin.at[:, :, :, cols], sp)
+
+    RS = (Y1, X1)
+
+    def add(target, source):
+        def step(n):
+            t, s = target(n), source(n)
+            t[...] = (t[...].astype(F32) + s[...].astype(F32)).astype(BF16)
+        return step
+
+    def accumulate(target, source, count):
+        pl.loop(0, count)(add(target, source))
+
+    ycols, xcols, zcols = slice(*Y1), slice(*X1), slice(*Z1)
+
+    def start_y():
+        return go(mine.at[pl.ds((1 - f) * 2, 2), :, :, ycols], y8, yp)
+
+    def start_x():
+        return [go(mine.at[ff * 2 + 1 - b, :, :, xcols], x8.at[ff], xp) for ff in range(2)]
+
+    def next_y(cp):
+        cp.wait_recv()
+        accumulate(lambda n: mine.at[f * 2 + n // 4, lax.rem(n, 4), :, ycols], lambda n: y8.at[n // 4, lax.rem(n, 4)], 8)
+        return go(mine.at[f * 2 + 1 - b, :, :, ycols], x4, xp)
+
+    def next_x(cps):
+        for cp in cps:
+            cp.wait_recv()
+        accumulate(lambda n: mine.at[n // 4 * 2 + b, lax.rem(n, 4), :, xcols], lambda n: x8.at[n // 4, lax.rem(n, 4)], 8)
+        return go(mine.at[(1 - f) * 2 + b, :, :, xcols], y4, yp)
+
+    def last_y(cp):
+        cp.wait_recv()
+        accumulate(lambda n: mine.at[f * 2 + b, n, :, ycols], lambda n: x4.at[n], 4)
+
+    def last_x(cp):
+        cp.wait_recv()
+        accumulate(lambda n: mine.at[f * 2 + b, n, :, xcols], lambda n: y4.at[n], 4)
+
+    def landing(span, step, part, single):
+        if single:
+            base = within(span, RS).start - span[0]
+            return z1r.at[step, :, base + part[0]:base + part[1]]
+        return z4.at[step, :, :, part[0]:part[1]]
+
+    def ring_source(aa, part, single):
+        cols = slice(part[0], part[1])
+        return mine.at[f * 2 + b, aa, :, cols] if single else mine.at[:, aa, :, cols]
+
+    def ring_send(span, step, single):
+        lo, hi = halves(span)
+        ud, dd = lax.rem(a + 3 - step, 4), lax.rem(a + 1 + step, 4)
+        return (go(ring_source(ud, lo, single), landing(span, step, lo, single), upp),
+                go(ring_source(dd, hi, single), landing(span, step, hi, single), downp))
+
+    def ring_add(span, step, single, cps):
+        lo, hi = halves(span)
+        ud, dd = lax.rem(a + 6 - step, 4), lax.rem(a + 2 + step, 4)
+        for cp, part, aa in zip(cps, (lo, hi), (ud, dd)):
+            cp.wait_recv()
+            got = landing(span, step, part, single)
+            if single:
+                add(lambda n: ring_source(aa, part, True), lambda n: got)(0)
+            else:
+                cols = slice(part[0], part[1])
+                accumulate(lambda n: mine.at[n, aa, :, cols], lambda n: got.at[n], 4)
+
+    def tail_z_y():
+        return go(mine.at[pl.ds((1 - f) * 2, 2), a, :, zcols], zyb, yp)
+
+    def tail_z_x(cp):
+        cp.wait_recv()
+        accumulate(lambda n: mine.at[f * 2 + n, a, :, zcols], lambda n: zyb.at[n], 2)
+        return go(mine.at[f * 2 + 1 - b, a, :, zcols], zxb, xp)
+
+    def tail_z_end(cp):
+        cp.wait_recv()
+        add(lambda n: mine.at[f * 2 + b, a, :, zcols], lambda n: zxb)(0)
+
+    class Gather:
+        def __init__(self, own, spot, span, first):
+            self.span, self.first, self.spot = span, first, spot
+            self.own = own
+            self.copy = pltpu.make_async_copy(own, spot(b, a, span), here.at[len(locals_)])
+            self.copy.start()
+            locals_.append(self.copy)
+            pending.append(go(own, spot(b, a, span), sp))
+            self.ring = go(own, spot(b, a, span), upp), go(own, spot(b, a, span), downp)
+            self.cross = go(own, spot(b, a, span), xp)
+
+        def spread(self, bb, aa):
+            p = self.spot(bb, aa, self.span)
+            pending.append(go(p, p, sp))
+
+        def passed(self, bb, ring):
+            lo, hi = halves(self.span)
+            ring[0].wait_recv()
+            p = self.spot(bb, down, lo)
+            first = go(p, p, upp)
+            ring[1].wait_recv()
+            p = self.spot(bb, up, hi)
+            second = go(p, p, downp)
+            for aa in (down, up):
+                self.spread(bb, aa)
+            return first, second
+
+        def arrived(self, bb, ring):
+            for cp in ring:
+                cp.wait_recv()
+            self.spread(bb, lax.rem(a + 2, 4))
+
+        def second(self):
+            self.ring2 = self.passed(b, self.ring)
+            if self.first == "b":
+                self.cross.wait_recv()
+                self.spread(1 - b, a)
+                p = self.spot(1 - b, a, self.span)
+                self.other = go(p, p, upp), go(p, p, downp)
+            else:
+                spots = [self.spot(b, aa, self.span) for aa in (down, up)]
+                self.more = [go(p, p, xp) for p in spots]
+
+        def third(self):
+            self.arrived(b, self.ring2)
+            if self.first == "b":
+                self.other2 = self.passed(1 - b, self.other)
+            else:
+                p = self.spot(b, lax.rem(a + 2, 4), self.span)
+                self.more.append(go(p, p, xp))
+                self.cross.wait_recv()
+                self.spread(1 - b, a)
+
+        def fourth(self):
+            if self.first == "b":
+                self.arrived(1 - b, self.other2)
+            else:
+                for cp, aa in zip(self.more, (down, up, lax.rem(a + 2, 4))):
+                    cp.wait_recv()
+                    self.spread(1 - b, aa)
+
+    locals_ = []
+
+    def early_spot(bb, aa, span):
+        return out.at[c, bb * 4 + aa, :, span[0]:span[1]]
+
+    def late_spot(bb, aa, span):
+        return late_out.at[aa, bb * 2 + c, :, span[0]:span[1]]
+
+    def early_gather(span, first):
+        return Gather(mine.at[f * 2 + b, a, :, span[0]:span[1]], early_spot, span, first)
+
+    def prepare():
+        @pl.loop(0, total // KB)
+        def _(n):
+            rows = pl.ds(pl.multiple_of(n * KB, KB), KB)
+            kt[:, rows] = kv_ref[rows, 0:256].astype(F32).T.astype(BF16)
+
+        @pl.loop(0, 4)
+        def _(stripe):
+            head = lane_head((SPAN, 256), 0)
+            headv = lane_head((SPAN, 256), 64)
+            q = q_ref[pl.ds(stripe * 2, 2)].reshape(SPAN, 256).astype(F32) * 0.125
+            grad = do_held[pl.ds(stripe * 2, 2)].reshape(SPAN, 256).astype(F32)
+            for h in range(3):
+                qm[stripe, h] = jnp.where(head == h, q, 0.0).astype(BF16)
+                dm[stripe, h] = jnp.where(headv == h, grad, 0.0).astype(BF16)
+            prod = grad.T * ot_ref[stripe]
+            for h in range(3):
+                delta[stripe, h:h + 1] = jnp.sum(prod[64 * (h + 1):64 * (h + 2)], axis=0, keepdims=True)
+            qpos = SPAN * (stripe * 2 + b) + lax.broadcasted_iota(jnp.int32, (1, SPAN), 1)
+            start, stop = doc_range(qpos, ends)
+            rowsc[stripe, 0:1] = start
+            rowsc[stripe, 1:2] = stop
+            acc[stripe] = jnp.zeros((256, SPAN), F32)
+
+    reach = total * 5 // 8 // KB
+
+    def attend(da, parity):
+        block = lax.rem(a + da, 4) * 2 + parity
+        krows = pl.ds(pl.multiple_of(block * KB, KB), KB)
+        dk[...] = jnp.zeros((KB, 256), F32)
+        dv[...] = jnp.zeros((KB, 256), F32)
+        @pl.loop(0, 4)
+        def _(stripe):
+            away = stripe * 2 + b - block
+
+            @pl.when((away <= reach) & (away >= -reach))
+            def _():
+                keys = kv_ref[krows, 0:256]
+                vals = kv_ref[krows, 128:384]
+                kpos = block * KB + lax.broadcasted_iota(jnp.int32, (KB, 1), 0)
+                allowed = (kpos >= rowsc[stripe, 0:1]) & (kpos < rowsc[stripe, 1:2])
+                newk, newv = dk[...], dv[...]
+                for h in range(3):
+                    s = jnp.where(allowed, dot(keys, qm[stripe, h], NT), MASKED)
+                    p = jnp.exp(s - lse_ref[stripe, h:h + 1])
+                    gp = dot(vals, dm[stripe, h], NT)
+                    ds = (p * (gp - delta[stripe, h:h + 1])).astype(BF16)
+                    newv = newv + dot(p.astype(BF16), dm[stripe, h], NN)
+                    newk = newk + dot(ds, qm[stripe, h], NN)
+                    hrows = pl.ds(64 * h, 64)
+                    acc[stripe, hrows] = acc[stripe, hrows] + dot(kt[hrows, krows], ds, NN)
+                dk[...] = newk
+                dv[...] = newv
+
+    def slot(block, bb):
+        return (block // 2 * 2 + bb) * 2 + lax.rem(block, 2)
+
+    def grads_of(dc):
+        rows = pl.ds(pl.multiple_of(lax.rem(c + dc, 2) * 128, 128), 128)
+        k, v = dk[rows], dv[rows]
+        return jnp.concatenate([k[:, :128], k[:, 128:] + v[:, :128], v[:, 128:]], axis=1)
+
+    FAR, NEXT = ((6, 1), (4, 0)), ((0, 0), (2, 1))
+    BACK, HERE = ((1, 0), (3, 1)), ((5, 1), (7, 0))
+    crossed = {}
+
+    def cross(members):
+        for n, dc in members:
+            xsend[n] = grads_of(dc).astype(BF16)
+            crossed[n] = go(xsend.at[n], rbuf.at[n], xp)
+
+    dkv_slot = lambda block: dkvo.at[block]
+    dkvs = {}
+
+    def settle(members):
+        for n, dc in members:
+            crossed[n].wait_recv()
+            value = (grads_of(dc) + rbuf[n].astype(F32)).astype(BF16)
+            if n == 7:
+                dkv_all[me] = value
+                dkvo[me] = value
+            else:
+                dkv_all[group.others[n]] = value
+                dkvs[n] = group.send(n, dkv_all.at[group.others[n]], dkv_slot, dkv_spare)
+
+    dq_slot = lambda block: dqo.at[block]
+    dqs = {}
+
+    produce("back", 0, 4, 1 - c, keep)
+    share(Y1)
+    swaps[6] = group.forward(swaps[6], do_slot, do_spare)
+    transpose_into(xt, att, 0)
+    transpose_into(xt, low, 768)
+    produce("out", 0, 1, 1 - c, keep)
+    produce("in", 0, 2, 1 - c, keep)
+    share(Z1)
+    core[Y1].wait_recv()
+    produce("back", 0, 4, c, join)
+    y1 = start_y()
+    core[Z1].wait_recv()
+    produce("out", 0, 1, c, join)
+    produce("in", 0, 2, c, join)
+    z1 = ring_send(Z1, 0, False)
+    produce("in", 2, 2, 1 - c, keep)
+    share(X1)
+    for cp in swaps.values():
+        cp.wait_recv()
+    prepare()
+    core[X1].wait_recv()
+    produce("in", 2, 2, c, join)
+    x1 = start_x()
+    attend(2, 1 - b)
+    cross(FAR)
+    ring_add(Z1, 0, False, z1)
+    z1 = ring_send(Z1, 1, False)
+    attend(1, 1 - b)
+    cross(NEXT)
+    ring_add(Z1, 1, False, z1)
+    z1 = ring_send(Z1, 2, False)
+    attend(3, 1 - b)
+    cross(BACK)
+    x1 = next_x(x1)
+    attend(0, 1 - b)
+    cross(HERE)
+    ring_add(Z1, 2, False, z1)
+    z1 = tail_z_y()
+    attend(2, b)
+    settle(FAR)
+    y1 = next_y(y1)
+    attend(1, b)
+    settle(NEXT)
+    last_x(x1)
+    x1 = ring_send(X1, 0, True)
+    z1 = tail_z_x(z1)
+    attend(3, b)
+    settle(BACK)
+    ring_add(X1, 0, True, x1)
+    x1 = ring_send(X1, 1, True)
+    tail_z_end(z1)
+    g_z1 = early_gather(Z1, "a")
+    attend(0, b)
+
+    @pl.loop(0, 4)
+    def _(stripe):
+        dq_all[pl.ds(stripe * 2, 2)] = (acc[stripe] * 0.125).T.astype(BF16).reshape(2, 128, 256)
+
+    for n in (6, 0, 1, 2, 3, 4, 5):
+        dqs[n] = group.send(n, dq_all.at[group.others[n]], dq_slot, dq_spare)
+    dqo[me] = dq_all[me]
+    settle(HERE)
+    dkvs[6] = group.forward(dkvs[6], dkv_slot, dkv_spare)
+
+    def project_back(n, right):
+        rows = pl.ds(pl.multiple_of(n * 96, 32), 96)
+        value = dot(tt[0, rows], right[0], NN)
+        for m in range(1, 8):
+            value = value + dot(tt[m, rows], right[m], NN)
+        return value
+
+    @pl.loop(0, 4)
+    def _(n):
+        theirs, ours = n * 2 + 1 - c, n * 2 + c
+        l_sib[n, :, 0:256] = project_back(theirs, dq_all).astype(BF16)
+        l_sib[n, :, 256:640] = project_back(theirs, dkv_all).astype(BF16)
+        l_acc[n, :, 0:256] = project_back(ours, dq_all)
+        l_acc[n, :, 256:640] = project_back(ours, dkv_all)
+
+    late = go(l_sib, l_in, sp)
+    last_y(y1)
+    y1 = ring_send(Y1, 0, True)
+    dqs[6] = group.forward(dqs[6], dq_slot, dq_spare)
+    late.wait_recv()
+
+    @pl.loop(0, 4)
+    def _(n):
+        l_mine[n] = (l_acc[n] + l_in[n].astype(F32)).astype(BF16)
+
+    late = go(l_mine.at[pl.ds((1 - f) * 2, 2)], ly, yp)
+    ring_add(X1, 1, True, x1)
+    x1 = ring_send(X1, 2, True)
+    g_z1.second()
+    ring_add(Y1, 0, True, y1)
+    y1 = ring_send(Y1, 1, True)
+    late.wait_recv()
+    accumulate(lambda n: l_mine.at[f * 2 + n], lambda n: ly.at[n], 2)
+    late = go(l_mine.at[f * 2 + 1 - b], lx, xp)
+    ring_add(X1, 2, True, x1)
+    g_x1 = early_gather(X1, "b")
+    ring_add(Y1, 1, True, y1)
+    y1 = ring_send(Y1, 2, True)
+
+    for cp in list(dqs.values()) + list(dkvs.values()):
+        cp.wait_recv()
+    lane = lax.broadcasted_iota(jnp.int32, (128, 384), 1)
+    for s in range(2):
+        rows = slice(s * 128, s * 128 + 128)
+        for p in range(2):
+            even, odd = 4 * p + s, 4 * p + 2 + s
+            blank = jnp.zeros((128, 128), F32)
+            qe = jnp.concatenate([dqo[even].astype(F32), blank], axis=1)
+            qo = jnp.concatenate([dqo[odd].astype(F32), blank], axis=1)
+            joined[rows, 384 * p:384 * p + 384] = pair_columns(qe, qo, lane, False).astype(BF16)
+            ke, ko = dkvo[even].astype(F32), dkvo[odd].astype(F32)
+            joined[rows, 768 + 384 * p:1152 + 384 * p] = pair_columns(ke, ko, lane, False).astype(BF16)
+            joined[rows, 1536 + 384 * p:1920 + 384 * p] = pair_columns(ke, ko, lane, True).astype(BF16)
+    v_own[...] = small[...]
+    v_own[0:1] = jnp.sum(joined[:, 0:768].astype(F32), axis=0, keepdims=True)
+    v_own[1:2] = jnp.sum(joined[:, 1536:2304].astype(F32), axis=0, keepdims=True)
+    vec = go(v_own, v_core, sp)
+
+    late.wait_recv()
+    add(lambda n: l_mine.at[f * 2 + b], lambda n: lx)(0)
+    g_l0 = Gather(l_mine.at[f * 2 + b, :, L0[0]:L0[1]], late_spot, L0, "a")
+    g_l1 = Gather(l_mine.at[f * 2 + b, :, L1[0]:L1[1]], late_spot, L1, "b")
+    ring_add(Y1, 2, True, y1)
+    g_y1 = early_gather(Y1, "b")
+    vec.wait_recv()
+    v_core[...] = v_own[...] + v_core[...]
+    vec = go(v_core.at[:, pl.ds(pl.multiple_of((1 - f) * 384, 128), 384)], v_f, yp)
+    g_z1.third()
+    g_x1.second()
+    g_l0.second()
+    g_l1.second()
+    vec.wait_recv()
+    v_b[b] = v_core[:, pl.ds(pl.multiple_of(f * 384, 128), 384)] + v_f[...]
+    vec = go(v_b.at[b], v_b.at[b], xp)
+    g_y1.second()
+    g_z1.fourth()
+    g_x1.third()
+    g_l0.third()
+    g_l1.third()
+    vec.wait_recv()
+    v_a[a] = v_b[0] + v_b[1]
+    vec = [go(v_a.at[a], v_a.at[a], device(lax.rem(a + k, 4), b, c, f, 2)) for k in range(1, 4)]
+    g_y1.third()
+    g_x1.fourth()
+    g_l0.fourth()
+    g_l1.fourth()
+    g_y1.fourth()
+    for cp in vec + pending:
+        cp.wait_recv()
+    small_out[...] = v_a[0] + v_a[1] + v_a[2] + v_a[3]
+    for cp in locals_:
+        cp.wait()
+    for cp in wires.made:
+        cp.wait_send()
+
+
+def reduce_all(lens, tt, att, low, act, gbr, ghid, gsec, small, do_sent, q, kv, ot, lse, ident):
+    wires = 192
+    total = kv.shape[0]
+    bf = lambda *shape: pltpu.VMEM(shape, BF16)
+    fl = lambda *shape: pltpu.VMEM(shape, F32)
+    anywhere = pl.BlockSpec(memory_space=pl.ANY)
+    return pl.pallas_call(
+        gradient_kernel,
+        out_shape=[jax.ShapeDtypeStruct((2, 8, BLK, 3456), BF16), jax.ShapeDtypeStruct((4, 4, 96, 640), BF16),
+                   jax.ShapeDtypeStruct((256, 2304), BF16), jax.ShapeDtypeStruct((16, 384), F32)],
+        in_specs=[pl.BlockSpec(memory_space=pltpu.SMEM)] + [vmem()] * 13, out_specs=[anywhere] * 2 + [vmem()] * 2,
+        scratch_shapes=[
+            bf(4608, 256), bf(4, 4, BLK, 3456), bf(4, 4, BLK, 3456), bf(4, 4, BLK, 3456),
+            bf(2, 4, BLK, 1536), bf(4, BLK, 768), bf(2, 4, BLK, 768), bf(4, BLK, 1536),
+            bf(3, 4, BLK, 1152), bf(3, BLK, 2304), bf(2, BLK, 1152), bf(BLK, 1152),
+            bf(8, 128, 256), bf(4, 3, SPAN, 256), bf(4, 3, SPAN, 256), bf(256, total), fl(KB, 256), fl(KB, 256), fl(4, 256, SPAN),
+            pltpu.VMEM((4, 8, SPAN), jnp.int32), fl(4, 8, SPAN),
+            bf(8, 128, 256), bf(8, 128, 384), bf(8, 128, 256), bf(8, 128, 384), bf(8, 128, 384), bf(8, 128, 384),
+            bf(4, 96, 640), bf(4, 96, 640), fl(4, 96, 640), bf(4, 96, 640), bf(2, 96, 640), bf(96, 640),
+            bf(128, 256), bf(128, 256), bf(128, 384),
+            fl(16, 768), fl(16, 768), fl(16, 384), fl(2, 16, 384), fl(4, 16, 384),
+            DMA((wires,)), DMA((wires,)), DMA((5,))],
+        compiler_params=pltpu.CompilerParams(collective_id=ident, has_side_effects=True, vmem_limit_bytes=62 << 20),
+        name="reduce_all",
+    )(lens, tt, att, low, act, gbr, ghid, gsec, small, do_sent, q, kv, ot, lse)
+
+
+def widen_kernel(grads, late, g_qkv, g_out, g_in, g_back):
+    for core in range(2):
+        part = grads.at[core]
+        g_out[:, core * 384:core * 384 + 384] = part[:, 0:384].astype(F32)
+        g_in[:, core * 1536:core * 1536 + 1536] = part[:, 384:1920].astype(F32)
+        for j in range(4):
+            g_back[j, :, core * 384:core * 384 + 384] = part[:, 1920 + 384 * j:2304 + 384 * j].astype(F32)
+    lane = lax.broadcasted_iota(jnp.int32, (96, 384), 1)
+    for p in range(2):
+        even, odd = late[2 * p, 0].astype(F32), late[2 * p + 1, 0].astype(F32)
+        g_qkv[:, 384 * p:384 * p + 384] = pair_columns(even[:, :384], odd[:, :384], lane, False)
+        ke, ko = even[:, 256:], odd[:, 256:]
+        g_qkv[:, 768 + 384 * p:1152 + 384 * p] = pair_columns(ke, ko, lane, False)
+        g_qkv[:, 1536 + 384 * p:1920 + 384 * p] = pair_columns(ke, ko, lane, True)
+
+
+def widen(grads, late):
+    rows, step = 384, 96
+    spec = lambda wide: pl.BlockSpec((step, wide), lambda n: (n, 0))
+    return pl.pallas_call(
+        widen_kernel,
+        grid=(rows // step,),
+        out_shape=[jax.ShapeDtypeStruct((rows, 2304), F32), jax.ShapeDtypeStruct((rows, 768), F32),
+                   jax.ShapeDtypeStruct((rows, 3072), F32), jax.ShapeDtypeStruct((4, rows, 768), F32)],
+        in_specs=[pl.BlockSpec((2, step, 3456), lambda n: (0, n, 0)), pl.BlockSpec((4, 1, step, 640), lambda n: (0, n, 0, 0))],
+        out_specs=[spec(2304), spec(768), spec(3072), pl.BlockSpec((4, step, 768), lambda n: (0, n, 0))],
+        compiler_params=pltpu.CompilerParams(vmem_limit_bytes=40 << 20),
+        name="widen",
+    )(grads, late)
+
+
 def layer_norm(values, gain_row, shift_row):
     average = jnp.mean(values, axis=-1, keepdims=True)
     centered = values - average
@@ -660,24 +1476,32 @@
     micro, per, width = tokens.shape
     nf, cols = lax.axis_size("fsdp"), lax.axis_size("ctx") // 8
     share = width // nf
-    tiny = jnp.concatenate(vectors).reshape(8, -1)
-    full_qkv, full_out, full_in, full_back, tinies = gather_weights((w_qkv, w_out, w_in, w_back), tiny, nf, cols)
-    tinies = tinies.reshape(nf, -1).astype(F32)
-    named, at = [], 0
-    for vector in vectors:
-        size = vector.shape[0]
-        named.append(tinies[:, at:at + size].reshape(-1))
-        at += size
-    b_query, b_value, b_out, b_in, b_back, gain_one, shift_one, gain_two, shift_two = named
     inputs = tokens.reshape(micro * per, width)
-    joined = jnp.dot(inputs, full_qkv, preferred_element_type=F32)
-    bias = jnp.concatenate([b_query, jnp.zeros_like(b_query), b_value])
-    joined = (joined + bias).astype(BF16)
-    q_sent = by_group(joined[:, :width], micro, 0, 64)
-    kv_sent = jnp.concatenate([by_group(joined[:, width:2 * width], micro, 0, 0), by_group(joined[:, 2 * width:], micro, 0, 0)], axis=2)
-    q_held, kv_held = spread(q_sent, kv_sent, cols, 2)
-    q_held = q_held.reshape(8 * per, 256)
-    kv_held = kv_held.reshape(-1, 384)
+    cube = nf == 2 and cols == 2
+    if cube:
+        q_held, kv_held, full_qkv, full_out, full_in, full_back, sides, turned = project(inputs, (w_qkv, w_out, w_in, w_back), vectors, 1)
+        q_held = q_held.reshape(8 * per, 256)
+        kv_held = kv_held.reshape(-1, 384)
+        b_out, b_back, gain_one, shift_one, gain_two, shift_two = [sides[:, n].reshape(-1) for n in range(2, 8)]
+        b_in = sides[:, 8:12].reshape(-1)
+    else:
+        tiny = jnp.concatenate(vectors).reshape(8, -1)
+        full_qkv, full_out, full_in, full_back, tinies = gather_weights((w_qkv, w_out, w_in, w_back), tiny, nf, cols)
+        tinies = tinies.reshape(nf, -1).astype(F32)
+        named, at = [], 0
+        for vector in vectors:
+            size = vector.shape[0]
+            named.append(tinies[:, at:at + size].reshape(-1))
+            at += size
+        b_query, b_value, b_out, b_in, b_back, gain_one, shift_one, gain_two, shift_two = named
+        joined = jnp.dot(inputs, full_qkv, preferred_element_type=F32)
+        bias = jnp.concatenate([b_query, jnp.zeros_like(b_query), b_value])
+        joined = (joined + bias).astype(BF16)
+        q_sent = by_group(joined[:, :width], micro, 0, 64)
+        kv_sent = jnp.concatenate([by_group(joined[:, width:2 * width], micro, 0, 0), by_group(joined[:, 2 * width:], micro, 0, 0)], axis=2)
+        q_held, kv_held = spread(q_sent, kv_sent, cols, 2)
+        q_held = q_held.reshape(8 * per, 256)
+        kv_held = kv_held.reshape(-1, 384)
     mixed, mixed_t, log_total = attend_forward(doc_lengths, q_held, kv_held, cols)
     (back,) = swap([mixed.reshape(8, per, 256)], cols, 3)
     attended = from_group(back, micro, 64)
@@ -701,7 +1525,18 @@
     grad_branch = grad_first.astype(BF16)
     g_out_bias = jnp.sum(grad_branch.astype(F32), axis=0)
     grad_attended = jnp.einsum("rm,km->rk", grad_branch, full_out, preferred_element_type=F32).astype(BF16)
-    (do_held,) = swap([by_group(grad_attended, micro, 64, 0)], cols, 4)
+    do_sent = by_group(grad_attended, micro, 64, 0)
+    if cube:
+        small = [jnp.zeros((2, width), F32)] + [x[None] for x in (g_out_bias, g_back_bias, g_gain_one, g_shift_one, g_gain_two, g_shift_two)]
+        small += [g_in_bias.reshape(2, 4, share).transpose(1, 0, 2).reshape(4, width), jnp.zeros((4, width), F32)]
+        grads, late, grad_joined, sums = reduce_all(
+            doc_lengths, turned, attended, normed_low, activated, grad_branch, grad_hidden, grad_second, jnp.concatenate(small),
+            do_sent, q_held.reshape(8, per, 256), kv_held, mixed_t, log_total, 5)
+        g_qkv, g_out, g_in, g_back = widen(grads.reshape(2, share, 3456), late)
+        input_grad = grad_first + jnp.einsum("rc,mc->rm", grad_joined, full_qkv, preferred_element_type=F32)
+        rows = [sums[0], sums[1], sums[2], sums[8:12].reshape(-1), sums[3], sums[4], sums[5], sums[6], sums[7]]
+        return (output.reshape(tokens.shape), input_grad.reshape(tokens.shape), g_qkv, g_out, g_in, g_back.reshape(4 * share, width)) + tuple(rows)
+    (do_held,) = swap([do_sent], cols, 4)
     dq, dkv = attend_backward(doc_lengths, q_held, kv_held, do_held.reshape(8 * per, 256), mixed_t, log_total, cols)
     dq_own, dkv_own = collect(dq.reshape(8, per, 256), dkv.reshape(8 * cols, per, 384), cols, 5)
     grad_joined = jnp.concatenate(

time: 579 us -> 328 us (0.57); the launches traced: 568 us -> 326 us
  local copies, waits for them, and re-layouts: 146 us -> 12.8 us
  Pallas kernels: 339 us -> 277 us
  other arithmetic: 34.2 us -> 4.11 us
  matrix products: 47.6 us -> 30.4 us
    reshape x19 -> x6, local copies, waits for them, and re-layouts: 48.5 us -> 0.64 us  [the longest x1 0.61 us: shards(): sums[8:12].reshape(-1)]
    pallas_call x5 -> x3, Pallas kernels: 296 us -> 249 us  [the longest x1 159 us: reduce_all(): pl.pallas_call(gradient_kernel, out_shape=[jax.ShapeDtypeStruct((2, 8, BL...]
    unnamed x104 -> x43, local copies, waits for them, and re-layouts: 42.7 us -> 5.87 us
    concatenate x6 -> x1, local copies, waits for them, and re-layouts: 24 us -> 1.26 us  [shards(): jnp.concatenate(small)]
    dot_general x5 -> x0, matrix products: 16.2 us -> none  [the longest x3 9.27 us: halves(): jnp.einsum('rm,rhc->hmc', left, right.reshape(-1, blocks, 384), preferred...]
    pallas_call x2 -> x1, Pallas kernels: 29.5 us -> 14 us  [swap(): pl.pallas_call(functools.partial(swap_kernel, cols, count), out_shape=[ja...]
    convert_element_type x5 -> x0, local copies, waits for them, and re-layouts: 13.4 us -> none  [the longest x3 9.7 us: columns(): return owned[first:last].transpose(1, 0, 2).reshape(share, -1).astype(F32)]
    concatenate x3 -> x0, other arithmetic: 12.7 us -> none  [the longest x1 12.4 us: shards(): jnp.concatenate([halves(inputs, grad_joined), halves(attended, grad_branc...]
where the time goes in v4:
time: 328 us; the launch traced here: 326 us
  Pallas kernels  277 us (84%)
  matrix products  30.4 us (9%)
  local copies, waits for them, and re-layouts  12.8 us (4%)
  other arithmetic  4.11 us (1%)
    pallas_call x1, Pallas kernels, reduce_all(): pl.pallas_call(gradient_kernel, out_shape=[jax.ShapeDtypeStruct((2, 8, BL...  159 us
    pallas_call x1, Pallas kernels, project(): pl.pallas_call(project_kernel, out_shape=[jax.ShapeDtypeStruct((8, 128, 2...  84.4 us
    pallas_call x1, Pallas kernels, attend_forward(): pl.pallas_call(functools.partial(forward_kernel, cols), out_shape=[jax.Sh...  14.8 us
    pallas_call x1, Pallas kernels, swap(): pl.pallas_call(functools.partial(swap_kernel, cols, count), out_shape=[ja...  14 us
    dot_general x1, matrix products, shards(): hidden = jnp.dot(normed_low, full_in, preferred_element_type=F32) + b_in  11.4 us

profile of v4, /device:TPU:9, one launch (start us, length us, event | category | flops | bytes accessed | tf_op | source)
XLA Modules:
  0.0 325.7 jit_solution(3356461849731807569)
XLA Ops:
  0.7 0.0 copy-start.6
  0.7 84.4 %project.1 = (bf16[8,128,256]{2,1,0:T(8,128)(2,1)}, bf16[16,128,384]{2,1,0:T(8,128)(2,1)}, bf16[768,2304]{1,0:T(8,128)(2,1)}, bf16[768,768]{1,0:T(8,128)(2,1)}, ...) custom-call(bf16[256,768]{1,0:T(8,128)(2,1)} %bitcast.65, ...), custom_call_target="tpu_custom_call" | custom-call | tf_op jit(solution)/shard_map/project/pallas_call | solution.py:879
  85.1 1.1 slice_reduce_fusion.1
  86.2 0.7 slice.55
  87.0 0.0 copy-done.6
  87.0 0.0 copy-start
  87.0 1.4 copy-done
  88.4 1.0 copy-done.2
  89.4 14.8 %attend_forward.1 = (bf16[1024,256]{1,0:T(8,128)(2,1)S(1)}, f32[4,256,256]{2,1,0:T(8,128)S(1)}, f32[4,8,256]{2,1,0:T(8,128)S(1)}) custom-call(s32[2,4]{1,0:T(2,128)S(1)} %copy-done.6, bf16[1024,256]{1,0:T(8,128)(2,1)S(1)} %bitcast.58, bf16[2048,384]{1,0:T(8,128)(2,1)S(1)} %bitcast.55), custom_call_target="tpu_custom_call" | custom-call | tf_op jit(solution)/shard_map/attend_forward/pallas_call | solution.py:550
  104.2 0.0 copy-start.4
  104.2 1.0 copy-done.4
  105.2 14.0 %swap.1 = bf16[8,128,256]{2,1,0:T(8,128)(2,1)S(1)} custom-call(bf16[8,128,256]{2,1,0:T(8,128)(2,1)S(1)} %bitcast.59), custom_call_target="tpu_custom_call" | custom-call | tf_op jit(solution)/shard_map/swap/pallas_call | solution.py:147
  119.2 0.0 copy-done.5
  119.2 0.2 slice.68
  119.4 0.4 copy.37
  119.9 0.0 copy-done.13
  119.9 1.6 fusion.18
  121.5 0.2 multiply_reduce_fusion.3
  121.7 0.0 copy-start.16
  121.7 0.0 slice-start
  121.8 0.2 fusion.12.low
  122.0 0.0 copy-start.11
  122.0 0.0 slice-start.1
  122.0 11.4 %multiply_convert_fusion = (bf16[256,3072]{1,0:T(8,128)(2,1)S(1)}, f32[256,3072]{1,0:T(8,128)}, f32[256,3072]{1,0:T(8,128)}) fusion(f32[3072]{0:T(1024)S(1)} %add.94, bf16[256,768]{1,0:T(8,128)(2,1)S(1)} %fusion.12.low, bf16[768,3072]{1,0:T(8,128)(2,1)} %get-tuple-element.39), kind=kOutput, calls=%fused_computation.5 | convolution fusion | flops 1259864064 | bytes 12988416 | tf_op jit(solution)/shard_map/dot_general | solution.py:1511
  133.3 0.0 copy-done.16
  133.3 0.0 copy-done.11
  133.3 0.0 copy-start.9
  133.4 0.0 slice-done
  133.4 0.0 slice-done.1
  133.4 0.0 copy-start.7
  133.4 1.5 fusion.19
  134.9 0.0 copy-done.9
  134.9 0.2 multiply_reduce_fusion.2
  135.2 0.0 copy-done.7
  135.2 0.4 fusion.11
  135.6 1.7 fusion.16
  137.2 0.1 copy.44
  137.3 0.9 copy.36.att
  138.2 0.7 negate_multiply_fusion.2
  138.9 0.1 convert_reduce_fusion.2
  139.1 6.4 %convert_reduce_fusion = (f32[3072]{0:T(1024)S(1)}, bf16[256,3072]{1,0:T(8,128)(2,1)S(1)}) fusion(f32[256,3072]{1,0:T(8,128)} %get-tuple-element.83, f32[256,3072]{1,0:T(8,128)} %get-tuple-element.87, bf16[256,768]{1,0:T(8,128)(2,1)S(1)} %get-tuple-element.75.gsec, bf16[3072,768]{1,0:T(8,128)(2,1)} %get-tuple-element.40), kind=kOutput, calls=%fused_computation.3 | convolution fusion | flops 1220539392 | bytes 12988416 | tf_op jit(solution)/shard_map/rm,km->rk/dot_general | solution.py:1520
  145.5 0.0 copy-done.12
  145.5 0.0 copy-start.10
  145.5 0.0 copy-start.17
  145.5 4.6 %multiply_reduce_fusion = (f32[768]{0:T(1024)S(1)}, f32[256]{0:T(256)S(1)}, f32[768]{0:T(1024)S(1)}, f32[256,768]{1,0:T(8,128)S(1)}) fusion(f32[256,768]{1,0:T(8,128)S(1)} %get-tuple-element.86, f32[256]{0:T(256)S(1)} %fusion.13, f32[256]{0:T(256)S(1)} %broadcast_multiply_fusion.1, f32[768]{0:T(1024)S(1)} %mul.155, ...), kind=kOutput, calls=%fused_computation.35 | convolution fusion | flops 1209923840 | bytes 8664064 | tf_op jit(solution)/shard_map/rf,mf->rm/dot_general | solution.py:1523
  150.1 0.0 copy-start.14
  150.1 0.0 copy-done.17
  150.1 0.3 fusion.15
  150.5 0.1 convert_reduce_fusion.3
  150.6 0.0 copy-start.8
  150.7 0.1 convert_reduce_fusion.1
  150.8 1.3 concatenate.3.small
  152.1 0.5 convolution_convert_fusion
  152.6 0.2 copy.34
  152.8 0.1 reshape.166
  152.9 0.4 copy.38
  153.2 1.0 pad.4.clone
  154.3 158.6 %reduce_all.1 = (bf16[2,8,48,3456]{3,2,1,0:T(8,128)(2,1)}, bf16[4,4,96,640]{3,2,1,0:T(8,128)(2,1)}, bf16[256,2304]{1,0:T(8,128)(2,1)}, f32[16,384]{1,0:T(8,128)}) custom-call(s32[2,4]{1,0:T(2,128)} %lens.3, bf16[8,768,128]{2,1,0:T(8,128)(2,1)} %get-tuple-element.41.tt, bf16[256,768]{1,0:T(8,128)(2,1)} %copy.36.att, bf16[256,768]{1,0:T(8,128)(2,1)} %copy-done.11, ...), custom_call_target="tpu_custom_call" | custom-call | tf_op jit(solution)/shard_map/reduce_all/pallas_call | solution.py:1400
  312.8 0.0 copy-start.1
  312.8 4.5 %convolution_add_fusion.2 = f32[256,768]{1,0:T(8,128)} fusion(bf16[256,2304]{1,0:T(8,128)(2,1)} %get-tuple-element.44, bf16[768,2304]{1,0:T(8,128)(2,1)} %get-tuple-element.45, f32[256,768]{1,0:T(8,128)S(1)} %get-tuple-element.79, f32[256]{0:T(256)S(1)} %negate_multiply_fusion.1), kind=kOutput, calls=%fused_computation.21 | convolution fusion | flops 906362880 | bytes 6292480 | tf_op jit(solution)/shard_map/rc,mc->rm/dot_general | solution.py:1536
  317.4 1.5 copy-done.3
  318.9 5.5 %widen.1 = (f32[384,2304]{1,0:T(8,128)}, f32[384,768]{1,0:T(8,128)}, f32[384,3072]{1,0:T(8,128)}, f32[4,384,768]{2,1,0:T(8,128)}) custom-call(bf16[2,384,3456]{2,1,0:T(8,128)(2,1)S(1)} %bitcast.56, bf16[4,4,96,640]{3,2,1,0:T(8,128)(2,1)S(1)} %copy-done.3), custom_call_target="tpu_custom_call" | custom-call | tf_op jit(solution)/shard_map/widen/pallas_call | solution.py:1440
  324.4 0.6 slice_reduce_fusion.6
  325.1 0.6 reshape.171
  (36 shorter events, 0.2 us)
Async XLA Ops:
  0.7 86.3 %copy-start.6 = (s32[2,4]{1,0:T(2,128)S(1)}, s32[2,4]{1,0:T(2,128)}, u32[]{:S(2)}) copy-start(s32[2,4]{1,0:T(2,128)} %lens.3) | copy-start | bytes 100
  87.0 1.4 copy-start
  88.4 1.0 copy-start.2
  89.4 30.4 %copy-start.13 = (bf16[768,768]{1,0:T(8,128)(2,1)S(1)}, bf16[768,768]{1,0:T(8,128)(2,1)}, u32[]{:S(2)}) copy-start(bf16[768,768]{1,0:T(8,128)(2,1)} %get-tuple-element.37) | copy-start | bytes 3538948
  104.2 1.0 copy-start.4
  105.2 14.0 %copy-start.5 = (f32[4,8,256]{2,1,0:T(8,128)}, f32[4,8,256]{2,1,0:T(8,128)S(1)}, u32[]{:S(2)}) copy-start(f32[4,8,256]{2,1,0:T(8,128)S(1)} %get-tuple-element.43.lse_ref) | copy-start | bytes 98308
  121.7 11.6 %copy-start.16 = (f32[256]{0:T(256)}, f32[256]{0:T(256)S(1)}, u32[]{:S(2)}) copy-start(f32[256]{0:T(256)S(1)} %multiply_reduce_fusion.3) | copy-start | bytes 3076
  121.7 11.6 %slice-start = ((s8[4718592]{0:T(1024)(128)(4,1)}), s8[4194304]{0:T(1024)(128)(4,1)S(1)}, s32[]{:S(2)}) async-start(s8[4718592]{0:T(1024)(128)(4,1)} %bitcast.69), calls=%async_computation | async-start | bytes 8388608
  122.0 11.4 %copy-start.11 = (bf16[256,768]{1,0:T(8,128)(2,1)}, bf16[256,768]{1,0:T(8,128)(2,1)S(1)}, u32[]{:S(2)}) copy-start(bf16[256,768]{1,0:T(8,128)(2,1)S(1)} %fusion.12.low) | copy-start | bytes 1179652
  122.0 11.4 %slice-start.1 = ((s8[4718592]{0:T(1024)(128)(4,1)}), s8[524288]{0:T(1024)(128)(4,1)S(1)}, s32[]{:S(2)}) async-start(s8[4718592]{0:T(1024)(128)(4,1)} %bitcast.69), calls=%async_computation.1 | async-start | bytes 1048576
  133.3 1.6 copy-start.9
  133.4 1.8 copy-start.7
  139.1 6.4 %copy-start.12 = (bf16[256,768]{1,0:T(8,128)(2,1)}, bf16[256,768]{1,0:T(8,128)(2,1)S(1)}, u32[]{:S(2)}) copy-start(bf16[256,768]{1,0:T(8,128)(2,1)S(1)} %get-tuple-element.75.gsec) | copy-start | bytes 1179652
  145.5 4.6 %copy-start.10 = (bf16[256,3072]{1,0:T(8,128)(2,1)}, bf16[256,3072]{1,0:T(8,128)(2,1)S(1)}, u32[]{:S(2)}) copy-start(bf16[256,3072]{1,0:T(8,128)(2,1)S(1)} %get-tuple-element.73.ghid) | copy-start | bytes 4718596
  145.5 4.6 %copy-start.17 = (f32[256]{0:T(256)S(1)}, f32[256]{0:T(256)}, u32[]{:S(2)}) copy-start(f32[256]{0:T(256)} %copy-done.16) | copy-start | bytes 3076
  150.1 2.0 copy-start.14
  150.6 3.7 %copy-start.8 = (bf16[256,768]{1,0:T(8,128)(2,1)}, bf16[256,768]{1,0:T(8,128)(2,1)S(1)}, u32[]{:S(2)}) copy-start(bf16[256,768]{1,0:T(8,128)(2,1)S(1)} %get-tuple-element.77.gbr) | copy-start | bytes 1179652
  312.8 4.5 %copy-start.1 = (bf16[2,8,48,3456]{3,2,1,0:T(8,128)(2,1)S(1)}, bf16[2,8,48,3456]{3,2,1,0:T(8,128)(2,1)}, u32[]{:S(2)}) copy-start(bf16[2,8,48,3456]{3,2,1,0:T(8,128)(2,1)} %get-tuple-element.46) | copy-start | bytes 15925252
  317.3 1.5 copy-start.3
  318.9 5.6 %copy-start.15 = (f32[16,384]{1,0:T(8,128)S(1)}, f32[16,384]{1,0:T(8,128)}, u32[]{:S(2)}) copy-start(f32[16,384]{1,0:T(8,128)} %get-tuple-element.52) | copy-start | bytes 73732

commit v5 on v4

--- a/solution.py
+++ b/solution.py
@@ -661,8 +661,8 @@
     shards, vectors = refs[:4], refs[4:13]
     q_held, kv_held, f_qkv, f_out, f_in, f_back, vec, turned = refs[13:21]
     own = refs[21:25]
-    whole, acc, q_sent, kv_sent, v_own, token, q_spare, kv_spare, held, held_spare = refs[25:35]
-    flat, (send, recv, here) = refs[35:44], refs[44:]
+    whole, acc, q_sent, kv_sent, v_own, token, q_spare, kv_spare, held = refs[25:34]
+    flat, (send, recv, here) = refs[34:43], refs[43:]
     fulls = (f_qkv, f_out, f_in, f_back)
     a, b, c, f = place(2)
     group = Octet(None)
@@ -738,13 +738,12 @@
     qkv = [Fetch(whole, 0, 0)]
     for cp in flats:
         cp.wait()
-    held_slot = lambda block: held.at[block]
 
     def token_block(dc):
         return token.at[pl.ds(pl.multiple_of(lax.rem(c + dc, 2) * 128, 128), 128)]
 
-    toks = {n: group.send(n, token_block(STEPS[n][1]), held_slot, held_spare) for n in (6, 0, 1, 2, 3, 4, 5)}
-    held[me] = token[pl.ds(pl.multiple_of(c * 128, 128), 128)]
+    toks = [go(token_block(STEPS[n][1]), held.at[m], group.devices[n]) for m, n in enumerate((0, 1, 2, 3, 5))]
+    held[5] = token[pl.ds(pl.multiple_of(c * 128, 128), 128)]
     for n in range(9):
         value = flat[n][...].astype(F32)
         if n == 3:
@@ -771,7 +770,6 @@
     outer = [Fetch(f_back, 3, chunk, chunk) for chunk in range(2)]
     rest = [Fetch(f_out, 1, chunk) for chunk in range(2)]
     inner = [Straight(f_in, 2, chunk, which) for chunk in range(2) for which in range(2)]
-    toks[6] = group.forward(toks[6], held_slot, held_spare)
     qkv[0].third()
     qkv[1].third()
     stores = []
@@ -846,10 +844,10 @@
     third[6] = group.forward(third[6], q_slot, q_spare)
     onward(4)
     onward(6)
-    for cp in toks.values():
+    for cp in toks:
         cp.wait_recv()
 
-    @pl.loop(0, 8)
+    @pl.loop(0, 6)
     def _(n):
         @pl.loop(0, 6)
         def _(m):
@@ -880,14 +878,14 @@
         project_kernel,
         out_shape=[jax.ShapeDtypeStruct((8, 128, 256), BF16), jax.ShapeDtypeStruct((16, 128, 384), BF16)]
         + [jax.ShapeDtypeStruct((2 * s.shape[0], s.shape[1]), BF16) for s in shards]
-        + [jax.ShapeDtypeStruct((2, 16, 384), F32), jax.ShapeDtypeStruct((8, 768, 128), BF16)],
+        + [jax.ShapeDtypeStruct((2, 16, 384), F32), jax.ShapeDtypeStruct((6, 768, 128), BF16)],
         in_specs=[pl.BlockSpec(memory_space=pltpu.HBM)] * 14,
         out_specs=[vmem()] * 2 + [anywhere] * 4 + [vmem()] * 2,
         scratch_shapes=[pltpu.VMEM(s.shape, BF16) for s in shards]
         + [pltpu.VMEM((768, 2304), BF16), pltpu.VMEM((256, 2304), F32), pltpu.VMEM((8, 128, 256), BF16),
            pltpu.VMEM((8, 128, 384), BF16), pltpu.VMEM((16, 384), F32), pltpu.VMEM(tokens.shape, BF16),
            pltpu.VMEM((128, 256), BF16), pltpu.VMEM((128, 384), BF16),
-           pltpu.VMEM((8, 128, 768), BF16), pltpu.VMEM((128, 768), BF16),
+           pltpu.VMEM((6, 128, 768), BF16),
            *[pltpu.VMEM(v.shape, BF16) for v in vectors], DMA((wires,)), DMA((wires,)), DMA((21,))],
         compiler_params=pltpu.CompilerParams(collective_id=ident, has_side_effects=True, vmem_limit_bytes=62 << 20),
         name="project",
@@ -895,8 +893,8 @@
 
 
 BLK = 48
-Z1, X1, Y1 = (0, 1152), (1152, 1920), (1920, 3456)
-L0, L1 = (0, 256), (256, 640)
+Z1, X1, Y1 = (0, 768), (768, 1920), (1920, 3456)
+LATE = (0, 640)
 
 
 class Wires:
@@ -940,12 +938,14 @@
         base += member[1] - member[0]
 
 
-def gradient_kernel(lens, tt, att, low, act, gbr, ghid, gsec, small, do_sent, q_ref, kv_ref, ot_ref, lse_ref,
-                    out, late_out, joined, small_out,
-                    xt, mine, sib, cin, y8, y4, x8, x4, z4, z1r, zyb, zxb,
+def gradient_kernel(lens, wqkv, gfirst, near, far, xt, gbr, ghid, gsec, small, do_sent, q_ref, kv_ref, ot_ref, lse_ref,
+                    out, late_out, igrad, small_out,
+                    joined, wqkv_held, mine, sib, cin, y8, y4, x8, x4, z4, z1r, zyb, zxb,
                     do_held, qm, dm, kt, dk, dv, acc, rowsc, delta, dq_all, dkv_all, dqo, dkvo, xsend, rbuf,
                     l_sib, l_in, l_acc, l_mine, ly, lx,
                     do_spare, dq_spare, dkv_spare, v_own, v_core, v_f, v_b, v_a, send, recv, here):
+    weights = pltpu.make_async_copy(wqkv, wqkv_held, here.at[5])
+    weights.start()
     group = Octet(None)
     a, b, c, f, me = group.a, group.b, group.c, group.f, group.me
     xp, yp, sp = device(a, 1 - b, c, f, 2), device(a, b, c, 1 - f, 2), device(a, b, 1 - c, f, 2)
@@ -962,7 +962,6 @@
     swaps = {n: group.send(n, do_sent.at[group.others[n]], do_slot, do_spare) for n in (6, 0, 1, 2, 3, 4, 5)}
     do_held[me] = do_sent[me]
 
-    transpose_into(xt, act, 1536)
 
     def produce(kind, first, count, part, finish):
         @pl.loop(0, 2 * count)
@@ -970,11 +969,11 @@
             ff, j = lax.rem(n, 2), first + n // 2
             if kind == "out":
                 left, right = xt[pl.ds(pl.multiple_of(ff * 384, 128), 384)], gbr[:, pl.ds(pl.multiple_of(part * 384, 128), 384)]
-                col = 0
+                col = 768
             elif kind == "in":
                 left = xt[pl.ds(pl.multiple_of(768 + ff * 384, 128), 384)]
                 right = ghid[:, pl.ds(pl.multiple_of(part * 1536 + j * 384, 128), 384)]
-                col = pl.multiple_of(384 + j * 384, 128)
+                col = pl.multiple_of(j * 384 + (384 if first else 0), 128)
             else:
                 left = xt[pl.ds(pl.multiple_of(1536 + ff * 1536 + j * 384, 128), 384)]
                 right = gsec[:, pl.ds(pl.multiple_of(part * 384, 128), 384)]
@@ -1231,58 +1230,49 @@
     dq_slot = lambda block: dqo.at[block]
     dqs = {}
 
+    produce("out", 0, 1, 1 - c, keep)
+    produce("in", 2, 2, 1 - c, keep)
+    share(X1)
     produce("back", 0, 4, 1 - c, keep)
     share(Y1)
+    core[X1].wait_recv()
+    produce("out", 0, 1, c, join)
+    produce("in", 2, 2, c, join)
+    x1 = start_x()
     swaps[6] = group.forward(swaps[6], do_slot, do_spare)
-    transpose_into(xt, att, 0)
-    transpose_into(xt, low, 768)
-    produce("out", 0, 1, 1 - c, keep)
-    produce("in", 0, 2, 1 - c, keep)
-    share(Z1)
     core[Y1].wait_recv()
     produce("back", 0, 4, c, join)
     y1 = start_y()
-    core[Z1].wait_recv()
-    produce("out", 0, 1, c, join)
-    produce("in", 0, 2, c, join)
-    z1 = ring_send(Z1, 0, False)
-    produce("in", 2, 2, 1 - c, keep)
-    share(X1)
+    produce("in", 0, 2, 1 - c, keep)
+    share(Z1)
     for cp in swaps.values():
         cp.wait_recv()
     prepare()
-    core[X1].wait_recv()
-    produce("in", 2, 2, c, join)
-    x1 = start_x()
+    core[Z1].wait_recv()
+    produce("in", 0, 2, c, join)
+    z1 = ring_send(Z1, 0, False)
     attend(2, 1 - b)
     cross(FAR)
+    attend(1, 1 - b)
+    cross(NEXT)
     ring_add(Z1, 0, False, z1)
     z1 = ring_send(Z1, 1, False)
-    attend(1, 1 - b)
-    cross(NEXT)
+    attend(3, 1 - b)
+    cross(BACK)
+    attend(0, 1 - b)
+    cross(HERE)
+    x1 = next_x(x1)
     ring_add(Z1, 1, False, z1)
     z1 = ring_send(Z1, 2, False)
-    attend(3, 1 - b)
-    cross(BACK)
-    x1 = next_x(x1)
-    attend(0, 1 - b)
-    cross(HERE)
+    attend(2, b)
+    settle(FAR)
+    attend(1, b)
+    settle(NEXT)
     ring_add(Z1, 2, False, z1)
     z1 = tail_z_y()
-    attend(2, b)
-    settle(FAR)
-    y1 = next_y(y1)
-    attend(1, b)
-    settle(NEXT)
-    last_x(x1)
-    x1 = ring_send(X1, 0, True)
-    z1 = tail_z_x(z1)
     attend(3, b)
     settle(BACK)
-    ring_add(X1, 0, True, x1)
-    x1 = ring_send(X1, 1, True)
-    tail_z_end(z1)
-    g_z1 = early_gather(Z1, "a")
+    y1 = next_y(y1)
     attend(0, b)
 
     @pl.loop(0, 4)
@@ -1297,9 +1287,11 @@
 
     def project_back(n, right):
         rows = pl.ds(pl.multiple_of(n * 96, 32), 96)
-        value = dot(tt[0, rows], right[0], NN)
-        for m in range(1, 8):
-            value = value + dot(tt[m, rows], right[m], NN)
+        value = dot(near[5, rows], right[me], NN)
+        for m, k in enumerate((0, 1, 2, 3, 5)):
+            value = value + dot(near[m, rows], right[group.sources[k]], NN)
+        for m, k in ((0, 4), (1, 6)):
+            value = value + dot(far[m, rows], right[group.sources[k]], NN)
         return value
 
     @pl.loop(0, 4)
@@ -1311,8 +1303,9 @@
         l_acc[n, :, 256:640] = project_back(ours, dkv_all)
 
     late = go(l_sib, l_in, sp)
-    last_y(y1)
-    y1 = ring_send(Y1, 0, True)
+    last_x(x1)
+    x1 = ring_send(X1, 0, True)
+    z1 = tail_z_x(z1)
     dqs[6] = group.forward(dqs[6], dq_slot, dq_spare)
     late.wait_recv()
 
@@ -1321,18 +1314,27 @@
         l_mine[n] = (l_acc[n] + l_in[n].astype(F32)).astype(BF16)
 
     late = go(l_mine.at[pl.ds((1 - f) * 2, 2)], ly, yp)
-    ring_add(X1, 1, True, x1)
-    x1 = ring_send(X1, 2, True)
-    g_z1.second()
-    ring_add(Y1, 0, True, y1)
-    y1 = ring_send(Y1, 1, True)
+    ring_add(X1, 0, True, x1)
+    x1 = ring_send(X1, 1, True)
+    tail_z_end(z1)
     late.wait_recv()
     accumulate(lambda n: l_mine.at[f * 2 + n], lambda n: ly.at[n], 2)
     late = go(l_mine.at[f * 2 + 1 - b], lx, xp)
+    last_y(y1)
+    y1 = ring_send(Y1, 0, True)
+    ring_add(X1, 1, True, x1)
+    x1 = ring_send(X1, 2, True)
+    g_z1 = early_gather(Z1, "a")
+    late.wait_recv()
+    add(lambda n: l_mine.at[f * 2 + b], lambda n: lx)(0)
+    g_l = Gather(l_mine.at[f * 2 + b], late_spot, LATE, "a")
+    ring_add(Y1, 0, True, y1)
+    y1 = ring_send(Y1, 1, True)
     ring_add(X1, 2, True, x1)
-    g_x1 = early_gather(X1, "b")
+    g_x1 = early_gather(X1, "a")
     ring_add(Y1, 1, True, y1)
     y1 = ring_send(Y1, 2, True)
+    g_z1.second()
 
     for cp in list(dqs.values()) + list(dkvs.values()):
         cp.wait_recv()
@@ -1353,34 +1355,34 @@
     v_own[1:2] = jnp.sum(joined[:, 1536:2304].astype(F32), axis=0, keepdims=True)
     vec = go(v_own, v_core, sp)
 
-    late.wait_recv()
-    add(lambda n: l_mine.at[f * 2 + b], lambda n: lx)(0)
-    g_l0 = Gather(l_mine.at[f * 2 + b, :, L0[0]:L0[1]], late_spot, L0, "a")
-    g_l1 = Gather(l_mine.at[f * 2 + b, :, L1[0]:L1[1]], late_spot, L1, "b")
     ring_add(Y1, 2, True, y1)
-    g_y1 = early_gather(Y1, "b")
+    g_y1 = early_gather(Y1, "a")
     vec.wait_recv()
     v_core[...] = v_own[...] + v_core[...]
     vec = go(v_core.at[:, pl.ds(pl.multiple_of((1 - f) * 384, 128), 384)], v_f, yp)
+    g_l.second()
+    g_x1.second()
     g_z1.third()
-    g_x1.second()
-    g_l0.second()
-    g_l1.second()
     vec.wait_recv()
     v_b[b] = v_core[:, pl.ds(pl.multiple_of(f * 384, 128), 384)] + v_f[...]
     vec = go(v_b.at[b], v_b.at[b], xp)
+    weights.wait()
+
+    @pl.loop(0, 3)
+    def _(n):
+        rows = pl.ds(pl.multiple_of(n * 256, 256), 256)
+        igrad[:, rows] = gfirst[:, rows] + dot(joined[...], wqkv_held[rows], NT)
+
     g_y1.second()
+    g_l.third()
+    g_x1.third()
     g_z1.fourth()
-    g_x1.third()
-    g_l0.third()
-    g_l1.third()
     vec.wait_recv()
     v_a[a] = v_b[0] + v_b[1]
     vec = [go(v_a.at[a], v_a.at[a], device(lax.rem(a + k, 4), b, c, f, 2)) for k in range(1, 4)]
     g_y1.third()
+    g_l.fourth()
     g_x1.fourth()
-    g_l0.fourth()
-    g_l1.fourth()
     g_y1.fourth()
     for cp in vec + pending:
         cp.wait_recv()
@@ -1391,7 +1393,7 @@
         cp.wait_send()
 
 
-def reduce_all(lens, tt, att, low, act, gbr, ghid, gsec, small, do_sent, q, kv, ot, lse, ident):
+def reduce_all(lens, wqkv, gfirst, near, far, xt, gbr, ghid, gsec, small, do_sent, q, kv, ot, lse, ident):
     wires = 192
     total = kv.shape[0]
     bf = lambda *shape: pltpu.VMEM(shape, BF16)
@@ -1400,29 +1402,30 @@
     return pl.pallas_call(
         gradient_kernel,
         out_shape=[jax.ShapeDtypeStruct((2, 8, BLK, 3456), BF16), jax.ShapeDtypeStruct((4, 4, 96, 640), BF16),
-                   jax.ShapeDtypeStruct((256, 2304), BF16), jax.ShapeDtypeStruct((16, 384), F32)],
-        in_specs=[pl.BlockSpec(memory_space=pltpu.SMEM)] + [vmem()] * 13, out_specs=[anywhere] * 2 + [vmem()] * 2,
+                   jax.ShapeDtypeStruct((256, 768), F32), jax.ShapeDtypeStruct((16, 384), F32)],
+        in_specs=[pl.BlockSpec(memory_space=pltpu.SMEM), anywhere] + [vmem()] * 13, out_specs=[anywhere] * 2 + [vmem()] * 2,
         scratch_shapes=[
-            bf(4608, 256), bf(4, 4, BLK, 3456), bf(4, 4, BLK, 3456), bf(4, 4, BLK, 3456),
-            bf(2, 4, BLK, 1536), bf(4, BLK, 768), bf(2, 4, BLK, 768), bf(4, BLK, 1536),
-            bf(3, 4, BLK, 1152), bf(3, BLK, 2304), bf(2, BLK, 1152), bf(BLK, 1152),
+            bf(256, 2304), bf(768, 2304), bf(4, 4, BLK, 3456), bf(4, 4, BLK, 3456), bf(4, 4, BLK, 3456),
+            bf(2, 4, BLK, 1536), bf(4, BLK, 1152), bf(2, 4, BLK, 1152), bf(4, BLK, 1536),
+            bf(3, 4, BLK, 768), bf(3, BLK, 2688), bf(2, BLK, 768), bf(BLK, 768),
             bf(8, 128, 256), bf(4, 3, SPAN, 256), bf(4, 3, SPAN, 256), bf(256, total), fl(KB, 256), fl(KB, 256), fl(4, 256, SPAN),
             pltpu.VMEM((4, 8, SPAN), jnp.int32), fl(4, 8, SPAN),
             bf(8, 128, 256), bf(8, 128, 384), bf(8, 128, 256), bf(8, 128, 384), bf(8, 128, 384), bf(8, 128, 384),
             bf(4, 96, 640), bf(4, 96, 640), fl(4, 96, 640), bf(4, 96, 640), bf(2, 96, 640), bf(96, 640),
             bf(128, 256), bf(128, 256), bf(128, 384),
             fl(16, 768), fl(16, 768), fl(16, 384), fl(2, 16, 384), fl(4, 16, 384),
-            DMA((wires,)), DMA((wires,)), DMA((5,))],
+            DMA((wires,)), DMA((wires,)), DMA((6,))],
         compiler_params=pltpu.CompilerParams(collective_id=ident, has_side_effects=True, vmem_limit_bytes=62 << 20),
         name="reduce_all",
-    )(lens, tt, att, low, act, gbr, ghid, gsec, small, do_sent, q, kv, ot, lse)
+    )(lens, wqkv, gfirst, near, far, xt, gbr, ghid, gsec, small, do_sent, q, kv, ot, lse)
 
 
 def widen_kernel(grads, late, g_qkv, g_out, g_in, g_back):
     for core in range(2):
         part = grads.at[core]
-        g_out[:, core * 384:core * 384 + 384] = part[:, 0:384].astype(F32)
-        g_in[:, core * 1536:core * 1536 + 1536] = part[:, 384:1920].astype(F32)
+        g_out[:, core * 384:core * 384 + 384] = part[:, 768:1152].astype(F32)
+        g_in[:, core * 1536:core * 1536 + 768] = part[:, 0:768].astype(F32)
+        g_in[:, core * 1536 + 768:core * 1536 + 1536] = part[:, 1152:1920].astype(F32)
         for j in range(4):
             g_back[j, :, core * 384:core * 384 + 384] = part[:, 1920 + 384 * j:2304 + 384 * j].astype(F32)
     lane = lax.broadcasted_iota(jnp.int32, (96, 384), 1)
@@ -1449,6 +1452,159 @@
     )(grads, late)
 
 
+def middle_kernel(o_sent, tokens, cotangent, w_out, w_in, w_back, vec,
+                  output, gfirst, xt, gbr, ghid, gsec, do_sent, small, far,
+                  o_held, o_spare, f_held, f_spare, v_out, v_in, v_back, normed, xhat1, final, slope, act, send, recv, here):
+    group = Octet(None)
+    a, b, c, f, me = group.a, group.b, group.c, group.f, group.me
+    loads = [pltpu.make_async_copy(s, t, here.at[n]) for n, (s, t) in enumerate(((w_out, v_out), (w_in, v_in), (w_back, v_back)))]
+    for cp in loads:
+        cp.start()
+    meet(group.devices)
+    wires = Wires(send, recv)
+    go = group.go = wires.go
+    o_slot = lambda block: o_held.at[block]
+    swaps = {n: group.send(n, o_sent.at[group.others[n]], o_slot, o_spare) for n in (6, 0, 1, 2, 3, 4, 5)}
+    o_held[me] = o_sent[me]
+    swaps[6] = group.forward(swaps[6], o_slot, o_spare)
+
+    def token_block(dc):
+        return tokens.at[pl.ds(pl.multiple_of(lax.rem(c + dc, 2) * 128, 128), 128)]
+
+    beyond = [go(token_block(dc), f_held.at[dc], group.devices[n]) for dc, n in ((0, 4),)]
+    relayed = go(token_block(1), f_spare, group.relay)
+
+    def row(n):
+        return jnp.concatenate([vec[0, n:n + 1], vec[1, n:n + 1]], axis=1)
+
+    def sums(n, value):
+        small[n:n + 1] = jnp.sum(value, axis=0, keepdims=True)
+
+    for cp in swaps.values():
+        cp.wait_recv()
+    lane = lax.broadcasted_iota(jnp.int32, (128, 384), 1)
+    blank = jnp.zeros((128, 128), F32)
+    att = act
+    for s in range(2):
+        rows = slice(s * 128, s * 128 + 128)
+        for p in range(2):
+            sides = [jnp.concatenate([pltpu.roll(o_held[4 * p + 2 * k + s].astype(F32), 192, 1), blank], axis=1) for k in range(2)]
+            att[rows, 384 * p:384 * p + 384] = pair_columns(sides[0], sides[1], lane, False).astype(BF16)
+    transpose_into(xt, att.at[:, 0:768], 0)
+
+    def norm(value):
+        mean = jnp.sum(value, axis=1, keepdims=True) * (1.0 / 768)
+        centered = value - mean
+        variance = jnp.sum(centered * centered, axis=1, keepdims=True) * (1.0 / 768)
+        inverse = lax.rsqrt(variance + EPSILON)
+        return centered * inverse, inverse
+
+    def norm_back(upstream, gain, hat, inverse):
+        scaled = upstream * gain
+        first = jnp.sum(scaled, axis=1, keepdims=True) * (1.0 / 768)
+        second = jnp.sum(scaled * hat, axis=1, keepdims=True) * (1.0 / 768)
+        return inverse * (scaled - first - hat * second)
+
+    loads[0].wait()
+    hat, inverse1 = norm(tokens[...].astype(F32) + (dot(att[:, 0:768], v_out[...], NN) + row(2)))
+    xhat1[...] = hat
+    value = hat * row(4) + row(5)
+    normed[...] = value
+    output[...] = value.astype(BF16)
+    transpose_into(xt, output, 768)
+    loads[1].wait()
+
+    @pl.loop(0, 4)
+    def _(n):
+        cols = pl.ds(pl.multiple_of(n * 768, 128), 768)
+        ff, j = n // 2, lax.rem(n, 2) * 2
+        bias = jnp.concatenate([vec[ff, pl.ds(8 + j, 1)], vec[ff, pl.ds(9 + j, 1)]], axis=1)
+        hidden = dot(output[...], v_in[:, cols], NN) + bias
+        half = 0.5 * (1.0 + lax.erf(hidden * 0.7071067811865476))
+        slope[:, cols] = half + hidden * (jnp.exp(-0.5 * hidden * hidden) * 0.3989422804014327)
+        act[:, cols] = (hidden * half).astype(BF16)
+
+    relayed.wait_recv()
+    beyond.append(go(f_spare, f_held.at[1], group.beyond))
+    transpose_into(xt, act, 1536)
+    loads[2].wait()
+    final[...] = normed[...] + (dot(act[...], v_back[...], NN) + row(3))
+    hat2, inverse2 = norm(final[...])
+    output[...] = (hat2 * row(6) + row(7)).astype(BF16)
+    upstream = cotangent[...].astype(F32)
+    sums(6, upstream * hat2)
+    sums(7, upstream)
+    gfinal = norm_back(upstream, row(6), hat2, inverse2)
+    final[...] = gfinal
+    gsec[...] = gfinal.astype(BF16)
+    sums(3, gsec[...].astype(F32))
+
+    @pl.loop(0, 4)
+    def _(n):
+        cols = pl.ds(pl.multiple_of(n * 768, 128), 768)
+        ff, j = n // 2, lax.rem(n, 2) * 2
+        value = (dot(gsec[...], v_back[cols], NT) * slope[:, cols]).astype(BF16)
+        ghid[:, cols] = value
+        total = jnp.sum(value.astype(F32), axis=0, keepdims=True)
+        lanes = pl.ds(pl.multiple_of(ff * 384, 128), 384)
+        small[pl.ds(8 + j, 1), lanes] = total[:, :384]
+        small[pl.ds(9 + j, 1), lanes] = total[:, 384:]
+
+    small[0:2] = jnp.zeros((2, 768), F32)
+    small[12:16] = jnp.zeros((4, 768), F32)
+
+    @pl.loop(0, 3)
+    def _(n):
+        cols = pl.ds(pl.multiple_of(n * 256, 128), 256)
+        final[:, cols] = final[:, cols] + dot(ghid[...], v_in[cols], NT)
+
+    hat = xhat1[...]
+    upstream = final[...]
+    sums(4, upstream * hat)
+    sums(5, upstream)
+    value = norm_back(upstream, row(4), hat, inverse1)
+    gfirst[...] = value
+    gbr[...] = value.astype(BF16)
+    sums(2, gbr[...].astype(F32))
+    normed[...] = dot(gbr[...], v_out[...], NT)
+    wide = lax.broadcasted_iota(jnp.int32, (256, 256), 1)
+    for p in range(2):
+        part = normed[:, 384 * p:384 * p + 384]
+        for k in range(2):
+            turned = part if k == 0 else pltpu.roll(part, 192, 1)
+            block = pltpu.roll(jnp.where(wide < 192, turned[:, :256], 0.0), 64, 1).astype(BF16)
+            for s in range(2):
+                do_sent[4 * p + 2 * k + s] = block[128 * s:128 * s + 128]
+    for cp in beyond:
+        cp.wait_recv()
+    for n in range(2):
+        @pl.loop(0, 6)
+        def _(m):
+            lanes = pl.ds(pl.multiple_of(m * 128, 128), 128)
+            far[n, lanes] = f_held[n, :, lanes].astype(F32).T.astype(BF16)
+    for cp in wires.made:
+        cp.wait_send()
+
+
+def middle(o_sent, tokens, cotangent, w_out, w_in, w_back, vec, ident):
+    bf = lambda *shape: pltpu.VMEM(shape, BF16)
+    fl = lambda *shape: pltpu.VMEM(shape, F32)
+    out = lambda d, *shape: jax.ShapeDtypeStruct(shape, d)
+    anywhere = pl.BlockSpec(memory_space=pl.ANY)
+    wires = 16
+    return pl.pallas_call(
+        middle_kernel,
+        out_shape=[out(BF16, 256, 768), out(F32, 256, 768), out(BF16, 4608, 256), out(BF16, 256, 768), out(BF16, 256, 3072),
+                   out(BF16, 256, 768), out(BF16, 8, 128, 256), out(F32, 16, 768), out(BF16, 2, 768, 128)],
+        in_specs=[vmem()] * 3 + [anywhere] * 3 + [vmem()], out_specs=[vmem()] * 9,
+        scratch_shapes=[bf(8, 128, 256), bf(128, 256), bf(2, 128, 768), bf(128, 768), bf(768, 768), bf(768, 3072), bf(3072, 768),
+                        fl(256, 768), fl(256, 768), fl(256, 768), fl(256, 3072), bf(256, 3072),
+                        DMA((wires,)), DMA((wires,)), DMA((3,))],
+        compiler_params=pltpu.CompilerParams(collective_id=ident, has_side_effects=True, vmem_limit_bytes=60 << 20),
+        name="middle",
+    )(o_sent, tokens, cotangent, w_out, w_in, w_back, vec)
+
+
 def layer_norm(values, gain_row, shift_row):
     average = jnp.mean(values, axis=-1, keepdims=True)
     centered = values - average
@@ -1479,29 +1635,34 @@
     inputs = tokens.reshape(micro * per, width)
     cube = nf == 2 and cols == 2
     if cube:
-        q_held, kv_held, full_qkv, full_out, full_in, full_back, sides, turned = project(inputs, (w_qkv, w_out, w_in, w_back), vectors, 1)
-        q_held = q_held.reshape(8 * per, 256)
+        q_held, kv_held, full_qkv, full_out, full_in, full_back, sides, near = project(inputs, (w_qkv, w_out, w_in, w_back), vectors, 1)
         kv_held = kv_held.reshape(-1, 384)
-        b_out, b_back, gain_one, shift_one, gain_two, shift_two = [sides[:, n].reshape(-1) for n in range(2, 8)]
-        b_in = sides[:, 8:12].reshape(-1)
-    else:
-        tiny = jnp.concatenate(vectors).reshape(8, -1)
-        full_qkv, full_out, full_in, full_back, tinies = gather_weights((w_qkv, w_out, w_in, w_back), tiny, nf, cols)
-        tinies = tinies.reshape(nf, -1).astype(F32)
-        named, at = [], 0
-        for vector in vectors:
-            size = vector.shape[0]
-            named.append(tinies[:, at:at + size].reshape(-1))
-            at += size
-        b_query, b_value, b_out, b_in, b_back, gain_one, shift_one, gain_two, shift_two = named
-        joined = jnp.dot(inputs, full_qkv, preferred_element_type=F32)
-        bias = jnp.concatenate([b_query, jnp.zeros_like(b_query), b_value])
-        joined = (joined + bias).astype(BF16)
-        q_sent = by_group(joined[:, :width], micro, 0, 64)
-        kv_sent = jnp.concatenate([by_group(joined[:, width:2 * width], micro, 0, 0), by_group(joined[:, 2 * width:], micro, 0, 0)], axis=2)
-        q_held, kv_held = spread(q_sent, kv_sent, cols, 2)
-        q_held = q_held.reshape(8 * per, 256)
-        kv_held = kv_held.reshape(-1, 384)
+        mixed, mixed_t, log_total = attend_forward(doc_lengths, q_held.reshape(8 * per, 256), kv_held, cols)
+        output, grad_first, xt, grad_branch, grad_hidden, grad_second, do_sent, small, far = middle(
+            mixed.reshape(8, per, 256), inputs, cotangent.reshape(inputs.shape), full_out, full_in, full_back, sides, 3)
+        grads, late, input_grad, sums = reduce_all(
+            doc_lengths, full_qkv, grad_first, near, far, xt, grad_branch, grad_hidden, grad_second, small, do_sent, q_held, kv_held,
+            mixed_t, log_total, 5)
+        g_qkv, g_out, g_in, g_back = widen(grads.reshape(2, share, 3456), late)
+        rows = [sums[0], sums[1], sums[2], sums[8:12].reshape(-1), sums[3], sums[4], sums[5], sums[6], sums[7]]
+        return (output.reshape(tokens.shape), input_grad.reshape(tokens.shape), g_qkv, g_out, g_in, g_back.reshape(4 * share, width)) + tuple(rows)
+    tiny = jnp.concatenate(vectors).reshape(8, -1)
+    full_qkv, full_out, full_in, full_back, tinies = gather_weights((w_qkv, w_out, w_in, w_back), tiny, nf, cols)
+    tinies = tinies.reshape(nf, -1).astype(F32)
+    named, at = [], 0
+    for vector in vectors:
+        size = vector.shape[0]
+        named.append(tinies[:, at:at + size].reshape(-1))
+        at += size
+    b_query, b_value, b_out, b_in, b_back, gain_one, shift_one, gain_two, shift_two = named
+    joined = jnp.dot(inputs, full_qkv, preferred_element_type=F32)
+    bias = jnp.concatenate([b_query, jnp.zeros_like(b_query), b_value])
+    joined = (joined + bias).astype(BF16)
+    q_sent = by_group(joined[:, :width], micro, 0, 64)
+    kv_sent = jnp.concatenate([by_group(joined[:, width:2 * width], micro, 0, 0), by_group(joined[:, 2 * width:], micro, 0, 0)], axis=2)
+    q_held, kv_held = spread(q_sent, kv_sent, cols, 2)
+    q_held = q_held.reshape(8 * per, 256)
+    kv_held = kv_held.reshape(-1, 384)
     mixed, mixed_t, log_total = attend_forward(doc_lengths, q_held, kv_held, cols)
     (back,) = swap([mixed.reshape(8, per, 256)], cols, 3)
     attended = from_group(back, micro, 64)
@@ -1525,18 +1686,7 @@
     grad_branch = grad_first.astype(BF16)
     g_out_bias = jnp.sum(grad_branch.astype(F32), axis=0)
     grad_attended = jnp.einsum("rm,km->rk", grad_branch, full_out, preferred_element_type=F32).astype(BF16)
-    do_sent = by_group(grad_attended, micro, 64, 0)
-    if cube:
-        small = [jnp.zeros((2, width), F32)] + [x[None] for x in (g_out_bias, g_back_bias, g_gain_one, g_shift_one, g_gain_two, g_shift_two)]
-        small += [g_in_bias.reshape(2, 4, share).transpose(1, 0, 2).reshape(4, width), jnp.zeros((4, width), F32)]
-        grads, late, grad_joined, sums = reduce_all(
-            doc_lengths, turned, attended, normed_low, activated, grad_branch, grad_hidden, grad_second, jnp.concatenate(small),
-            do_sent, q_held.reshape(8, per, 256), kv_held, mixed_t, log_total, 5)
-        g_qkv, g_out, g_in, g_back = widen(grads.reshape(2, share, 3456), late)
-        input_grad = grad_first + jnp.einsum("rc,mc->rm", grad_joined, full_qkv, preferred_element_type=F32)
-        rows = [sums[0], sums[1], sums[2], sums[8:12].reshape(-1), sums[3], sums[4], sums[5], sums[6], sums[7]]
-        return (output.reshape(tokens.shape), input_grad.reshape(tokens.shape), g_qkv, g_out, g_in, g_back.reshape(4 * share, width)) + tuple(rows)
-    (do_held,) = swap([do_sent], cols, 4)
+    (do_held,) = swap([by_group(grad_attended, micro, 64, 0)], cols, 4)
     dq, dkv = attend_backward(doc_lengths, q_held, kv_held, do_held.reshape(8 * per, 256), mixed_t, log_total, cols)
     dq_own, dkv_own = collect(dq.reshape(8, per, 256), dkv.reshape(8 * cols, per, 384), cols, 5)
     grad_joined = jnp.concatenate(

time: 328 us -> 297 us (0.905)
  matrix products: 30.4 us -> 0 us
  other arithmetic: 4.11 us -> 0 us
    pallas_call x1, Pallas kernels: 14 us -> 45.4 us  [middle(): pl.pallas_call(middle_kernel, out_shape=[out(BF16, 256, 768), out(F32, 25...]
    dot_general x7 -> x0, matrix products: 30.4 us -> none  [the longest x1 11.4 us: shards(): hidden = jnp.dot(normed_low, full_in, preferred_element_type=F32) + b_in]
    pallas_call x1, Pallas kernels: 84.4 us -> 70.4 us  [project(): pl.pallas_call(project_kernel, out_shape=[jax.ShapeDtypeStruct((8, 128, 2...]
    pallas_call x1, Pallas kernels: 159 us -> 146 us  [reduce_all(): pl.pallas_call(gradient_kernel, out_shape=[jax.ShapeDtypeStruct((2, 8, BL...]
    unnamed x43 -> x22, local copies, waits for them, and re-layouts: 5.87 us -> 10.5 us
where the time goes in v5:
time: 297 us; the launch traced here: 295 us
  Pallas kernels  280 us (94%)
  local copies, waits for them, and re-layouts  13.5 us (5%)
    pallas_call x1, Pallas kernels, reduce_all(): pl.pallas_call(gradient_kernel, out_shape=[jax.ShapeDtypeStruct((2, 8, BL...  146 us
    pallas_call x1, Pallas kernels, project(): pl.pallas_call(project_kernel, out_shape=[jax.ShapeDtypeStruct((8, 128, 2...  70.4 us
    pallas_call x1, Pallas kernels, middle(): pl.pallas_call(middle_kernel, out_shape=[out(BF16, 256, 768), out(F32, 25...  45.4 us
    pallas_call x1, Pallas kernels, attend_forward(): pl.pallas_call(functools.partial(forward_kernel, cols), out_shape=[jax.Sh...  13 us
    unnamed x22, local copies, waits for them, and re-layouts  10.5 us

profile of v5, /device:TPU:9, one launch (start us, length us, event | category | flops | bytes accessed | tf_op | source)
XLA Modules:
  0.0 294.6 jit_solution(2802677871679683458)
XLA Ops:
  0.7 0.0 copy-start.7
  0.7 70.4 %project.1 = (bf16[8,128,256]{2,1,0:T(8,128)(2,1)}, bf16[16,128,384]{2,1,0:T(8,128)(2,1)}, bf16[768,2304]{1,0:T(8,128)(2,1)}, bf16[768,768]{1,0:T(8,128)(2,1)}, ...) custom-call(bf16[256,768]{1,0:T(8,128)(2,1)} %bitcast.14, ...), custom_call_target="tpu_custom_call" | custom-call | tf_op jit(solution)/shard_map/project/pallas_call | solution.py:877
  71.1 0.0 copy-done.7
  71.1 0.0 copy-start
  71.1 1.4 copy-done
  72.5 0.0 copy-start.2
  72.5 1.0 copy-done.2
  73.5 13.0 %attend_forward.1 = (bf16[1024,256]{1,0:T(8,128)(2,1)S(1)}, f32[4,256,256]{2,1,0:T(8,128)S(1)}, f32[4,8,256]{2,1,0:T(8,128)S(1)}) custom-call(s32[2,4]{1,0:T(2,128)S(1)} %copy-done.7, bf16[1024,256]{1,0:T(8,128)(2,1)S(1)} %bitcast.12, bf16[2048,384]{1,0:T(8,128)(2,1)S(1)} %bitcast.10), custom_call_target="tpu_custom_call" | custom-call | tf_op jit(solution)/shard_map/attend_forward/pallas_call | solution.py:550
  86.5 0.0 copy-start.4
  86.5 1.0 copy-done.4
  87.5 0.0 copy-start.5
  87.5 0.8 copy-done.5
  88.3 0.0 copy-start.6
  88.3 0.6 copy-done.6
  88.9 45.4 %middle.1 = (bf16[256,768]{1,0:T(8,128)(2,1)}, f32[256,768]{1,0:T(8,128)}, bf16[4608,256]{1,0:T(8,128)(2,1)}, bf16[256,768]{1,0:T(8,128)(2,1)}, bf16[256,3072]{1...) custom-call(bf16[8,128,256]{2,1,0:T(8,128)(2,1)} %bitcast.13, ...), custom_call_target="tpu_custom_call" | custom-call | tf_op jit(solution)/shard_map/middle/pallas_call | solution.py:1595
  134.3 146.2 %reduce_all.1 = (bf16[2,8,48,3456]{3,2,1,0:T(8,128)(2,1)}, bf16[4,4,96,640]{3,2,1,0:T(8,128)(2,1)}, f32[256,768]{1,0:T(8,128)}, f32[16,384]{1,0:T(8,128)}) custom-call(s32[2,4]{1,0:T(2,128)} %lens.3, bf16[768,2304]{1,0:T(8,128)(2,1)} %get-tuple-element.51.wqkv, f32[256,768]{1,0:T(8,128)} %get-tuple-element.52.gfirst, ...), custom_call_target="tpu_custom_call" | custom-call | tf_op jit(solution)/shard_map/reduce_all/pallas_call | solution.py:1402
  280.5 0.7 slice.30
  281.2 1.6 slice_reduce_fusion
  282.8 0.6 reshape.69
  283.4 0.0 copy-start.1
  283.4 2.5 copy-done.1
  285.9 0.0 copy-start.3
  285.9 1.5 copy-done.3
  287.5 0.0 copy-start.9
  287.5 0.0 copy-start.8
  287.5 5.5 %widen.1 = (f32[384,2304]{1,0:T(8,128)}, f32[384,768]{1,0:T(8,128)}, f32[384,3072]{1,0:T(8,128)}, f32[4,384,768]{2,1,0:T(8,128)}) custom-call(bf16[2,384,3456]{2,1,0:T(8,128)(2,1)S(1)} %bitcast.11, bf16[4,4,96,640]{3,2,1,0:T(8,128)(2,1)S(1)} %copy-done.3), custom_call_target="tpu_custom_call" | custom-call | tf_op jit(solution)/shard_map/widen/pallas_call | solution.py:1443
  293.0 0.0 copy-done.9
  293.0 0.7 copy.33
  293.8 0.0 copy-done.8
  293.8 0.9 copy.34
Async XLA Ops:
  0.7 70.4 %copy-start.7 = (s32[2,4]{1,0:T(2,128)S(1)}, s32[2,4]{1,0:T(2,128)}, u32[]{:S(2)}) copy-start(s32[2,4]{1,0:T(2,128)} %lens.3) | copy-start | bytes 100
  71.1 1.4 copy-start
  72.5 1.0 copy-start.2
  86.5 1.0 copy-start.4
  87.5 0.8 copy-start.5
  88.3 0.6 copy-start.6
  283.4 2.5 copy-start.1
  285.9 1.5 copy-start.3
  287.5 5.6 %copy-start.9 = (bf16[256,768]{1,0:T(8,128)(2,1)S(1)}, bf16[256,768]{1,0:T(8,128)(2,1)}, u32[]{:S(2)}) copy-start(bf16[256,768]{1,0:T(8,128)(2,1)} %get-tuple-element.50) | copy-start | bytes 1179652
  287.5 6.3 %copy-start.8 = (f32[256,768]{1,0:T(8,128)S(1)}, f32[256,768]{1,0:T(8,128)}, u32[]{:S(2)}) copy-start(f32[256,768]{1,0:T(8,128)} %get-tuple-element.63) | copy-start | bytes 2359300

commit v6 on v5

--- a/solution.py
+++ b/solution.py
@@ -554,7 +554,7 @@
         in_specs=[pl.BlockSpec(memory_space=pltpu.SMEM), vmem(), vmem()],
         out_specs=[vmem()] * 3,
         scratch_shapes=[pltpu.VMEM((3, SPAN, 256), BF16), pltpu.VMEM((256, total), BF16), pltpu.VMEM((256, SPAN), F32)],
-        compiler_params=pltpu.CompilerParams(vmem_limit_bytes=32 << 20),
+        compiler_params=pltpu.CompilerParams(vmem_limit_bytes=62 << 20),
         name="attend_forward",
     )(lens, q, kv)
 
@@ -644,25 +644,17 @@
         self.others = [lax.rem(a + da, 4) * 2 + lax.rem(c + dc, 2) for da, dc in STEPS]
         self.sources = [lax.rem(a + 4 - da, 4) * 2 + lax.rem(c + dc, 2) for da, dc in STEPS]
         self.devices = [device(lax.rem(a + da, 4), b, lax.rem(c + dc, 2), f, 2) for da, dc in STEPS]
-        self.relay, self.beyond = self.devices[3], self.devices[1]
-        self.origin = lax.rem(a + 1, 4) * 2 + 1 - c
-
-    def send(self, n, source, target, spare):
-        if n < 6:
-            return self.go(source, target(self.me), self.devices[n])
-        return self.go(source, spare, self.relay)
-
-    def forward(self, copy, target, spare):
-        copy.wait_recv()
-        return self.go(spare, target(self.origin), self.beyond)
+
+    def send(self, n, source, target):
+        return self.go(source, target(self.me), self.devices[n])
 
 
 def project_kernel(tokens, *refs):
     shards, vectors = refs[:4], refs[4:13]
     q_held, kv_held, f_qkv, f_out, f_in, f_back, vec, turned = refs[13:21]
     own = refs[21:25]
-    whole, acc, q_sent, kv_sent, v_own, token, q_spare, kv_spare, held = refs[25:34]
-    flat, (send, recv, here) = refs[34:43], refs[43:]
+    whole, acc, q_sent, kv_sent, v_own, token, held = refs[25:32]
+    flat, (send, recv, here) = refs[32:41], refs[41:]
     fulls = (f_qkv, f_out, f_in, f_back)
     a, b, c, f = place(2)
     group = Octet(None)
@@ -767,7 +759,7 @@
     qkv[0].second()
     qkv.append(Fetch(whole, 0, 1))
     qkv[1].second()
-    outer = [Fetch(f_back, 3, chunk, chunk) for chunk in range(2)]
+    outer = [Fetch(f_back, 3, chunk) for chunk in range(2)]
     rest = [Fetch(f_out, 1, chunk) for chunk in range(2)]
     inner = [Straight(f_in, 2, chunk, which) for chunk in range(2) for which in range(2)]
     qkv[0].third()
@@ -816,14 +808,14 @@
 
     kv_slot = lambda block: kv_held.at[slot(block, b)]
     q_slot = lambda block: q_held.at[block]
-    first = [group.send(n, kv_sent.at[group.others[n]], kv_slot, kv_spare) for n in (6, 0, 1, 2, 3, 4, 5)]
+    first = [group.send(n, kv_sent.at[group.others[n]], kv_slot) for n in (6, 0, 1, 2, 3, 4, 5)]
     first = first[1:] + first[:1]
     own_kv = pltpu.make_async_copy(kv_sent.at[me], kv_held.at[slot(me, b)], here.at[9])
     own_kv.start()
     own_q = pltpu.make_async_copy(q_sent.at[me], q_held.at[me], here.at[10])
     own_q.start()
     crossed = [go(kv_sent.at[me], kv_held.at[slot(me, b)], xp)]
-    third = [group.send(n, q_sent.at[group.others[n]], q_slot, q_spare) for n in (6, 0, 1, 2, 3, 4, 5)]
+    third = [group.send(n, q_sent.at[group.others[n]], q_slot) for n in (6, 0, 1, 2, 3, 4, 5)]
     third = third[1:] + third[:1]
 
     def onward(n):
@@ -834,14 +826,12 @@
     onward(5)
     onward(0)
     onward(1)
-    first[6] = group.forward(first[6], kv_slot, kv_spare)
     for cp in outer:
         cp.second()
     for cp in rest:
         cp.second()
     onward(2)
     onward(3)
-    third[6] = group.forward(third[6], q_slot, q_spare)
     onward(4)
     onward(6)
     for cp in toks:
@@ -884,7 +874,6 @@
         scratch_shapes=[pltpu.VMEM(s.shape, BF16) for s in shards]
         + [pltpu.VMEM((768, 2304), BF16), pltpu.VMEM((256, 2304), F32), pltpu.VMEM((8, 128, 256), BF16),
            pltpu.VMEM((8, 128, 384), BF16), pltpu.VMEM((16, 384), F32), pltpu.VMEM(tokens.shape, BF16),
-           pltpu.VMEM((128, 256), BF16), pltpu.VMEM((128, 384), BF16),
            pltpu.VMEM((6, 128, 768), BF16),
            *[pltpu.VMEM(v.shape, BF16) for v in vectors], DMA((wires,)), DMA((wires,)), DMA((21,))],
         compiler_params=pltpu.CompilerParams(collective_id=ident, has_side_effects=True, vmem_limit_bytes=62 << 20),
@@ -943,7 +932,7 @@
                     joined, wqkv_held, mine, sib, cin, y8, y4, x8, x4, z4, z1r, zyb, zxb,
                     do_held, qm, dm, kt, dk, dv, acc, rowsc, delta, dq_all, dkv_all, dqo, dkvo, xsend, rbuf,
                     l_sib, l_in, l_acc, l_mine, ly, lx,
-                    do_spare, dq_spare, dkv_spare, v_own, v_core, v_f, v_b, v_a, send, recv, here):
+                    v_own, v_core, v_f, v_b, v_a, send, recv, here):
     weights = pltpu.make_async_copy(wqkv, wqkv_held, here.at[5])
     weights.start()
     group = Octet(None)
@@ -959,7 +948,7 @@
     pending = []
 
     do_slot = lambda block: do_held.at[block]
-    swaps = {n: group.send(n, do_sent.at[group.others[n]], do_slot, do_spare) for n in (6, 0, 1, 2, 3, 4, 5)}
+    swaps = {n: group.send(n, do_sent.at[group.others[n]], do_slot) for n in (6, 0, 1, 2, 3, 4, 5)}
     do_held[me] = do_sent[me]
 
 
@@ -1225,7 +1214,7 @@
                 dkvo[me] = value
             else:
                 dkv_all[group.others[n]] = value
-                dkvs[n] = group.send(n, dkv_all.at[group.others[n]], dkv_slot, dkv_spare)
+                dkvs[n] = group.send(n, dkv_all.at[group.others[n]], dkv_slot)
 
     dq_slot = lambda block: dqo.at[block]
     dqs = {}
@@ -1239,7 +1228,6 @@
     produce("out", 0, 1, c, join)
     produce("in", 2, 2, c, join)
     x1 = start_x()
-    swaps[6] = group.forward(swaps[6], do_slot, do_spare)
     core[Y1].wait_recv()
     produce("back", 0, 4, c, join)
     y1 = start_y()
@@ -1266,24 +1254,30 @@
     z1 = ring_send(Z1, 2, False)
     attend(2, b)
     settle(FAR)
+    y1 = next_y(y1)
     attend(1, b)
     settle(NEXT)
     ring_add(Z1, 2, False, z1)
     z1 = tail_z_y()
     attend(3, b)
     settle(BACK)
-    y1 = next_y(y1)
+    last_x(x1)
+    x1 = ring_send(X1, 0, True)
     attend(0, b)
 
     @pl.loop(0, 4)
     def _(stripe):
         dq_all[pl.ds(stripe * 2, 2)] = (acc[stripe] * 0.125).T.astype(BF16).reshape(2, 128, 256)
 
-    for n in (6, 0, 1, 2, 3, 4, 5):
-        dqs[n] = group.send(n, dq_all.at[group.others[n]], dq_slot, dq_spare)
+    def send_dq(*which):
+        for n in which:
+            dqs[n] = group.send(n, dq_all.at[group.others[n]], dq_slot)
+
     dqo[me] = dq_all[me]
     settle(HERE)
-    dkvs[6] = group.forward(dkvs[6], dkv_slot, dkv_spare)
+    z1 = tail_z_x(z1)
+    ring_add(X1, 0, True, x1)
+    x1 = ring_send(X1, 1, True)
 
     def project_back(n, right):
         rows = pl.ds(pl.multiple_of(n * 96, 32), 96)
@@ -1303,38 +1297,39 @@
         l_acc[n, :, 256:640] = project_back(ours, dkv_all)
 
     late = go(l_sib, l_in, sp)
-    last_x(x1)
-    x1 = ring_send(X1, 0, True)
-    z1 = tail_z_x(z1)
-    dqs[6] = group.forward(dqs[6], dq_slot, dq_spare)
-    late.wait_recv()
-
-    @pl.loop(0, 4)
-    def _(n):
-        l_mine[n] = (l_acc[n] + l_in[n].astype(F32)).astype(BF16)
-
-    late = go(l_mine.at[pl.ds((1 - f) * 2, 2)], ly, yp)
-    ring_add(X1, 0, True, x1)
-    x1 = ring_send(X1, 1, True)
-    tail_z_end(z1)
-    late.wait_recv()
-    accumulate(lambda n: l_mine.at[f * 2 + n], lambda n: ly.at[n], 2)
-    late = go(l_mine.at[f * 2 + 1 - b], lx, xp)
+    send_dq(6, 4)
     last_y(y1)
     y1 = ring_send(Y1, 0, True)
     ring_add(X1, 1, True, x1)
     x1 = ring_send(X1, 2, True)
+    send_dq(0, 2)
+    late.wait_recv()
+
+    @pl.loop(0, 4)
+    def _(n):
+        l_mine[n] = (l_acc[n] + l_in[n].astype(F32)).astype(BF16)
+
+    late = go(l_mine.at[pl.ds((1 - f) * 2, 2)], ly, yp)
+    tail_z_end(z1)
     g_z1 = early_gather(Z1, "a")
+    ring_add(Y1, 0, True, y1)
+    y1 = ring_send(Y1, 1, True)
+    send_dq(1, 3)
+    late.wait_recv()
+    accumulate(lambda n: l_mine.at[f * 2 + n], lambda n: ly.at[n], 2)
+    late = go(l_mine.at[f * 2 + 1 - b], lx, xp)
+    ring_add(X1, 2, True, x1)
+    g_x1 = early_gather(X1, "a")
+    send_dq(5)
+    ring_add(Y1, 1, True, y1)
+    y1 = ring_send(Y1, 2, True)
     late.wait_recv()
     add(lambda n: l_mine.at[f * 2 + b], lambda n: lx)(0)
     g_l = Gather(l_mine.at[f * 2 + b], late_spot, LATE, "a")
-    ring_add(Y1, 0, True, y1)
-    y1 = ring_send(Y1, 1, True)
-    ring_add(X1, 2, True, x1)
-    g_x1 = early_gather(X1, "a")
-    ring_add(Y1, 1, True, y1)
-    y1 = ring_send(Y1, 2, True)
     g_z1.second()
+    g_x1.second()
+    ring_add(Y1, 2, True, y1)
+    g_y1 = early_gather(Y1, "a")
 
     for cp in list(dqs.values()) + list(dkvs.values()):
         cp.wait_recv()
@@ -1355,14 +1350,12 @@
     v_own[1:2] = jnp.sum(joined[:, 1536:2304].astype(F32), axis=0, keepdims=True)
     vec = go(v_own, v_core, sp)
 
-    ring_add(Y1, 2, True, y1)
-    g_y1 = early_gather(Y1, "a")
+    g_l.second()
     vec.wait_recv()
     v_core[...] = v_own[...] + v_core[...]
     vec = go(v_core.at[:, pl.ds(pl.multiple_of((1 - f) * 384, 128), 384)], v_f, yp)
-    g_l.second()
-    g_x1.second()
     g_z1.third()
+    g_x1.third()
     vec.wait_recv()
     v_b[b] = v_core[:, pl.ds(pl.multiple_of(f * 384, 128), 384)] + v_f[...]
     vec = go(v_b.at[b], v_b.at[b], xp)
@@ -1375,14 +1368,13 @@
 
     g_y1.second()
     g_l.third()
-    g_x1.third()
     g_z1.fourth()
+    g_x1.fourth()
     vec.wait_recv()
     v_a[a] = v_b[0] + v_b[1]
     vec = [go(v_a.at[a], v_a.at[a], device(lax.rem(a + k, 4), b, c, f, 2)) for k in range(1, 4)]
     g_y1.third()
     g_l.fourth()
-    g_x1.fourth()
     g_y1.fourth()
     for cp in vec + pending:
         cp.wait_recv()
@@ -1412,7 +1404,6 @@
             pltpu.VMEM((4, 8, SPAN), jnp.int32), fl(4, 8, SPAN),
             bf(8, 128, 256), bf(8, 128, 384), bf(8, 128, 256), bf(8, 128, 384), bf(8, 128, 384), bf(8, 128, 384),
             bf(4, 96, 640), bf(4, 96, 640), fl(4, 96, 640), bf(4, 96, 640), bf(2, 96, 640), bf(96, 640),
-            bf(128, 256), bf(128, 256), bf(128, 384),
             fl(16, 768), fl(16, 768), fl(16, 384), fl(2, 16, 384), fl(4, 16, 384),
             DMA((wires,)), DMA((wires,)), DMA((6,))],
         compiler_params=pltpu.CompilerParams(collective_id=ident, has_side_effects=True, vmem_limit_bytes=62 << 20),
@@ -1420,7 +1411,7 @@
     )(lens, wqkv, gfirst, near, far, xt, gbr, ghid, gsec, small, do_sent, q, kv, ot, lse)
 
 
-def widen_kernel(grads, late, g_qkv, g_out, g_in, g_back):
+def widen_kernel(grads, late, low, igrad, sums, g_qkv, g_out, g_in, g_back, low_out, igrad_out, *vectors):
     for core in range(2):
         part = grads.at[core]
         g_out[:, core * 384:core * 384 + 384] = part[:, 768:1152].astype(F32)
@@ -1435,26 +1426,44 @@
         ke, ko = even[:, 256:], odd[:, 256:]
         g_qkv[:, 768 + 384 * p:1152 + 384 * p] = pair_columns(ke, ko, lane, False)
         g_qkv[:, 1536 + 384 * p:1920 + 384 * p] = pair_columns(ke, ko, lane, True)
-
-
-def widen(grads, late):
+    low_out[...] = low[...]
+    igrad_out[...] = igrad[...]
+
+    @pl.when(pl.program_id(0) == 0)
+    def _():
+        for n, ref in enumerate(vectors):
+            if n == 3:
+                for j in range(4):
+                    ref[384 * j:384 * j + 384] = sums[8 + j:9 + j].reshape(384)
+            else:
+                row = n if n < 3 else n - 1
+                ref[...] = sums[row:row + 1].reshape(384)
+
+
+def widen(grads, late, low, igrad, sums):
     rows, step = 384, 96
-    spec = lambda wide: pl.BlockSpec((step, wide), lambda n: (n, 0))
+    spec = lambda tall, wide: pl.BlockSpec((tall, wide), lambda n: (n, 0))
+    flat = lambda size: pl.BlockSpec((size,), lambda n: (0,))
+    sizes = [384] * 3 + [1536] + [384] * 5
     return pl.pallas_call(
         widen_kernel,
         grid=(rows // step,),
         out_shape=[jax.ShapeDtypeStruct((rows, 2304), F32), jax.ShapeDtypeStruct((rows, 768), F32),
-                   jax.ShapeDtypeStruct((rows, 3072), F32), jax.ShapeDtypeStruct((4, rows, 768), F32)],
-        in_specs=[pl.BlockSpec((2, step, 3456), lambda n: (0, n, 0)), pl.BlockSpec((4, 1, step, 640), lambda n: (0, n, 0, 0))],
-        out_specs=[spec(2304), spec(768), spec(3072), pl.BlockSpec((4, step, 768), lambda n: (0, n, 0))],
-        compiler_params=pltpu.CompilerParams(vmem_limit_bytes=40 << 20),
+                   jax.ShapeDtypeStruct((rows, 3072), F32), jax.ShapeDtypeStruct((4, rows, 768), F32),
+                   jax.ShapeDtypeStruct(low.shape, BF16), jax.ShapeDtypeStruct(igrad.shape, F32)]
+        + [jax.ShapeDtypeStruct((size,), F32) for size in sizes],
+        in_specs=[pl.BlockSpec((2, step, 3456), lambda n: (0, n, 0)), pl.BlockSpec((4, 1, step, 640), lambda n: (0, n, 0, 0)),
+                  spec(64, 768), spec(64, 768), pl.BlockSpec((16, 384), lambda n: (0, 0))],
+        out_specs=[spec(step, 2304), spec(step, 768), spec(step, 3072), pl.BlockSpec((4, step, 768), lambda n: (0, n, 0)),
+                   spec(64, 768), spec(64, 768)] + [flat(size) for size in sizes],
+        compiler_params=pltpu.CompilerParams(vmem_limit_bytes=62 << 20),
         name="widen",
-    )(grads, late)
+    )(grads, late, low, igrad, sums)
 
 
 def middle_kernel(o_sent, tokens, cotangent, w_out, w_in, w_back, vec,
                   output, gfirst, xt, gbr, ghid, gsec, do_sent, small, far,
-                  o_held, o_spare, f_held, f_spare, v_out, v_in, v_back, normed, xhat1, final, slope, act, send, recv, here):
+                  o_held, f_held, v_out, v_in, v_back, normed, xhat1, final, slope, act, send, recv, here):
     group = Octet(None)
     a, b, c, f, me = group.a, group.b, group.c, group.f, group.me
     loads = [pltpu.make_async_copy(s, t, here.at[n]) for n, (s, t) in enumerate(((w_out, v_out), (w_in, v_in), (w_back, v_back)))]
@@ -1464,15 +1473,13 @@
     wires = Wires(send, recv)
     go = group.go = wires.go
     o_slot = lambda block: o_held.at[block]
-    swaps = {n: group.send(n, o_sent.at[group.others[n]], o_slot, o_spare) for n in (6, 0, 1, 2, 3, 4, 5)}
+    swaps = {n: group.send(n, o_sent.at[group.others[n]], o_slot) for n in (6, 0, 1, 2, 3, 4, 5)}
     o_held[me] = o_sent[me]
-    swaps[6] = group.forward(swaps[6], o_slot, o_spare)
 
     def token_block(dc):
         return tokens.at[pl.ds(pl.multiple_of(lax.rem(c + dc, 2) * 128, 128), 128)]
 
-    beyond = [go(token_block(dc), f_held.at[dc], group.devices[n]) for dc, n in ((0, 4),)]
-    relayed = go(token_block(1), f_spare, group.relay)
+    beyond = [go(token_block(dc), f_held.at[dc], group.devices[n]) for dc, n in ((0, 4), (1, 6))]
 
     def row(n):
         return jnp.concatenate([vec[0, n:n + 1], vec[1, n:n + 1]], axis=1)
@@ -1524,8 +1531,6 @@
         slope[:, cols] = half + hidden * (jnp.exp(-0.5 * hidden * hidden) * 0.3989422804014327)
         act[:, cols] = (hidden * half).astype(BF16)
 
-    relayed.wait_recv()
-    beyond.append(go(f_spare, f_held.at[1], group.beyond))
     transpose_into(xt, act, 1536)
     loads[2].wait()
     final[...] = normed[...] + (dot(act[...], v_back[...], NN) + row(3))
@@ -1597,7 +1602,7 @@
         out_shape=[out(BF16, 256, 768), out(F32, 256, 768), out(BF16, 4608, 256), out(BF16, 256, 768), out(BF16, 256, 3072),
                    out(BF16, 256, 768), out(BF16, 8, 128, 256), out(F32, 16, 768), out(BF16, 2, 768, 128)],
         in_specs=[vmem()] * 3 + [anywhere] * 3 + [vmem()], out_specs=[vmem()] * 9,
-        scratch_shapes=[bf(8, 128, 256), bf(128, 256), bf(2, 128, 768), bf(128, 768), bf(768, 768), bf(768, 3072), bf(3072, 768),
+        scratch_shapes=[bf(8, 128, 256), bf(2, 128, 768), bf(768, 768), bf(768, 3072), bf(3072, 768),
                         fl(256, 768), fl(256, 768), fl(256, 768), fl(256, 3072), bf(256, 3072),
                         DMA((wires,)), DMA((wires,)), DMA((3,))],
         compiler_params=pltpu.CompilerParams(collective_id=ident, has_side_effects=True, vmem_limit_bytes=60 << 20),
@@ -1643,8 +1648,7 @@
         grads, late, input_grad, sums = reduce_all(
             doc_lengths, full_qkv, grad_first, near, far, xt, grad_branch, grad_hidden, grad_second, small, do_sent, q_held, kv_held,
             mixed_t, log_total, 5)
-        g_qkv, g_out, g_in, g_back = widen(grads.reshape(2, share, 3456), late)
-        rows = [sums[0], sums[1], sums[2], sums[8:12].reshape(-1), sums[3], sums[4], sums[5], sums[6], sums[7]]
+        g_qkv, g_out, g_in, g_back, output, input_grad, *rows = widen(grads.reshape(2, share, 3456), late, output, input_grad, sums)
         return (output.reshape(tokens.shape), input_grad.reshape(tokens.shape), g_qkv, g_out, g_in, g_back.reshape(4 * share, width)) + tuple(rows)
     tiny = jnp.concatenate(vectors).reshape(8, -1)
     full_qkv, full_out, full_in, full_back, tinies = gather_weights((w_qkv, w_out, w_in, w_back), tiny, nf, cols)

time: 297 us -> 279 us (0.939)
  local copies, waits for them, and re-layouts: 13.5 us -> 0 us
  Pallas kernels: 280 us -> 276 us
    unnamed x22 -> x0, local copies, waits for them, and re-layouts: 10.5 us -> none
    pallas_call x1, Pallas kernels: 146 us -> 141 us  [reduce_all(): pl.pallas_call(gradient_kernel, out_shape=[jax.ShapeDtypeStruct((2, 8, BL...]
    pallas_call x1, Pallas kernels: 5.55 us -> 9.6 us  [widen(): pl.pallas_call(widen_kernel, grid=(rows // step,), out_shape=[jax.ShapeDt...]
    pallas_call x1, Pallas kernels: 13 us -> 16.9 us  [attend_forward(): pl.pallas_call(functools.partial(forward_kernel, cols), out_shape=[jax.Sh...]
    pallas_call x1, Pallas kernels: 45.4 us -> 41.8 us  [middle(): pl.pallas_call(middle_kernel, out_shape=[out(BF16, 256, 768), out(F32, 25...]
    pallas_call x1, Pallas kernels: 70.4 us -> 67.3 us  [project(): pl.pallas_call(project_kernel, out_shape=[jax.ShapeDtypeStruct((8, 128, 2...]
where the time goes in v6:
time: 279 us; the launch traced here: 277 us
  Pallas kernels  276 us (99%)
    pallas_call x1, Pallas kernels, reduce_all(): pl.pallas_call(gradient_kernel, out_shape=[jax.ShapeDtypeStruct((2, 8, BL...  141 us
    pallas_call x1, Pallas kernels, project(): pl.pallas_call(project_kernel, out_shape=[jax.ShapeDtypeStruct((8, 128, 2...  67.3 us
    pallas_call x1, Pallas kernels, middle(): pl.pallas_call(middle_kernel, out_shape=[out(BF16, 256, 768), out(F32, 25...  41.8 us
    pallas_call x1, Pallas kernels, attend_forward(): pl.pallas_call(functools.partial(forward_kernel, cols), out_shape=[jax.Sh...  16.9 us
    pallas_call x1, Pallas kernels, widen(): pl.pallas_call(widen_kernel, grid=(rows // step,), out_shape=[jax.ShapeDt...  9.6 us

profile of v6, /device:TPU:9, one launch (start us, length us, event | category | flops | bytes accessed | tf_op | source)
XLA Modules:
  0.0 276.9 jit_solution(6879549373536298918)
XLA Ops:
  0.7 67.3 %project.1 = (bf16[8,128,256]{2,1,0:T(8,128)(2,1)}, bf16[16,128,384]{2,1,0:T(8,128)(2,1)}, bf16[768,2304]{1,0:T(8,128)(2,1)}, bf16[768,768]{1,0:T(8,128)(2,1)}, ...) custom-call(bf16[256,768]{1,0:T(8,128)(2,1)} %bitcast.13, ...), custom_call_target="tpu_custom_call" | custom-call | tf_op jit(solution)/shard_map/project/pallas_call | solution.py:867
  67.9 16.9 %attend_forward.1 = (bf16[1024,256]{1,0:T(8,128)(2,1)}, f32[4,256,256]{2,1,0:T(8,128)}, f32[4,8,256]{2,1,0:T(8,128)}) custom-call(s32[2,4]{1,0:T(2,128)} %lens.3, bf16[1024,256]{1,0:T(8,128)(2,1)} %bitcast.12, bf16[2048,384]{1,0:T(8,128)(2,1)} %bitcast.9), custom_call_target="tpu_custom_call" | custom-call | tf_op jit(solution)/shard_map/attend_forward/pallas_call | solution.py:550
  84.8 41.8 %middle.1 = (bf16[256,768]{1,0:T(8,128)(2,1)}, f32[256,768]{1,0:T(8,128)}, bf16[4608,256]{1,0:T(8,128)(2,1)}, bf16[256,768]{1,0:T(8,128)(2,1)}, bf16[256,3072]{1...) custom-call(bf16[8,128,256]{2,1,0:T(8,128)(2,1)} %bitcast.15, ...), custom_call_target="tpu_custom_call" | custom-call | tf_op jit(solution)/shard_map/middle/pallas_call | solution.py:1600
  126.7 140.5 %reduce_all.1 = (bf16[2,8,48,3456]{3,2,1,0:T(8,128)(2,1)}, bf16[4,4,96,640]{3,2,1,0:T(8,128)(2,1)}, f32[256,768]{1,0:T(8,128)}, f32[16,384]{1,0:T(8,128)}) custom-call(s32[2,4]{1,0:T(2,128)} %lens.3, bf16[768,2304]{1,0:T(8,128)(2,1)} %get-tuple-element.54.wqkv, f32[256,768]{1,0:T(8,128)} %get-tuple-element.62.gfirst, ...), custom_call_target="tpu_custom_call" | custom-call | tf_op jit(solution)/shard_map/reduce_all/pallas_call | solution.py:1394
  267.2 9.6 %widen.1 = (f32[384,2304]{1,0:T(8,128)}, f32[384,768]{1,0:T(8,128)}, f32[384,3072]{1,0:T(8,128)}, f32[4,384,768]{2,1,0:T(8,128)}, bf16[256,768]{1,0:T(8,128)(2,1...) custom-call(bf16[2,384,3456]{2,1,0:T(8,128)(2,1)} %bitcast.11, ...), custom_call_target="tpu_custom_call" | custom-call | tf_op jit(solution)/shard_map/widen/pallas_call | solution.py:1448

commit v7 on v6

--- a/solution.py
+++ b/solution.py
@@ -491,7 +491,7 @@
     lane = lax.broadcasted_iota(jnp.int32, shape, 1)
     return (lane - shift) // 64
 
-def forward_kernel(cols, lens, q_ref, kv_ref, o_ref, ot_ref, lse_ref, qm, vt, acc):
+def forward_kernel(cols, packed, lens, q_ref, kv_ref, o_ref, ot_ref, lse_ref, qm, vt, acc):
     index = lax.axis_index("ctx")
     b, c = lax.rem(index // 2, cols), lax.rem(index, 2)
     ends = bounds(lens, c)
@@ -507,7 +507,10 @@
         base = SPAN * (stripe * cols + b)
         rows = pl.ds(pl.multiple_of(stripe * SPAN, SPAN), SPAN)
         head = lane_head((SPAN, 256), 0)
-        q = q_ref[rows].astype(F32) * 0.125
+        if packed:
+            q = jnp.concatenate([unpack(q_ref[stripe * 2 + i].astype(F32), 0) for i in range(2)], axis=0) * 0.125
+        else:
+            q = q_ref[rows].astype(F32) * 0.125
         for h in range(3):
             qm[h] = jnp.where(head == h, q, 0.0).astype(BF16)
         qpos = base + lax.broadcasted_iota(jnp.int32, (1, SPAN), 1)
@@ -540,15 +543,20 @@
             acc[hrows] = acc[hrows] * (1.0 / tot)
             lse_ref[stripe, pl.ds(h, 1)] = top + jnp.log(tot)
         ot_ref[stripe] = acc[...]
-        o_ref[rows] = acc[...].T.astype(BF16)
+        value = acc[...].T
+        if packed:
+            for i in range(2):
+                o_ref[stripe * 2 + i] = pack(value[128 * i:128 * i + 128], 64).astype(BF16)
+        else:
+            o_ref[rows] = value.astype(BF16)
 
 def vmem():
     return pl.BlockSpec(memory_space=pltpu.VMEM)
 
-def attend_forward(lens, q, kv, cols):
+def attend_forward(lens, q, kv, cols, packed=False):
     total = kv.shape[0]
     return pl.pallas_call(
-        functools.partial(forward_kernel, cols),
+        functools.partial(forward_kernel, cols, packed),
         out_shape=[jax.ShapeDtypeStruct(q.shape, BF16), jax.ShapeDtypeStruct((4, 256, SPAN), F32),
                    jax.ShapeDtypeStruct((4, 8, SPAN), F32)],
         in_specs=[pl.BlockSpec(memory_space=pltpu.SMEM), vmem(), vmem()],
@@ -631,6 +639,30 @@
         compiler_params=pltpu.CompilerParams(vmem_limit_bytes=40 << 20),
         name="attend_backward",
     )(lens, q, kv, do, ot, lse)
+
+
+def pack(block, base):
+    free = 0 if base else 192
+    lane = lax.broadcasted_iota(jnp.int32, (32, 256), 1)
+    tail = block[96:128]
+    rows = []
+    for k in range(3):
+        moved = pltpu.roll(tail, (free - base - 64 * k) % 256, 1)
+        rows.append(jnp.where((lane >= free) & (lane < free + 64), moved, block[32 * k:32 * k + 32]))
+    return jnp.concatenate(rows, axis=0)
+
+
+def unpack(packed, base):
+    free = 0 if base else 192
+    lane = lax.broadcasted_iota(jnp.int32, (32, 256), 1)
+    tail = jnp.zeros((32, 256), F32)
+    rows = []
+    for k in range(3):
+        part = packed[32 * k:32 * k + 32]
+        rows.append(jnp.where((lane >= free) & (lane < free + 64), 0.0, part))
+        spot = base + 64 * k
+        tail = jnp.where((lane >= spot) & (lane < spot + 64), pltpu.roll(part, (spot - free) % 256, 1), tail)
+    return jnp.concatenate(rows + [tail], axis=0)
 
 
 STEPS = ((1, 0), (3, 0), (1, 1), (3, 1), (2, 0), (0, 1), (2, 1))
@@ -796,12 +828,11 @@
         even = jnp.where(lane < 192, k, turned_v).astype(BF16)
         odd = jnp.where(lane < 192, turned_k, v).astype(BF16)
         q = column(p)
-        q_even = jnp.where(lane < 192, q, 0.0)[:, :256].astype(BF16)
-        q_odd = jnp.where(lane < 192, pltpu.roll(q, 192, 1), 0.0)[:, :256].astype(BF16)
+        q_even, q_odd = q[:, :256], pltpu.roll(q, 192, 1)[:, :256]
         for s in range(2):
             rows = slice(128 * s, 128 * s + 128)
             kv_sent[4 * p + s], kv_sent[4 * p + 2 + s] = even[rows], odd[rows]
-            q_sent[4 * p + s], q_sent[4 * p + 2 + s] = q_even[rows], q_odd[rows]
+            q_sent[4 * p + s], q_sent[4 * p + 2 + s] = pack(q_even[rows], 0).astype(BF16), pack(q_odd[rows], 0).astype(BF16)
 
     def slot(block, bb):
         return (block // 2 * 2 + bb) * 2 + lax.rem(block, 2)
@@ -866,13 +897,13 @@
     wires = 80
     return pl.pallas_call(
         project_kernel,
-        out_shape=[jax.ShapeDtypeStruct((8, 128, 256), BF16), jax.ShapeDtypeStruct((16, 128, 384), BF16)]
+        out_shape=[jax.ShapeDtypeStruct((8, 96, 256), BF16), jax.ShapeDtypeStruct((16, 128, 384), BF16)]
         + [jax.ShapeDtypeStruct((2 * s.shape[0], s.shape[1]), BF16) for s in shards]
         + [jax.ShapeDtypeStruct((2, 16, 384), F32), jax.ShapeDtypeStruct((6, 768, 128), BF16)],
         in_specs=[pl.BlockSpec(memory_space=pltpu.HBM)] * 14,
         out_specs=[vmem()] * 2 + [anywhere] * 4 + [vmem()] * 2,
         scratch_shapes=[pltpu.VMEM(s.shape, BF16) for s in shards]
-        + [pltpu.VMEM((768, 2304), BF16), pltpu.VMEM((256, 2304), F32), pltpu.VMEM((8, 128, 256), BF16),
+        + [pltpu.VMEM((768, 2304), BF16), pltpu.VMEM((256, 2304), F32), pltpu.VMEM((8, 96, 256), BF16),
            pltpu.VMEM((8, 128, 384), BF16), pltpu.VMEM((16, 384), F32), pltpu.VMEM(tokens.shape, BF16),
            pltpu.VMEM((6, 128, 768), BF16),
            *[pltpu.VMEM(v.shape, BF16) for v in vectors], DMA((wires,)), DMA((wires,)), DMA((21,))],
@@ -927,14 +958,16 @@
         base += member[1] - member[0]
 
 
-def gradient_kernel(lens, wqkv, gfirst, near, far, xt, gbr, ghid, gsec, small, do_sent, q_ref, kv_ref, ot_ref, lse_ref,
+def gradient_kernel(lens, wqkv, gfirst_hbm, near_hbm, far_hbm, q_hbm, kv_hbm, ot_hbm, xt, gbr, ghid, gsec, small, do_sent, lse_ref,
                     out, late_out, igrad, small_out,
-                    joined, wqkv_held, mine, sib, cin, y8, y4, x8, x4, z4, z1r, zyb, zxb,
-                    do_held, qm, dm, kt, dk, dv, acc, rowsc, delta, dq_all, dkv_all, dqo, dkvo, xsend, rbuf,
+                    joined, wqkv_held, gfirst, near, far, q_held, kv_ref, ot_ref, mine, sib, cin, y8, y4, x8, x4, z4, z1r, zyb, zxb,
+                    do_held, qm, dm, kt, dk, dv, acc, rowsc, delta, dq_sent, dq_all, dkv_all, dqo, dkvo, xsend, rbuf,
                     l_sib, l_in, l_acc, l_mine, ly, lx,
                     v_own, v_core, v_f, v_b, v_a, send, recv, here):
-    weights = pltpu.make_async_copy(wqkv, wqkv_held, here.at[5])
-    weights.start()
+    inputs = [pltpu.make_async_copy(s, t, here.at[5 + n]) for n, (s, t) in enumerate(
+        ((kv_hbm, kv_ref), (q_hbm, q_held), (ot_hbm, ot_ref), (near_hbm, near), (far_hbm, far), (gfirst_hbm, gfirst), (wqkv, wqkv_held)))]
+    for cp in inputs:
+        cp.start()
     group = Octet(None)
     a, b, c, f, me = group.a, group.b, group.c, group.f, group.me
     xp, yp, sp = device(a, 1 - b, c, f, 2), device(a, b, c, 1 - f, 2), device(a, b, 1 - c, f, 2)
@@ -1141,8 +1174,8 @@
         def _(stripe):
             head = lane_head((SPAN, 256), 0)
             headv = lane_head((SPAN, 256), 64)
-            q = q_ref[pl.ds(stripe * 2, 2)].reshape(SPAN, 256).astype(F32) * 0.125
-            grad = do_held[pl.ds(stripe * 2, 2)].reshape(SPAN, 256).astype(F32)
+            q = jnp.concatenate([unpack(q_held[stripe * 2 + i].astype(F32), 0) for i in range(2)], axis=0) * 0.125
+            grad = jnp.concatenate([unpack(do_held[stripe * 2 + i].astype(F32), 64) for i in range(2)], axis=0)
             for h in range(3):
                 qm[stripe, h] = jnp.where(head == h, q, 0.0).astype(BF16)
                 dm[stripe, h] = jnp.where(headv == h, grad, 0.0).astype(BF16)
@@ -1235,6 +1268,8 @@
     share(Z1)
     for cp in swaps.values():
         cp.wait_recv()
+    for cp in inputs[:3]:
+        cp.wait()
     prepare()
     core[Z1].wait_recv()
     produce("in", 0, 2, c, join)
@@ -1267,13 +1302,16 @@
 
     @pl.loop(0, 4)
     def _(stripe):
-        dq_all[pl.ds(stripe * 2, 2)] = (acc[stripe] * 0.125).T.astype(BF16).reshape(2, 128, 256)
+        value = (acc[stripe] * 0.125).T
+        dq_all[pl.ds(stripe * 2, 2)] = value.astype(BF16).reshape(2, 128, 256)
+        for i in range(2):
+            dq_sent[stripe * 2 + i] = pack(value[128 * i:128 * i + 128], 0).astype(BF16)
 
     def send_dq(*which):
         for n in which:
-            dqs[n] = group.send(n, dq_all.at[group.others[n]], dq_slot)
-
-    dqo[me] = dq_all[me]
+            dqs[n] = group.send(n, dq_sent.at[group.others[n]], dq_slot)
+
+    dqo[me] = dq_sent[me]
     settle(HERE)
     z1 = tail_z_x(z1)
     ring_add(X1, 0, True, x1)
@@ -1287,6 +1325,9 @@
         for m, k in ((0, 4), (1, 6)):
             value = value + dot(far[m, rows], right[group.sources[k]], NN)
         return value
+
+    for cp in inputs[3:]:
+        cp.wait()
 
     @pl.loop(0, 4)
     def _(n):
@@ -1339,8 +1380,8 @@
         for p in range(2):
             even, odd = 4 * p + s, 4 * p + 2 + s
             blank = jnp.zeros((128, 128), F32)
-            qe = jnp.concatenate([dqo[even].astype(F32), blank], axis=1)
-            qo = jnp.concatenate([dqo[odd].astype(F32), blank], axis=1)
+            qe = jnp.concatenate([unpack(dqo[even].astype(F32), 0), blank], axis=1)
+            qo = jnp.concatenate([unpack(dqo[odd].astype(F32), 0), blank], axis=1)
             joined[rows, 384 * p:384 * p + 384] = pair_columns(qe, qo, lane, False).astype(BF16)
             ke, ko = dkvo[even].astype(F32), dkvo[odd].astype(F32)
             joined[rows, 768 + 384 * p:1152 + 384 * p] = pair_columns(ke, ko, lane, False).astype(BF16)
@@ -1359,7 +1400,6 @@
     vec.wait_recv()
     v_b[b] = v_core[:, pl.ds(pl.multiple_of(f * 384, 128), 384)] + v_f[...]
     vec = go(v_b.at[b], v_b.at[b], xp)
-    weights.wait()
 
     @pl.loop(0, 3)
     def _(n):
@@ -1395,20 +1435,21 @@
         gradient_kernel,
         out_shape=[jax.ShapeDtypeStruct((2, 8, BLK, 3456), BF16), jax.ShapeDtypeStruct((4, 4, 96, 640), BF16),
                    jax.ShapeDtypeStruct((256, 768), F32), jax.ShapeDtypeStruct((16, 384), F32)],
-        in_specs=[pl.BlockSpec(memory_space=pltpu.SMEM), anywhere] + [vmem()] * 13, out_specs=[anywhere] * 2 + [vmem()] * 2,
+        in_specs=[pl.BlockSpec(memory_space=pltpu.SMEM)] + [anywhere] * 7 + [vmem()] * 7, out_specs=[anywhere] * 2 + [vmem()] * 2,
         scratch_shapes=[
-            bf(256, 2304), bf(768, 2304), bf(4, 4, BLK, 3456), bf(4, 4, BLK, 3456), bf(4, 4, BLK, 3456),
+            bf(256, 2304), bf(768, 2304), fl(256, 768), bf(6, 768, 128), bf(2, 768, 128), bf(8, 96, 256), bf(total, 384), fl(4, 256, SPAN),
+            bf(4, 4, BLK, 3456), bf(4, 4, BLK, 3456), bf(4, 4, BLK, 3456),
             bf(2, 4, BLK, 1536), bf(4, BLK, 1152), bf(2, 4, BLK, 1152), bf(4, BLK, 1536),
             bf(3, 4, BLK, 768), bf(3, BLK, 2688), bf(2, BLK, 768), bf(BLK, 768),
-            bf(8, 128, 256), bf(4, 3, SPAN, 256), bf(4, 3, SPAN, 256), bf(256, total), fl(KB, 256), fl(KB, 256), fl(4, 256, SPAN),
+            bf(8, 96, 256), bf(4, 3, SPAN, 256), bf(4, 3, SPAN, 256), bf(256, total), fl(KB, 256), fl(KB, 256), fl(4, 256, SPAN),
             pltpu.VMEM((4, 8, SPAN), jnp.int32), fl(4, 8, SPAN),
-            bf(8, 128, 256), bf(8, 128, 384), bf(8, 128, 256), bf(8, 128, 384), bf(8, 128, 384), bf(8, 128, 384),
+            bf(8, 96, 256), bf(8, 128, 256), bf(8, 128, 384), bf(8, 96, 256), bf(8, 128, 384), bf(8, 128, 384), bf(8, 128, 384),
             bf(4, 96, 640), bf(4, 96, 640), fl(4, 96, 640), bf(4, 96, 640), bf(2, 96, 640), bf(96, 640),
             fl(16, 768), fl(16, 768), fl(16, 384), fl(2, 16, 384), fl(4, 16, 384),
-            DMA((wires,)), DMA((wires,)), DMA((6,))],
+            DMA((wires,)), DMA((wires,)), DMA((12,))],
         compiler_params=pltpu.CompilerParams(collective_id=ident, has_side_effects=True, vmem_limit_bytes=62 << 20),
         name="reduce_all",
-    )(lens, wqkv, gfirst, near, far, xt, gbr, ghid, gsec, small, do_sent, q, kv, ot, lse)
+    )(lens, wqkv, gfirst, near, far, q, kv, ot, xt, gbr, ghid, gsec, small, do_sent, lse)
 
 
 def widen_kernel(grads, late, low, igrad, sums, g_qkv, g_out, g_in, g_back, low_out, igrad_out, *vectors):
@@ -1479,7 +1520,6 @@
     def token_block(dc):
         return tokens.at[pl.ds(pl.multiple_of(lax.rem(c + dc, 2) * 128, 128), 128)]
 
-    beyond = [go(token_block(dc), f_held.at[dc], group.devices[n]) for dc, n in ((0, 4), (1, 6))]
 
     def row(n):
         return jnp.concatenate([vec[0, n:n + 1], vec[1, n:n + 1]], axis=1)
@@ -1489,13 +1529,14 @@
 
     for cp in swaps.values():
         cp.wait_recv()
+    beyond = [go(token_block(dc), f_held.at[dc], group.devices[n]) for dc, n in ((0, 4), (1, 6))]
     lane = lax.broadcasted_iota(jnp.int32, (128, 384), 1)
     blank = jnp.zeros((128, 128), F32)
     att = act
     for s in range(2):
         rows = slice(s * 128, s * 128 + 128)
         for p in range(2):
-            sides = [jnp.concatenate([pltpu.roll(o_held[4 * p + 2 * k + s].astype(F32), 192, 1), blank], axis=1) for k in range(2)]
+            sides = [jnp.concatenate([pltpu.roll(unpack(o_held[4 * p + 2 * k + s].astype(F32), 64), 192, 1), blank], axis=1) for k in range(2)]
             att[rows, 384 * p:384 * p + 384] = pair_columns(sides[0], sides[1], lane, False).astype(BF16)
     transpose_into(xt, att.at[:, 0:768], 0)
 
@@ -1577,9 +1618,9 @@
         part = normed[:, 384 * p:384 * p + 384]
         for k in range(2):
             turned = part if k == 0 else pltpu.roll(part, 192, 1)
-            block = pltpu.roll(jnp.where(wide < 192, turned[:, :256], 0.0), 64, 1).astype(BF16)
+            block = pltpu.roll(jnp.where(wide < 192, turned[:, :256], 0.0), 64, 1)
             for s in range(2):
-                do_sent[4 * p + 2 * k + s] = block[128 * s:128 * s + 128]
+                do_sent[4 * p + 2 * k + s] = pack(block[128 * s:128 * s + 128], 64).astype(BF16)
     for cp in beyond:
         cp.wait_recv()
     for n in range(2):
@@ -1600,9 +1641,9 @@
     return pl.pallas_call(
         middle_kernel,
         out_shape=[out(BF16, 256, 768), out(F32, 256, 768), out(BF16, 4608, 256), out(BF16, 256, 768), out(BF16, 256, 3072),
-                   out(BF16, 256, 768), out(BF16, 8, 128, 256), out(F32, 16, 768), out(BF16, 2, 768, 128)],
+                   out(BF16, 256, 768), out(BF16, 8, 96, 256), out(F32, 16, 768), out(BF16, 2, 768, 128)],
         in_specs=[vmem()] * 3 + [anywhere] * 3 + [vmem()], out_specs=[vmem()] * 9,
-        scratch_shapes=[bf(8, 128, 256), bf(2, 128, 768), bf(768, 768), bf(768, 3072), bf(3072, 768),
+        scratch_shapes=[bf(8, 96, 256), bf(2, 128, 768), bf(768, 768), bf(768, 3072), bf(3072, 768),
                         fl(256, 768), fl(256, 768), fl(256, 768), fl(256, 3072), bf(256, 3072),
                         DMA((wires,)), DMA((wires,)), DMA((3,))],
         compiler_params=pltpu.CompilerParams(collective_id=ident, has_side_effects=True, vmem_limit_bytes=60 << 20),
@@ -1642,9 +1683,9 @@
     if cube:
         q_held, kv_held, full_qkv, full_out, full_in, full_back, sides, near = project(inputs, (w_qkv, w_out, w_in, w_back), vectors, 1)
         kv_held = kv_held.reshape(-1, 384)
-        mixed, mixed_t, log_total = attend_forward(doc_lengths, q_held.reshape(8 * per, 256), kv_held, cols)
+        mixed, mixed_t, log_total = attend_forward(doc_lengths, q_held, kv_held, cols, True)
         output, grad_first, xt, grad_branch, grad_hidden, grad_second, do_sent, small, far = middle(
-            mixed.reshape(8, per, 256), inputs, cotangent.reshape(inputs.shape), full_out, full_in, full_back, sides, 3)
+            mixed, inputs, cotangent.reshape(inputs.shape), full_out, full_in, full_back, sides, 3)
         grads, late, input_grad, sums = reduce_all(
             doc_lengths, full_qkv, grad_first, near, far, xt, grad_branch, grad_hidden, grad_second, small, do_sent, q_held, kv_held,
             mixed_t, log_total, 5)

time: 279 us -> 265 us (0.950)
  Pallas kernels: 276 us -> 265 us
    pallas_call x1, Pallas kernels: 41.8 us -> 34 us  [middle(): pl.pallas_call(middle_kernel, out_shape=[out(BF16, 256, 768), out(F32, 25...]
where the time goes in v7:
time: 265 us; the launch traced here: 266 us
  Pallas kernels  265 us (100%)
    pallas_call x1, Pallas kernels, reduce_all(): pl.pallas_call(gradient_kernel, out_shape=[jax.ShapeDtypeStruct((2, 8, BL...  139 us
    pallas_call x1, Pallas kernels, project(): pl.pallas_call(project_kernel, out_shape=[jax.ShapeDtypeStruct((8, 96, 25...  67.3 us
    pallas_call x1, Pallas kernels, middle(): pl.pallas_call(middle_kernel, out_shape=[out(BF16, 256, 768), out(F32, 25...  34 us
    pallas_call x1, Pallas kernels, attend_forward(): pl.pallas_call(functools.partial(forward_kernel, cols, packed), out_shape...  15.5 us
    pallas_call x1, Pallas kernels, widen(): pl.pallas_call(widen_kernel, grid=(rows // step,), out_shape=[jax.ShapeDt...  9.6 us

profile of v7, /device:TPU:9, one launch (start us, length us, event | category | flops | bytes accessed | tf_op | source)
XLA Modules:
  0.0 265.7 jit_solution(13278787236675627789)
XLA Ops:
  0.7 67.3 %project.1 = (bf16[8,96,256]{2,1,0:T(8,128)(2,1)}, bf16[16,128,384]{2,1,0:T(8,128)(2,1)}, bf16[768,2304]{1,0:T(8,128)(2,1)}, bf16[768,768]{1,0:T(8,128)(2,1)}, b...) custom-call(bf16[256,768]{1,0:T(8,128)(2,1)} %bitcast.10, ...), custom_call_target="tpu_custom_call" | custom-call | tf_op jit(solution)/shard_map/project/pallas_call | solution.py:898
  68.0 15.5 %attend_forward.1 = (bf16[8,96,256]{2,1,0:T(8,128)(2,1)}, f32[4,256,256]{2,1,0:T(8,128)}, f32[4,8,256]{2,1,0:T(8,128)}) custom-call(s32[2,4]{1,0:T(2,128)} %lens.3, bf16[8,96,256]{2,1,0:T(8,128)(2,1)} %get-tuple-element.55.q_ref.q_hbm, bf16[2048,384]{1,0:T(8,128)(2,1)} %bitcast.7), custom_call_target="tpu_custom_call" | custom-call | tf_op jit(solution)/shard_map/attend_forward/pallas_call | solution.py:558
  83.4 34.0 %middle.1 = (bf16[256,768]{1,0:T(8,128)(2,1)}, f32[256,768]{1,0:T(8,128)}, bf16[4608,256]{1,0:T(8,128)(2,1)}, bf16[256,768]{1,0:T(8,128)(2,1)}, bf16[256,3072]{1...) custom-call(bf16[8,96,256]{2,1,0:T(8,128)(2,1)} %get-tuple-element.5, ...), custom_call_target="tpu_custom_call" | custom-call | tf_op jit(solution)/shard_map/middle/pallas_call | solution.py:1641
  117.4 138.5 %reduce_all.1 = (bf16[2,8,48,3456]{3,2,1,0:T(8,128)(2,1)}, bf16[4,4,96,640]{3,2,1,0:T(8,128)(2,1)}, f32[256,768]{1,0:T(8,128)}, f32[16,384]{1,0:T(8,128)}) custom-call(s32[2,4]{1,0:T(2,128)} %lens.3, bf16[768,2304]{1,0:T(8,128)(2,1)} %get-tuple-element.54.wqkv, f32[256,768]{1,0:T(8,128)} %get-tuple-element.62.gfirst_hbm, ...), custom_call_target="tpu_custom_call" | custom-call | tf_op jit(solution)/shard_map/reduce_all/pallas_call | solution.py:1434
  255.9 9.6 %widen.1 = (f32[384,2304]{1,0:T(8,128)}, f32[384,768]{1,0:T(8,128)}, f32[384,3072]{1,0:T(8,128)}, f32[4,384,768]{2,1,0:T(8,128)}, bf16[256,768]{1,0:T(8,128)(2,1...) custom-call(bf16[2,384,3456]{2,1,0:T(8,128)(2,1)} %bitcast.9, ...), custom_call_target="tpu_custom_call" | custom-call | tf_op jit(solution)/shard_map/widen/pallas_call | solution.py:1489

commit v8 on v7

--- a/solution.py
+++ b/solution.py
@@ -1460,9 +1460,9 @@
         g_in[:, core * 1536 + 768:core * 1536 + 1536] = part[:, 1152:1920].astype(F32)
         for j in range(4):
             g_back[j, :, core * 384:core * 384 + 384] = part[:, 1920 + 384 * j:2304 + 384 * j].astype(F32)
-    lane = lax.broadcasted_iota(jnp.int32, (96, 384), 1)
+    lane = lax.broadcasted_iota(jnp.int32, (192, 384), 1)
     for p in range(2):
-        even, odd = late[2 * p, 0].astype(F32), late[2 * p + 1, 0].astype(F32)
+        even, odd = late[2 * p].astype(F32), late[2 * p + 1].astype(F32)
         g_qkv[:, 384 * p:384 * p + 384] = pair_columns(even[:, :384], odd[:, :384], lane, False)
         ke, ko = even[:, 256:], odd[:, 256:]
         g_qkv[:, 768 + 384 * p:1152 + 384 * p] = pair_columns(ke, ko, lane, False)
@@ -1482,7 +1482,7 @@
 
 
 def widen(grads, late, low, igrad, sums):
-    rows, step = 384, 96
+    rows, step = 384, 192
     spec = lambda tall, wide: pl.BlockSpec((tall, wide), lambda n: (n, 0))
     flat = lambda size: pl.BlockSpec((size,), lambda n: (0,))
     sizes = [384] * 3 + [1536] + [384] * 5
@@ -1493,13 +1493,13 @@
                    jax.ShapeDtypeStruct((rows, 3072), F32), jax.ShapeDtypeStruct((4, rows, 768), F32),
                    jax.ShapeDtypeStruct(low.shape, BF16), jax.ShapeDtypeStruct(igrad.shape, F32)]
         + [jax.ShapeDtypeStruct((size,), F32) for size in sizes],
-        in_specs=[pl.BlockSpec((2, step, 3456), lambda n: (0, n, 0)), pl.BlockSpec((4, 1, step, 640), lambda n: (0, n, 0, 0)),
-                  spec(64, 768), spec(64, 768), pl.BlockSpec((16, 384), lambda n: (0, 0))],
+        in_specs=[pl.BlockSpec((2, step, 3456), lambda n: (0, n, 0)), pl.BlockSpec((4, step, 640), lambda n: (0, n, 0)),
+                  spec(128, 768), spec(128, 768), pl.BlockSpec((16, 384), lambda n: (0, 0))],
         out_specs=[spec(step, 2304), spec(step, 768), spec(step, 3072), pl.BlockSpec((4, step, 768), lambda n: (0, n, 0)),
-                   spec(64, 768), spec(64, 768)] + [flat(size) for size in sizes],
+                   spec(128, 768), spec(128, 768)] + [flat(size) for size in sizes],
         compiler_params=pltpu.CompilerParams(vmem_limit_bytes=62 << 20),
         name="widen",
-    )(grads, late, low, igrad, sums)
+    )(grads, late.reshape(4, rows, 640), low, igrad, sums)
 
 
 def middle_kernel(o_sent, tokens, cotangent, w_out, w_in, w_back, vec,
@@ -1570,9 +1570,10 @@
         hidden = dot(output[...], v_in[:, cols], NN) + bias
         half = 0.5 * (1.0 + lax.erf(hidden * 0.7071067811865476))
         slope[:, cols] = half + hidden * (jnp.exp(-0.5 * hidden * hidden) * 0.3989422804014327)
-        act[:, cols] = (hidden * half).astype(BF16)
-
-    transpose_into(xt, act, 1536)
+        value = hidden * half
+        act[:, cols] = value.astype(BF16)
+        xt[pl.ds(pl.multiple_of(1536 + n * 768, 128), 768)] = value.T.astype(BF16)
+
     loads[2].wait()
     final[...] = normed[...] + (dot(act[...], v_back[...], NN) + row(3))
     hat2, inverse2 = norm(final[...])

time: 265 us -> 264 us (level)
  Pallas kernels: 265 us -> 262 us
where the time goes in v8:
time: 264 us; the launch traced here: 263 us
  Pallas kernels  262 us (99%)
    pallas_call x1, Pallas kernels, reduce_all(): pl.pallas_call(gradient_kernel, out_shape=[jax.ShapeDtypeStruct((2, 8, BL...  137 us
    pallas_call x1, Pallas kernels, project(): pl.pallas_call(project_kernel, out_shape=[jax.ShapeDtypeStruct((8, 96, 25...  67.3 us
    pallas_call x1, Pallas kernels, middle(): pl.pallas_call(middle_kernel, out_shape=[out(BF16, 256, 768), out(F32, 25...  34 us
    pallas_call x1, Pallas kernels, attend_forward(): pl.pallas_call(functools.partial(forward_kernel, cols, packed), out_shape...  15.5 us
    pallas_call x1, Pallas kernels, widen(): pl.pallas_call(widen_kernel, grid=(rows // step,), out_shape=[jax.ShapeDt...  8.26 us

profile of v8, /device:TPU:9, one launch (start us, length us, event | category | flops | bytes accessed | tf_op | source)
XLA Modules:
  0.0 263.1 jit_solution(7357579532719155049)
XLA Ops:
  0.7 67.3 %project.1 = (bf16[8,96,256]{2,1,0:T(8,128)(2,1)}, bf16[16,128,384]{2,1,0:T(8,128)(2,1)}, bf16[768,2304]{1,0:T(8,128)(2,1)}, bf16[768,768]{1,0:T(8,128)(2,1)}, b...) custom-call(bf16[256,768]{1,0:T(8,128)(2,1)} %bitcast.12, ...), custom_call_target="tpu_custom_call" | custom-call | tf_op jit(solution)/shard_map/project/pallas_call | solution.py:898
  68.0 15.5 %attend_forward.1 = (bf16[8,96,256]{2,1,0:T(8,128)(2,1)}, f32[4,256,256]{2,1,0:T(8,128)}, f32[4,8,256]{2,1,0:T(8,128)}) custom-call(s32[2,4]{1,0:T(2,128)} %lens.3, bf16[8,96,256]{2,1,0:T(8,128)(2,1)} %get-tuple-element.55.q_ref.q_hbm, bf16[2048,384]{1,0:T(8,128)(2,1)} %bitcast.8), custom_call_target="tpu_custom_call" | custom-call | tf_op jit(solution)/shard_map/attend_forward/pallas_call | solution.py:558
  83.4 34.0 %middle.1 = (bf16[256,768]{1,0:T(8,128)(2,1)}, f32[256,768]{1,0:T(8,128)}, bf16[4608,256]{1,0:T(8,128)(2,1)}, bf16[256,768]{1,0:T(8,128)(2,1)}, bf16[256,3072]{1...) custom-call(bf16[8,96,256]{2,1,0:T(8,128)(2,1)} %get-tuple-element.5, ...), custom_call_target="tpu_custom_call" | custom-call | tf_op jit(solution)/shard_map/middle/pallas_call | solution.py:1642
  117.4 137.3 %reduce_all.1 = (bf16[2,8,48,3456]{3,2,1,0:T(8,128)(2,1)}, bf16[4,4,96,640]{3,2,1,0:T(8,128)(2,1)}, f32[256,768]{1,0:T(8,128)}, f32[16,384]{1,0:T(8,128)}) custom-call(s32[2,4]{1,0:T(2,128)} %lens.3, bf16[768,2304]{1,0:T(8,128)(2,1)} %get-tuple-element.54.wqkv, f32[256,768]{1,0:T(8,128)} %get-tuple-element.62.gfirst_hbm, ...), custom_call_target="tpu_custom_call" | custom-call | tf_op jit(solution)/shard_map/reduce_all/pallas_call | solution.py:1434
  254.7 8.3 %widen.1 = (f32[384,2304]{1,0:T(8,128)}, f32[384,768]{1,0:T(8,128)}, f32[384,3072]{1,0:T(8,128)}, f32[4,384,768]{2,1,0:T(8,128)}, bf16[256,768]{1,0:T(8,128)(2,1...) custom-call(bf16[2,384,3456]{2,1,0:T(8,128)(2,1)} %bitcast.10, ...), custom_call_target="tpu_custom_call" | custom-call | tf_op jit(solution)/shard_map/widen/pallas_call | solution.py:1489
